TPU v7x, 256 devices: a whole 4x4x8 slice. The times are simulated.
256 devices in a mesh: ctx: 64 (over y, z, core), head: 4 (over x).
Axes of the slice: x: 4, y: 4, z: 8, core: 2. Of those that a mesh axis runs over, the one named last changes fastest.
Arguments:
- query: bfloat16 [8192, 32, 128], P('ctx', 'head'), may hold values from -6 to 6
- key: bfloat16 [8192, 4, 128], P(('ctx', 'head')), may hold values from -6 to 6
- value: bfloat16 [8192, 4, 128], P(('ctx', 'head')), may hold values from -6 to 6
- d_out: bfloat16 [8192, 32, 128], P('ctx', 'head'), may hold values from -6 to 6
- seg_blocks: int32 [32], replicated, may hold values from 1 to 4, 64 in all
- seg_audio: int32 [32], replicated, may hold values 0 or 1
Outputs:
- d_query: bfloat16 [8192, 32, 128], P('ctx', 'head')
- d_key: bfloat16 [8192, 4, 128], P(('ctx', 'head'))
- d_value: bfloat16 [8192, 4, 128], P(('ctx', 'head'))
Inputs may be any that keep to these rules, and one draw needn't show every extreme that they name: `seg_blocks`: the segments tile the 64 blocks in order: their lengths sum to 64.
All inputs are finite; a program needn't handle non-finite values.
Results may differ from a plain program's by a relative error of at most 0.0055.
Values may be sent and summed in bfloat16 or wider, within the bound.
No kernel may reach another device: no remote copies, remote signals or barrier semaphores. Data moves between devices by JAX's collectives and lax.ppermute only.
A program may use at most 128 MiB of HBM per device.

v0:
```python
import math

import jax
import jax.numpy as jnp
from jax import lax
from jax.sharding import PartitionSpec as P

DH = 128
GROUP = 8
BLK = 128


NEG = -1e30


def segment_tables(seg_blocks, seg_audio, positions):
    ends = jnp.cumsum(seg_blocks)
    starts = ends - seg_blocks
    blocks = positions // BLK
    inside = (starts[None, :] <= blocks[:, None]) & (blocks[:, None] < ends[None, :])
    numbers = jnp.arange(seg_blocks.shape[0], dtype=jnp.int32)
    segment = jnp.sum(jnp.where(inside, numbers[None, :], 0), axis=1)
    audio = jnp.sum(jnp.where(inside, seg_audio[None, :], 0), axis=1)
    return (segment, audio)


def visible(query_pos, key_pos, query_seg, query_audio, key_seg):
    causal = key_pos[None, :] <= query_pos[:, None]
    span = (query_seg[:, None] == key_seg[None, :]) & (query_audio[:, None] == 1)
    return causal | span


def prepare(rows_query, rows_out, query_pos, seg_blocks, seg_audio):
    tokens = rows_query.shape[0]
    query_seg, query_audio = segment_tables(seg_blocks, seg_audio, query_pos)
    query_flat = rows_query.reshape(tokens * GROUP, DH)
    out_flat = rows_out.reshape(tokens * GROUP, DH)
    return (query_flat, out_flat, query_pos, query_seg, query_audio)


def piece_mask(group_data, keys, seg_blocks, seg_audio):
    query_flat, out_flat, query_pos, query_seg, query_audio = group_data
    key_pos = jnp.arange(keys.shape[0], dtype=jnp.int32)
    key_seg = segment_tables(seg_blocks, seg_audio, key_pos)[0]
    return visible(query_pos, key_pos, query_seg, query_audio, key_seg)


def contract_rows(left, right):
    return lax.dot_general(
        left, right, (((1,), (1,)), ((), ())), preferred_element_type=jnp.float32
    )


def contract_first(left, right):
    return lax.dot_general(
        left, right, (((0,), (0,)), ((), ())), preferred_element_type=jnp.float32
    )


def stats_group(group_data, state, piece, seg_blocks, seg_audio):
    query_flat, out_flat, query_pos, query_seg, query_audio = group_data
    keys, values = piece
    count = keys.shape[0]
    tokens = query_pos.shape[0]
    scale = 1.0 / math.sqrt(DH)
    mask = piece_mask(group_data, keys, seg_blocks, seg_audio)

    def stats_compute(kept):
        highest, total, weighted = kept
        wide = mask[:, None, :]
        scores = (contract_rows(query_flat, keys) * scale).reshape(tokens, GROUP, count)
        new_high = jnp.maximum(highest, jnp.max(jnp.where(wide, scores, NEG), axis=2))
        probs = jnp.where(wide, jnp.exp(scores - new_high[:, :, None]), 0.0)
        d_probs = contract_rows(out_flat, values).reshape(tokens, GROUP, count)
        return (new_high, jnp.sum(probs, axis=2), jnp.sum(probs * d_probs, axis=2))

    def stats_skipped(kept):
        return kept

    return lax.cond(jnp.any(mask), stats_compute, stats_skipped, state)


def grad_group(group_data, finals, grad_rows, piece, seg_blocks, seg_audio):
    query_flat, out_flat, query_pos, query_seg, query_audio = group_data
    lse, delta = finals
    keys, values = piece
    count = keys.shape[0]
    tokens = query_pos.shape[0]
    scale = 1.0 / math.sqrt(DH)
    mask = piece_mask(group_data, keys, seg_blocks, seg_audio)

    def grad_compute(grad_rows):
        wide = mask[:, None, :]
        scores = (contract_rows(query_flat, keys) * scale).reshape(tokens, GROUP, count)
        probs = jnp.where(wide, jnp.exp(scores - lse[:, :, None]), 0.0)
        d_probs = contract_rows(out_flat, values).reshape(tokens, GROUP, count)
        probs_low = probs.astype(jnp.bfloat16).reshape(tokens * GROUP, count)
        d_scores = (
            (probs * (d_probs - delta[:, :, None]))
            .astype(jnp.bfloat16)
            .reshape(tokens * GROUP, count)
        )
        value_part = contract_first(probs_low, out_flat)
        key_part = contract_first(d_scores, query_flat)
        grad_rows = jnp.dot(d_scores, keys, preferred_element_type=jnp.float32)
        return (grad_rows, key_part, value_part)

    def grad_skipped(grad_rows):
        blank = jnp.zeros((count, keys.shape[1]), jnp.float32)
        return (grad_rows, blank, blank)

    return lax.cond(jnp.any(mask), grad_compute, grad_skipped, grad_rows)


def body(query, key, value, d_out, seg_blocks, seg_audio):
    key, value = (
        lax.all_to_all(key, "head", split_axis=1, concat_axis=0, tiled=True),
        lax.all_to_all(value, "head", split_axis=1, concat_axis=0, tiled=True),
    )
    rows = query.shape[0]
    half = rows // 2
    place = lax.axis_index("ctx")
    scale = 1.0 / math.sqrt(DH)
    keys = key[:, 0, :]
    values = value[:, 0, :]
    own_pos = place * rows + jnp.arange(rows, dtype=jnp.int32)
    first = prepare(query[:half], d_out[:half], own_pos[:half], seg_blocks, seg_audio)
    second = prepare(query[half:], d_out[half:], own_pos[half:], seg_blocks, seg_audio)
    groups = (first, second)
    blank_stats = jnp.zeros((half, GROUP), jnp.float32)
    start_stats = tuple(
        (
            (jnp.full((half, GROUP), NEG, jnp.float32), blank_stats, blank_stats)
            for group_data in groups
        )
    )
    piece = (
        lax.all_gather(keys, "ctx", axis=0, tiled=True),
        lax.all_gather(values, "ctx", axis=0, tiled=True),
    )
    stats = tuple(
        (
            stats_group(group_data, state, piece, seg_blocks, seg_audio)
            for group_data, state in zip(groups, start_stats)
        )
    )
    finals = tuple(
        ((highest + jnp.log(total), weighted / total) for highest, total, weighted in stats)
    )
    blank_rows = jnp.zeros((half * GROUP, DH), jnp.float32)
    piece = (
        lax.all_gather(keys, "ctx", axis=0, tiled=True),
        lax.all_gather(values, "ctx", axis=0, tiled=True),
    )
    grad_list = (blank_rows, blank_rows)
    piece_keys = piece[0]
    count = piece_keys.shape[0]
    key_sum = jnp.zeros((count, DH), jnp.float32)
    value_sum = jnp.zeros((count, DH), jnp.float32)
    new_rows = []
    for group_data, group_finals, grad_rows in zip(groups, finals, grad_list):
        grad_rows, key_part, value_part = grad_group(
            group_data, group_finals, grad_rows, piece, seg_blocks, seg_audio
        )
        key_sum = key_sum + key_part
        value_sum = value_sum + value_part
        new_rows.append(grad_rows)
    update = jnp.stack([key_sum, value_sum], axis=1)
    key_grad = update
    grads = (key_grad, tuple(new_rows))
    key_grad, grad_list = grads
    summed = lax.psum_scatter(key_grad, "ctx", scatter_dimension=0, tiled=True)
    d_key = (summed[:, 0, :] * scale).astype(jnp.bfloat16)[:, None, :]
    d_value = summed[:, 1, :].astype(jnp.bfloat16)[:, None, :]
    first_rows = (grad_list[0] * scale).astype(jnp.bfloat16).reshape(half, GROUP, DH)
    second_rows = (grad_list[1] * scale).astype(jnp.bfloat16).reshape(half, GROUP, DH)
    d_query = jnp.concatenate([first_rows, second_rows], axis=0)
    d_key, d_value = (
        lax.all_to_all(d_key, "head", split_axis=0, concat_axis=1, tiled=True),
        lax.all_to_all(d_value, "head", split_axis=0, concat_axis=1, tiled=True),
    )
    return (d_query, d_key, d_value)


def solution(mesh):
    placed = (
        P("ctx", "head", None),
        P(("ctx", "head"), None, None),
        P(("ctx", "head"), None, None),
        P("ctx", "head", None),
        P(),
        P(),
    )
    return jax.shard_map(
        body,
        mesh=mesh,
        in_specs=placed,
        out_specs=(
            P("ctx", "head", None),
            P(("ctx", "head"), None, None),
            P(("ctx", "head"), None, None),
        ),
        check_vma=False,
    )
```

profile of v0, /device:TPU:16, one launch (start us, length us, event | category | flops | bytes accessed | tf_op | source)
XLA Modules:
  0.0 555.0 jit_solution(9331188242737443876)
XLA Ops:
  7.2 0.8 copy.34
  8.0 9.6 %all_to_all.66 = bf16[32,4,128]{2,0,1:T(8,128)(2,1)} all-to-all(bf16[32,4,128]{2,0,1:T(8,128)(2,1)S(1)} %copy.34), channel_id=1, replica_groups=mesh['ctx'=64,'head'=4] {'head'}, dimensions={1} | all-to-all | bytes 65536 | tf_op jit(solution)/shard_map/all_to_all | solution.py:117
  17.7 0.8 copy.35
  18.5 8.5 %all_to_all.67 = bf16[32,4,128]{2,0,1:T(8,128)(2,1)} all-to-all(bf16[32,4,128]{2,0,1:T(8,128)(2,1)S(1)} %copy.35), channel_id=1, replica_groups=mesh['ctx'=64,'head'=4] {'head'}, dimensions={1} | all-to-all | bytes 65536 | tf_op jit(solution)/shard_map/all_to_all | solution.py:118
  27.0 0.7 copy.33
  27.8 0.1 reduce.12
  27.9 0.7 sub.100
  28.7 0.7 select_reduce_fusion.3
  29.4 0.3 select_reduce_fusion
  29.8 2.3 fusion.16
  33.4 1.8 slice_bitcast_fusion.2
  35.2 60.0 %all-gather.3.cloned.1.call-done = bf16[8192,128]{1,0:T(8,128)(2,1)} async-done(((bf16[128,128]{1,0:T(8,128)(2,1)}), bf16[8192,128]{1,0:T(8,128)(2,1)}) %all-gather.3.cloned.1.call-update) | async-done | bytes 2097168 | tf_op jit(solution)/shard_map/all_gather | solution.py:152
  95.2 77.8 %all-gather.5.cloned.1.call-done = bf16[8192,128]{1,0:T(8,128)(2,1)} async-done(((bf16[128,128]{1,0:T(8,128)(2,1)}), bf16[8192,128]{1,0:T(8,128)(2,1)}) %all-gather.5.cloned.1.call-update) | async-done | bytes 2097168 | tf_op jit(solution)/shard_map/all_gather | solution.py:139
  173.0 30.0 %conditional.4 = (f32[64,8]{1,0:T(8,128)}, f32[64,8]{1,0:T(8,128)}, f32[64,8]{1,0:T(8,128)}) conditional(s32[]{:T(128)} %convert_element_type.36, () %tuple.57, (pred[64,8192]{1,0:T(8,128)(4,1)S(1)}, bf16[512,128]{1,0:T(8,128)(2,1)S(1)}, bf16[8192,128]{1,0:T(8,128)(2,1)}, bf16[512,128]{1,0:T(8,128)(2,1)}, bf16[8192,128]{1,0:T(8,128)(2,1)}) %tuple.58), branch_computations={%region_5.6_spmd, %region_6.10_spmd} | conditional | flops 2197814784 | bytes 65308752 | solution.py:80
  173.0 9.5 %fusion = (f32[512]{0:T(512)S(1)}, f32[512,8192]{1,0:T(8,128)}) fusion(pred[64,8192]{1,0:T(8,128)(4,1)S(1)} %get-tuple-element.80, bf16[512,128]{1,0:T(8,128)(2,1)S(1)} %get-tuple-element.81, bf16[8192,128]{1,0:T(8,128)(2,1)} %get-tuple-element.82), kind=kOutput, calls=%fused_computation.2 | convolution fusion | flops 1086324224 | bytes 19531776 | tf_op jit(solution)/shard_map/cond/branch_1_fun/dot_general | solution.py:49
  182.5 9.9 %multiply_reduce_fusion = f32[512]{0:T(512)S(1)} fusion(bf16[512,128]{1,0:T(8,128)(2,1)S(1)} %copy-done.10, bf16[8192,128]{1,0:T(8,128)(2,1)S(1)} %copy-done.6, f32[512,8192]{1,0:T(8,128)} %get-tuple-element.172, f32[512]{0:T(512)S(1)} %broadcast_maximum_fusion, pred[64,8192]{1,0:T(8,128)(4,1)S(1)} %get-tuple-element.80), kind=kOutput, calls=%fused_computation.3 | convolution fusion | flops 1094712832 | bytes 19533824 | tf_op jit(solution)/shard_map/cond/branch_1_fun/dot_general | solution.py:49
  192.4 8.5 %fusion.1 = f32[512]{0:T(512)S(1)} fusion(f32[512,8192]{1,0:T(8,128)} %get-tuple-element.172, f32[512]{0:T(512)S(1)} %broadcast_maximum_fusion, pred[64,8192]{1,0:T(8,128)(4,1)S(1)} %get-tuple-element.80), kind=kLoop, calls=%fused_computation.4 | loop fusion | flops 16776704 | bytes 17305600 | tf_op jit(solution)/shard_map/cond/branch_1_fun/reduce_sum | solution.py:75
  200.9 0.7 div.47
  201.6 0.7 max_broadcast_in_dim.21
  202.3 0.7 log.21
  203.0 38.1 %conditional.5 = (f32[512,128]{1,0:T(8,128)S(1)}, f32[8192,128]{1,0:T(8,128)}, f32[8192,128]{1,0:T(8,128)}) conditional(s32[]{:T(128)} %convert_element_type.36, () %tuple.56, (pred[64,8192]{1,0:T(8,128)(4,1)S(1)}, bf16[512,128]{1,0:T(8,128)(2,1)S(1)}, bf16[8192,128]{1,0:T(8,128)(2,1)}, f32[64,8]{1,0:T(8,128)}, f32[64,8]{1,0:T(8,128)}, ...), branch_computations={%region_10.11_spmd, %region_11.12_spmd} | conditional | flops 5398069760 | bytes 209471680 | solution.py:112
  203.5 0.8 sub.84
  204.4 0.8 add.23
  205.2 0.1 sub.81
  205.3 6.2 %exponential_select_fusion = f32[512,8192]{1,0:T(8,128)S(1)} fusion(bf16[512,128]{1,0:T(8,128)(2,1)S(1)} %get-tuple-element.86, bf16[8192,128]{1,0:T(8,128)(2,1)} %get-tuple-element.87, f32[512]{0:T(512)S(1)} %sub.81, pred[64,8192]{1,0:T(8,128)(4,1)S(1)} %get-tuple-element.85), kind=kOutput, calls=%fused_computation.7 | convolution fusion | flops 1086324736 | bytes 19531776 | tf_op jit(solution)/shard_map/cond/branch_1_fun/dot_general | solution.py:49
  211.5 5.7 %copy-done = f32[512,8192]{1,0:T(8,128)} copy-done((f32[512,8192]{1,0:T(8,128)}, f32[512,8192]{1,0:T(8,128)S(1)}, u32[]{:S(2)}) %copy-start) | copy-done | bytes 16777240 | tf_op jit(solution)/shard_map/cond
  217.2 4.3 fusion.2
  221.5 9.4 %multiply_convert_fusion = bf16[512,8192]{1,0:T(8,128)(2,1)} fusion(f32[512,8192]{1,0:T(8,128)} %copy-done, bf16[512,128]{1,0:T(8,128)(2,1)S(1)} %copy-done.11, bf16[8192,128]{1,0:T(8,128)(2,1)S(1)} %copy-done.7, f32[512]{0:T(512)S(1)} %sub.84), kind=kOutput, calls=%fused_computation.6 | convolution fusion | flops 1086324736 | bytes 27396096 | tf_op jit(solution)/shard_map/cond/branch_1_fun/dot_general | solution.py:49
  230.9 5.9 %fusion.23 = f32[512,128]{1,0:T(8,128)S(1)} fusion(bf16[512,8192]{1,0:T(8,128)(2,1)} %multiply_convert_fusion, bf16[8192,128]{1,0:T(8,128)(2,1)S(1)} %copy-done.4), kind=kOutput, calls=%fused_computation.67 | convolution fusion | flops 1073741824 | bytes 10747904 | tf_op jit(solution)/shard_map/cond/branch_1_fun/dot_general | solution.py:105
  236.8 4.4 fusion.24
  241.2 28.4 %conditional.6 = (f32[64,8]{1,0:T(8,128)S(1)}, f32[64,8]{1,0:T(8,128)S(1)}, f32[64,8]{1,0:T(8,128)S(1)}) conditional(s32[]{:T(128)} %convert_element_type.38, () %tuple.61, (pred[64,8192]{1,0:T(8,128)(4,1)S(1)}, bf16[512,128]{1,0:T(8,128)(2,1)S(1)}, bf16[8192,128]{1,0:T(8,128)(2,1)}, bf16[512,128]{1,0:T(8,128)(2,1)S(1)}, ...), branch_computations={%region_15.16_spmd, %region_16.20_spmd} | conditional | flops 2197814784 | bytes 64784436 | solution.py:80
  241.3 9.6 %fusion.4 = (f32[512]{0:T(512)S(1)}, f32[512,8192]{1,0:T(8,128)}) fusion(pred[64,8192]{1,0:T(8,128)(4,1)S(1)} %get-tuple-element.93, bf16[512,128]{1,0:T(8,128)(2,1)S(1)} %get-tuple-element.94, bf16[8192,128]{1,0:T(8,128)(2,1)} %get-tuple-element.95), kind=kOutput, calls=%fused_computation.12 | convolution fusion | flops 1086324224 | bytes 19531776 | tf_op jit(solution)/shard_map/cond/branch_1_fun/dot_general | solution.py:49
  250.9 9.9 %multiply_reduce_fusion.1 = f32[512]{0:T(512)S(1)} fusion(bf16[512,128]{1,0:T(8,128)(2,1)S(1)} %get-tuple-element.96, bf16[8192,128]{1,0:T(8,128)(2,1)S(1)} %copy-done.8, f32[512,8192]{1,0:T(8,128)} %get-tuple-element.176, f32[512]{0:T(512)S(1)} %broadcast_maximum_fusion.1, pred[64,8192]{1,0:T(8,128)(4,1)S(1)} %get-tuple-element.93), kind=kOutput, calls=%fused_computation.13 | convolution fusion | flops 1094712832 | bytes 19533824 | tf_op jit(solution)/shard_map/cond/branch_1_fun/dot_general | solution.py:49
  260.8 8.5 %fusion.5 = f32[512]{0:T(512)S(1)} fusion(f32[512,8192]{1,0:T(8,128)} %get-tuple-element.176, f32[512]{0:T(512)S(1)} %broadcast_maximum_fusion.1, pred[64,8192]{1,0:T(8,128)(4,1)S(1)} %get-tuple-element.93), kind=kLoop, calls=%fused_computation.14 | loop fusion | flops 16776704 | bytes 17305600 | tf_op jit(solution)/shard_map/cond/branch_1_fun/reduce_sum | solution.py:75
  269.3 0.1 div.49
  269.5 36.6 %conditional.7 = (f32[512,128]{1,0:T(8,128)S(1)}, f32[8192,128]{1,0:T(8,128)}, f32[8192,128]{1,0:T(8,128)}) conditional(s32[]{:T(128)} %convert_element_type.38, () %tuple.60, (pred[64,8192]{1,0:T(8,128)(4,1)S(1)}, bf16[512,128]{1,0:T(8,128)(2,1)S(1)}, bf16[8192,128]{1,0:T(8,128)(2,1)}, f32[64,8]{1,0:T(8,128)S(1)}, f32[64,8]{1,0:T(8,128)S(1)}, ...), branch_computations={%region_20.21_spmd, %region_21.22_spmd} | conditional | flops 5398069760 | bytes 208947360 | solution.py:112
  269.8 0.1 sub.92
  269.9 0.1 sub.89
  270.0 6.2 %exponential_select_fusion.1 = f32[512,8192]{1,0:T(8,128)S(1)} fusion(bf16[512,128]{1,0:T(8,128)(2,1)S(1)} %get-tuple-element.99, bf16[8192,128]{1,0:T(8,128)(2,1)} %get-tuple-element.100, f32[512]{0:T(512)S(1)} %sub.89, pred[64,8192]{1,0:T(8,128)(4,1)S(1)} %get-tuple-element.98), kind=kOutput, calls=%fused_computation.17 | convolution fusion | flops 1086324736 | bytes 19531776 | tf_op jit(solution)/shard_map/cond/branch_1_fun/dot_general | solution.py:49
  276.2 5.7 %copy-done.1 = f32[512,8192]{1,0:T(8,128)} copy-done((f32[512,8192]{1,0:T(8,128)}, f32[512,8192]{1,0:T(8,128)S(1)}, u32[]{:S(2)}) %copy-start.1) | copy-done | bytes 16777240 | tf_op jit(solution)/shard_map/cond
  281.9 4.4 fusion.6
  286.3 9.4 %multiply_convert_fusion.1 = bf16[512,8192]{1,0:T(8,128)(2,1)} fusion(f32[512,8192]{1,0:T(8,128)} %copy-done.1, bf16[512,128]{1,0:T(8,128)(2,1)S(1)} %get-tuple-element.103, bf16[8192,128]{1,0:T(8,128)(2,1)S(1)} %copy-done.9, f32[512]{0:T(512)S(1)} %sub.92), kind=kOutput, calls=%fused_computation.16 | convolution fusion | flops 1086324736 | bytes 27396096 | tf_op jit(solution)/shard_map/cond/branch_1_fun/dot_general | solution.py:49
  295.7 5.9 %fusion.25 = f32[512,128]{1,0:T(8,128)S(1)} fusion(bf16[512,8192]{1,0:T(8,128)(2,1)} %multiply_convert_fusion.1, bf16[8192,128]{1,0:T(8,128)(2,1)S(1)} %copy-done.5), kind=kOutput, calls=%fused_computation.69 | convolution fusion | flops 1073741824 | bytes 10747904 | tf_op jit(solution)/shard_map/cond/branch_1_fun/dot_general | solution.py:105
  301.6 4.3 fusion.26
  306.1 3.9 add.32
  310.0 3.9 add.31
  313.9 8.8 %pad_maximum_fusion = f32[8192,2,128]{2,1,0:T(2,128)} fusion(f32[8192,1,128]{2,1,0:T(1,128)S(1)} %bitcast.84, f32[8192,1,128]{2,1,0:T(1,128)S(1)} %bitcast.85), kind=kLoop, calls=%fused_computation.20 | loop fusion | flops 2097152 | bytes 16777216 | tf_op jit(solution)/shard_map/stack | solution.py:168
  322.7 0.6 copy-done.12
  323.4 0.6 dynamic-slice
  324.7 201.6 %all-reduce.3.cloned.1.call-done = f32[8192,2,128]{2,1,0:T(2,128)} async-done(((f32[8192,2,128]{2,1,0:T(2,128)}), f32[8192,2,128]{2,1,0:T(2,128)}) %all-reduce.3.cloned.1.call-update) | async-done | bytes 8388624
  526.2 1.0 dynamic-slice_convert_fusion
  527.2 0.5 broadcast.207
  527.7 0.8 reduce.14
  528.5 0.6 reshape.175
  529.2 4.2 all-to-all-start.3
  533.4 1.0 fusion.12
  534.4 0.8 reduce.13
  535.2 0.6 reshape.173
  535.9 3.0 all-to-all-done.3
  538.9 3.3 all-to-all-start.2
  542.1 0.7 pad_maximum_fusion.1
  542.9 0.6 copy.37
  543.6 4.0 all-to-all-done.2
  547.6 0.6 copy.36
  (47 shorter events, 0.7 us)
Async XLA Ops:
  7.2 88.0 %all-gather.3.cloned.1.call-start = ((), (), s32[]{:S(2)}) async-start(), calls=%async_computation.4 | async-start | bytes 2129920 | tf_op jit(solution)/shard_map/all_gather | solution.py:152
  17.6 155.3 %all-gather.5.cloned.1.call-start = ((), (), s32[]{:S(2)}) async-start(), calls=%async_computation.5 | async-start | bytes 2129920 | tf_op jit(solution)/shard_map/all_gather | solution.py:139
  26.9 499.3 %all-reduce.3.cloned.1.call-start = ((), (), s32[]{:S(2)}) async-start(), calls=%async_computation.6 | async-start | bytes 16777216
  173.0 9.6 %copy-start.6 = (bf16[8192,128]{1,0:T(8,128)(2,1)S(1)}, bf16[8192,128]{1,0:T(8,128)(2,1)}, u32[]{:S(2)}) copy-start(bf16[8192,128]{1,0:T(8,128)(2,1)} %get-tuple-element.84) | copy-start | bytes 6291460 | tf_op jit(solution)/shard_map/cond
  173.0 9.6 %copy-start.10 = (bf16[512,128]{1,0:T(8,128)(2,1)S(1)}, bf16[512,128]{1,0:T(8,128)(2,1)}, u32[]{:S(2)}) copy-start(bf16[512,128]{1,0:T(8,128)(2,1)} %get-tuple-element.83) | copy-start | bytes 393220 | tf_op jit(solution)/shard_map/cond
  205.2 11.9 %copy-start.11 = (bf16[512,128]{1,0:T(8,128)(2,1)S(1)}, bf16[512,128]{1,0:T(8,128)(2,1)}, u32[]{:S(2)}) copy-start(bf16[512,128]{1,0:T(8,128)(2,1)} %get-tuple-element.90) | copy-start | bytes 393220 | tf_op jit(solution)/shard_map/cond
  211.5 5.7 %copy-start = (f32[512,8192]{1,0:T(8,128)}, f32[512,8192]{1,0:T(8,128)S(1)}, u32[]{:S(2)}) copy-start(f32[512,8192]{1,0:T(8,128)S(1)} %exponential_select_fusion) | copy-start | bytes 50331652 | tf_op jit(solution)/shard_map/cond
  217.2 4.3 copy-start.7
  221.5 9.4 %copy-start.4 = (bf16[8192,128]{1,0:T(8,128)(2,1)S(1)}, bf16[8192,128]{1,0:T(8,128)(2,1)}, u32[]{:S(2)}) copy-start(bf16[8192,128]{1,0:T(8,128)(2,1)} %get-tuple-element.87) | copy-start | bytes 6291460 | tf_op jit(solution)/shard_map/cond
  230.9 5.9 %copy-start.2 = (bf16[512,8192]{1,0:T(8,128)(2,1)S(1)}, bf16[512,8192]{1,0:T(8,128)(2,1)}, u32[]{:S(2)}) copy-start(bf16[512,8192]{1,0:T(8,128)(2,1)} %multiply_convert_fusion) | copy-start | bytes 25165828 | tf_op jit(solution)/shard_map/cond
  241.3 9.6 %copy-start.8 = (bf16[8192,128]{1,0:T(8,128)(2,1)S(1)}, bf16[8192,128]{1,0:T(8,128)(2,1)}, u32[]{:S(2)}) copy-start(bf16[8192,128]{1,0:T(8,128)(2,1)} %get-tuple-element.97) | copy-start | bytes 6291460 | tf_op jit(solution)/shard_map/cond
  276.2 5.7 %copy-start.1 = (f32[512,8192]{1,0:T(8,128)}, f32[512,8192]{1,0:T(8,128)S(1)}, u32[]{:S(2)}) copy-start(f32[512,8192]{1,0:T(8,128)S(1)} %exponential_select_fusion.1) | copy-start | bytes 50331652 | tf_op jit(solution)/shard_map/cond
  281.9 4.4 copy-start.9
  286.3 9.4 %copy-start.5 = (bf16[8192,128]{1,0:T(8,128)(2,1)S(1)}, bf16[8192,128]{1,0:T(8,128)(2,1)}, u32[]{:S(2)}) copy-start(bf16[8192,128]{1,0:T(8,128)(2,1)} %get-tuple-element.100) | copy-start | bytes 6291460 | tf_op jit(solution)/shard_map/cond
  295.7 5.9 %copy-start.3 = (bf16[512,8192]{1,0:T(8,128)(2,1)S(1)}, bf16[512,8192]{1,0:T(8,128)(2,1)}, u32[]{:S(2)}) copy-start(bf16[512,8192]{1,0:T(8,128)(2,1)} %multiply_convert_fusion.1) | copy-start | bytes 25165828 | tf_op jit(solution)/shard_map/cond
  322.7 0.7 copy-start.12
  529.2 9.7 %all-to-all-start.3 = ((bf16[4,2,2048]{2,1,0:T(2,128)(2,1)}), bf16[4,2,2048]{2,1,0:T(2,128)(2,1)S(1)}, u32[]{:S(2)}, u32[]{:S(2)}) async-start(bf16[4,2,2048]{2,1,0:T(2,128)(2,1)} %reshape.175), calls=%async_computation.3 | async-start | bytes 65536 | tf_op jit(solution)/shard_map/all_to_all | solution.py:180
  538.9 8.7 %all-to-all-start.2 = ((bf16[4,2,2048]{2,1,0:T(2,128)(2,1)}), bf16[4,2,2048]{2,1,0:T(2,128)(2,1)S(1)}, u32[]{:S(2)}, u32[]{:S(2)}) async-start(bf16[4,2,2048]{2,1,0:T(2,128)(2,1)} %reshape.173), calls=%async_computation.2 | async-start | bytes 65536 | tf_op jit(solution)/shard_map/all_to_all | solution.py:179
Sparse Core Ops, SparseCore 0:
  17.8 77.3 all-gather.2
  98.0 74.9 all-gather.4
  322.8 203.3 all-reduce.2
where the time goes:
time: 564 us; the launch traced here: 555 us
  waiting for transfers between devices  346 us (61%)
  matrix products  99.2 us (18%)
  other arithmetic  42 us (7%)
  local copies, waits for them, and re-layouts  24.3 us (4%)
  blocking collectives  18.1 us (3%)
  between operations  16.1 us (3%)
  starting transfers between devices  7.63 us (1%)
    unnamed x4, waiting for transfers between devices  202 us
    all_gather x1, waiting for transfers between devices, body(): lax.all_gather(values, 'ctx', axis=0, tiled=True)  77.8 us
    dot_general x8, matrix products, contract_rows(): lax.dot_general(left, right, (((1,), (1,)), ((), ())), preferred_element_...  70.1 us
    all_gather x1, waiting for transfers between devices, body(): lax.all_gather(keys, 'ctx', axis=0, tiled=True)  60 us
    dot_general x4, matrix products, contract_first(): lax.dot_general(left, right, (((0,), (0,)), ((), ())), preferred_element_...  17.4 us
    reduce_sum x2, other arithmetic, stats_compute(): return (new_high, jnp.sum(probs, axis=2), jnp.sum(probs * d_probs, axis=2))  17 us
    dot_general x2, matrix products, grad_compute(): grad_rows = jnp.dot(d_scores, keys, preferred_element_type=jnp.float32)  11.7 us
    cond x24, local copies, waits for them, and re-layouts  11.4 us
  transfers between devices with their start and end apart: 5, of which 5 were waited for; matrix products, arithmetic and copies ran while one was open for 2% of the time, Pallas kernels for 0%

commit v1 on v0

v1 whole, which is shorter than its diff:
```python
import math

import jax
import jax.numpy as jnp
from jax import lax
from jax.experimental import pallas as pl
from jax.experimental.pallas import tpu as pltpu
from jax.sharding import Mesh, PartitionSpec as P

DH = 128
GROUP = 8
BLK = 128
NY, NZ, NC, NX = 4, 8, 2, 4
NSEG = 32
ROWS = BLK * GROUP
SLICE = BLK // NY
COL = NZ * NC * SLICE
NEG = -1e30
SCALE = 1.0 / math.sqrt(DH)
SCALE2 = SCALE * math.log2(math.e)
RB = 512
CROSS = 4 * SLICE
BF, F32 = jnp.bfloat16, jnp.float32
VM = pl.BlockSpec(memory_space=pltpu.VMEM)
SM = pl.BlockSpec(memory_space=pltpu.SMEM)
HB = pl.BlockSpec(memory_space=pl.ANY)


def dot_nt(a, b):
    return lax.dot_general(a, b, (((1,), (1,)), ((), ())), preferred_element_type=F32)


def dot_nn(a, b):
    return lax.dot_general(a, b, (((1,), (0,)), ((), ())), preferred_element_type=F32)


def dot_tn(a, b):
    return lax.dot_general(a, b, (((0,), (0,)), ((), ())), preferred_element_type=F32)


def span_ends(where, seg_blocks, seg_audio):
    blocks = [i * NZ * NC + where[1] * NC + where[2] for i in range(NY)]

    def step(s, carry):
        start, found = carry
        end = start + seg_blocks[s]
        value = jnp.where(seg_audio[s] == 1, end * BLK, 0)
        found = tuple(
            jnp.where((start <= b) & (b < end), value, f) for b, f in zip(blocks, found)
        )
        return (end, found)

    zero = jnp.int32(0)
    return lax.fori_loop(0, NSEG, step, (zero, (zero,) * NY))[1]


def pick(i, values):
    out = values[0]
    for n in range(1, len(values)):
        out = jnp.where(i == n, values[n], out)
    return out


def load_all(where, q_refs, o_refs, z_ref, c_ref, q_buf, o_buf, kv_buf, sem):
    y, z, c, x = (where[n] for n in range(4))
    copies = []
    for d in range(NY):
        i = lax.rem(y + d, NY)
        copies.append(pltpu.make_async_copy(q_refs[d], q_buf.at[i], sem.at[0]))
        copies.append(pltpu.make_async_copy(o_refs[d], o_buf.at[i], sem.at[0]))
    for e, ref in enumerate((z_ref, c_ref)):
        for d in range(NZ):
            block = lax.rem(z + NZ - d, NZ) * NC + (c if e == 0 else 1 - c)
            for r in range(NX):
                j = lax.rem(x + NX - r, NX)
                copies.append(
                    pltpu.make_async_copy(ref.at[d, r], kv_buf.at[:, j, block], sem.at[0])
                )
    for copy in copies:
        copy.start()
    for copy in copies:
        copy.wait()


def visible(where, ends, j, i, count, rows_from, rows):
    n = lax.broadcasted_iota(jnp.int32, (count, 1), 0)
    key_pos = (j * NZ * NC + n // SLICE) * BLK + where[0] * SLICE + n % SLICE
    r = lax.broadcasted_iota(jnp.int32, (1, rows), 1) + rows_from
    query_pos = (i * NZ * NC + where[1] * NC + where[2]) * BLK + r // GROUP
    return key_pos < jnp.maximum(query_pos + 1, pick(i, ends))


def each_pair(ends, pair):
    def full(p, carry):
        i = 1 + (p >= 1).astype(jnp.int32) + (p >= 3).astype(jnp.int32)
        pair(p - i * (i - 1) // 2, i, COL, False)
        return carry

    def diagonal(i, carry):
        pair(i, i, COL, True)
        return carry

    def crossing(i, carry):
        @pl.when(pick(i, ends) > (i + 1) * NZ * NC * BLK)
        def _():
            pair(i + 1, i, CROSS, True)

        return carry

    lax.fori_loop(0, NY, diagonal, 0)
    lax.fori_loop(0, NY * (NY - 1) // 2, full, 0)
    lax.fori_loop(0, NY - 1, crossing, 0)


def stats_kernel(where, seg_blocks, seg_audio, *refs):
    q_refs, o_refs = refs[:NY], refs[NY : 2 * NY]
    z_ref, c_ref, out, q_buf, o_buf, kv_buf, high, total, weighted, sem = refs[2 * NY :]
    load_all(where, q_refs, o_refs, z_ref, c_ref, q_buf, o_buf, kv_buf, sem)
    ends = span_ends(where, seg_blocks, seg_audio)
    high[...] = jnp.full_like(high, NEG)
    total[...] = jnp.zeros_like(total)
    weighted[...] = jnp.zeros_like(weighted)

    def pair(j, i, count, masked):
        k = kv_buf[0, j].reshape(COL, DH)[:count]
        v = kv_buf[1, j].reshape(COL, DH)[:count]
        for r in range(0, ROWS, RB):
            rows = slice(r, r + RB)
            s = dot_nt(k, q_buf[i, rows, :]) * SCALE2
            if masked:
                seen = visible(where, ends, j, i, count, r, RB)
                s = jnp.where(seen, s, NEG)
            dp = dot_nt(v, o_buf[i, rows, :]).reshape(count // 8, 8, RB)
            s = s.reshape(count // 8, 8, RB)
            old = high[i, :, rows]
            new = jnp.maximum(old, jnp.max(s, axis=0))
            fix = jnp.exp2(old - new)
            p = jnp.exp2(s - new[None])
            if masked:
                p = jnp.where(seen.reshape(count // 8, 8, RB), p, 0.0)
            high[i, :, rows] = new
            total[i, :, rows] = total[i, :, rows] * fix + jnp.sum(p, axis=0)
            weighted[i, :, rows] = weighted[i, :, rows] * fix + jnp.sum(p * dp, axis=0)

    each_pair(ends, pair)
    top = jnp.max(high[...], axis=1, keepdims=True)
    fix = jnp.exp2(high[...] - top)
    out[:, 0:1, :] = top
    out[:, 1:2, :] = jnp.sum(total[...] * fix, axis=1, keepdims=True)
    out[:, 2:3, :] = jnp.sum(weighted[...] * fix, axis=1, keepdims=True)


def grad_kernel(where, seg_blocks, seg_audio, *refs):
    q_refs, o_refs, st_refs = refs[:NY], refs[NY : 2 * NY], refs[2 * NY : 3 * NY]
    (z_ref, c_ref, dq_out, own_out, other_out, q_buf, o_buf, kv_buf, lse, delta, dq, dk, dv, sem) = (
        refs[3 * NY :]
    )
    load_all(where, q_refs, o_refs, z_ref, c_ref, q_buf, o_buf, kv_buf, sem)
    ends = span_ends(where, seg_blocks, seg_audio)
    tops = [ref[:, 0:1, :] for ref in st_refs]
    top = jnp.maximum(jnp.maximum(tops[0], tops[1]), jnp.maximum(tops[2], tops[3]))
    fixes = [jnp.exp2(t - top) for t in tops]
    total = sum(f * ref[:, 1:2, :] for f, ref in zip(fixes, st_refs))
    lse[...] = top + jnp.log2(total)
    delta[...] = sum(f * ref[:, 2:3, :] for f, ref in zip(fixes, st_refs)) / total
    dq[...] = jnp.zeros_like(dq)
    dk[...] = jnp.zeros_like(dk)
    dv[...] = jnp.zeros_like(dv)

    def pair(j, i, count, masked):
        k = kv_buf[0, j].reshape(COL, DH)[:count]
        v = kv_buf[1, j].reshape(COL, DH)[:count]
        p_parts, ds_parts = [], []
        for r in range(0, ROWS, RB):
            rows = slice(r, r + RB)
            s = dot_nt(k, q_buf[i, rows, :]) * SCALE2
            p = jnp.exp2(s - lse[i, :, rows])
            if masked:
                p = jnp.where(visible(where, ends, j, i, count, r, RB), p, 0.0)
            dp = dot_nt(v, o_buf[i, rows, :])
            ds = (p * (dp - delta[i, :, rows])).astype(BF)
            dq[i, :, rows] += dot_tn(k, ds)
            p_parts.append(p.astype(BF))
            ds_parts.append(ds)
        dv[j, :count, :] += dot_nn(jnp.concatenate(p_parts, axis=1), o_buf[i])
        dk[j, :count, :] += dot_nn(jnp.concatenate(ds_parts, axis=1), q_buf[i])

    each_pair(ends, pair)
    y, z, c, x = (where[n] for n in range(4))
    for d in range(NY):
        dq_out[d] = (dq[lax.rem(y + d, NY)].T * SCALE).astype(BF)
    for d in range(NZ):
        first = lax.rem(z + d, NZ) * NC
        for r in range(NX):
            j = lax.rem(x + NX - r, NX)
            for block, out in ((first + c, own_out), (first + 1 - c, other_out)):
                rows = pl.ds(pl.multiple_of(block * SLICE, SLICE), SLICE)
                out[d, r, 0] = dk[j, rows, :] * SCALE
                out[d, r, 1] = dv[j, rows, :]


def buffers():
    return [
        pltpu.VMEM((NY, ROWS, DH), BF),
        pltpu.VMEM((NY, ROWS, DH), BF),
        pltpu.VMEM((2, NY, NZ * NC, SLICE, DH), BF),
    ]


def stats_call(where, seg_blocks, seg_audio, q, o, z_all, c_all):
    return pl.pallas_call(
        stats_kernel,
        out_shape=jax.ShapeDtypeStruct((NY, 3, ROWS), F32),
        in_specs=[SM] * 3 + [HB] * (2 * NY + 2),
        out_specs=VM,
        scratch_shapes=buffers()
        + [pltpu.VMEM((NY, 8, ROWS), F32)] * 3
        + [pltpu.SemaphoreType.DMA((1,))],
        compiler_params=pltpu.CompilerParams(vmem_limit_bytes=56 << 20),
        name="stats",
    )(where, seg_blocks, seg_audio, *q, *o, z_all, c_all)


def grad_call(where, seg_blocks, seg_audio, q, o, st, z_all, c_all):
    part = jax.ShapeDtypeStruct((NZ, NX, 2, SLICE, DH), F32)
    return pl.pallas_call(
        grad_kernel,
        out_shape=(jax.ShapeDtypeStruct((NY, ROWS, DH), BF), part, part),
        in_specs=[SM] * 3 + [HB] * (2 * NY) + [VM] * NY + [HB] * 2,
        out_specs=(VM,) * 3,
        scratch_shapes=buffers()
        + [
            pltpu.VMEM((NY, 1, ROWS), F32),
            pltpu.VMEM((NY, 1, ROWS), F32),
            pltpu.VMEM((NY, DH, ROWS), F32),
            pltpu.VMEM((NY, COL, DH), F32),
            pltpu.VMEM((NY, COL, DH), F32),
            pltpu.SemaphoreType.DMA((1,)),
        ],
        compiler_params=pltpu.CompilerParams(vmem_limit_bytes=56 << 20),
        name="grads",
    )(where, seg_blocks, seg_audio, *q, *o, *st, z_all, c_all)


def shift(value, axis, size, by):
    return lax.ppermute(value, axis, [((n + by) % size, n) for n in range(size)])


def body(query, key, value, d_out, seg_blocks, seg_audio):
    y, z, c, x = (lax.axis_index(name).astype(jnp.int32) for name in ("y", "z", "c", "x"))
    where = jnp.stack([y, z, c, x])
    heads = jnp.stack([key, value]).transpose(2, 0, 1, 3)
    rounds = []
    for r in range(NX):
        piece = lax.dynamic_index_in_dim(heads, (y + r) % NX, 0, keepdims=False)
        perm = [
            (b * NX + a, a * NX + (b + r) % NX) for b in range(NY) for a in range(NX)
        ]
        rounds.append(lax.ppermute(piece, ("y", "x"), perm))
    own = jnp.stack(rounds)
    q0, o0 = query.reshape(ROWS, DH), d_out.reshape(ROWS, DH)
    q1, q3 = shift(q0, "y", NY, 1), shift(q0, "y", NY, -1)
    o1, o3 = shift(o0, "y", NY, 1), shift(o0, "y", NY, -1)
    q2, o2 = shift(q1, "y", NY, 1), shift(o3, "y", NY, -1)
    z_all = jnp.stack([own] + [shift(own, "z", NZ, -d) for d in range(1, NZ)])
    c_all = shift(z_all, "c", NC, 1)
    q, o = (q0, q1, q2, q3), (o0, o1, o2, o3)
    st = stats_call(where, seg_blocks, seg_audio, q, o, z_all, c_all)
    sts = (st,) + tuple(shift(st, "y", NY, d) for d in range(1, NY))
    dq, own_part, other_part = grad_call(
        where, seg_blocks, seg_audio, q, o, sts, z_all, c_all
    )
    dq_sum = dq[0].astype(F32)
    for d in range(1, NY):
        dq_sum = dq_sum + shift(dq[d], "y", NY, -d).astype(F32)
    d_query = dq_sum.astype(BF).reshape(BLK, GROUP, DH)
    both = own_part + shift(other_part, "c", NC, 1)
    low = both.astype(BF)
    kv_sum = both[0]
    for d in range(1, NZ):
        kv_sum = kv_sum + shift(low[d], "z", NZ, -d).astype(F32)
    kv_low = kv_sum.astype(BF)
    back = []
    for r in range(NX):
        perm = [
            (a * NX + (b + r) % NX, b * NX + a) for b in range(NY) for a in range(NX)
        ]
        back.append(lax.ppermute(kv_low[r], ("y", "x"), perm))
    ring = jnp.stack(back + back)
    ring = lax.dynamic_slice_in_dim(ring, (NX - y) % NX, NX, axis=0)
    ring = ring.transpose(1, 2, 0, 3)
    return (d_query, ring[0], ring[1])


def solution(mesh):
    fine = Mesh(mesh.devices.reshape(NY, NZ, NC, NX), ("y", "z", "c", "x"))
    ctx = ("y", "z", "c")
    rows, tokens = P(ctx, "x", None), P(("y", "z", "c", "x"), None, None)
    return jax.shard_map(
        body,
        mesh=fine,
        in_specs=(rows, tokens, tokens, rows, P(), P()),
        out_specs=(rows, tokens, tokens),
        check_vma=False,
    )
```

time: 564 us -> 168 us (0.30); the launches traced: 555 us -> 167 us
  waiting for transfers between devices: 346 us -> 48.5 us
  matrix products: 99.2 us -> 0 us
  starting transfers between devices: 7.63 us -> 74.4 us
  other arithmetic: 42 us -> 3.18 us
  Pallas kernels: 0 us -> 35 us
  local copies, waits for them, and re-layouts: 24.3 us -> 5.17 us
  blocking collectives: 18.1 us -> 0 us
  between operations: 16.1 us -> 1 us
    unnamed x4 -> x0, waiting for transfers between devices: 202 us -> none
    all_gather x2 -> x0, waiting for transfers between devices: 138 us -> none  [the longest x1 77.8 us: body(): lax.all_gather(values, 'ctx', axis=0, tiled=True)]
    dot_general x14 -> x0, matrix products: 99.2 us -> none  [the longest x8 70.1 us: contract_rows(): lax.dot_general(left, right, (((1,), (1,)), ((), ())), preferred_element_...]
    ppermute x0 -> x36, starting transfers between devices: none -> 74.4 us  [the longest x28 54.6 us: shift(): lax.ppermute(value, axis, [((n + by) % size, n) for n in range(size)])]
    ppermute x0 -> x36, waiting for transfers between devices: none -> 48.5 us  [the longest x28 39.6 us: shift(): lax.ppermute(value, axis, [((n + by) % size, n) for n in range(size)])]
    pallas_call x0 -> x2, Pallas kernels: none -> 35 us  [the longest x1 22.3 us: grad_call(): pl.pallas_call(grad_kernel, out_shape=(jax.ShapeDtypeStruct((NY, ROWS, DH...]
    all_to_all x2 -> x0, blocking collectives: 18.1 us -> none  [the longest x1 9.64 us: body(): lax.all_to_all(key, 'head', split_axis=1, concat_axis=0, tiled=True)]
    reduce_sum x4 -> x0, other arithmetic: 18 us -> none  [the longest x2 17 us: stats_compute(): return (new_high, jnp.sum(probs, axis=2), jnp.sum(probs * d_probs, axis=2))]
  transfers between devices with their start and end apart: 5 -> 36, of which waited for: 5 -> 15; matrix products, arithmetic and copies ran while one was open for 2% -> 1% of each run, Pallas kernels for 0% -> 0%
where the time goes in v1:
time: 168 us; the launch traced here: 167 us
  starting transfers between devices  74.4 us (44%)
  waiting for transfers between devices  48.5 us (29%)
  Pallas kernels  35 us (21%)
  local copies, waits for them, and re-layouts  5.17 us (3%)
  other arithmetic  3.18 us (2%)
    ppermute x28, starting transfers between devices, shift(): lax.ppermute(value, axis, [((n + by) % size, n) for n in range(size)])  54.6 us
    ppermute x28, waiting for transfers between devices, shift(): lax.ppermute(value, axis, [((n + by) % size, n) for n in range(size)])  39.6 us
    pallas_call x1, Pallas kernels, grad_call(): pl.pallas_call(grad_kernel, out_shape=(jax.ShapeDtypeStruct((NY, ROWS, DH...  22.3 us
    pallas_call x1, Pallas kernels, stats_call(): pl.pallas_call(stats_kernel, out_shape=jax.ShapeDtypeStruct((NY, 3, ROWS)...  12.7 us
    ppermute x4, starting transfers between devices, body(): back.append(lax.ppermute(kv_low[r], ('y', 'x'), perm))  12.3 us
    ppermute x4, starting transfers between devices, body(): rounds.append(lax.ppermute(piece, ('y', 'x'), perm))  7.45 us
    ppermute x4, waiting for transfers between devices, body(): back.append(lax.ppermute(kv_low[r], ('y', 'x'), perm))  7.2 us
    unnamed x43, local copies, waits for them, and re-layouts  4.22 us
  transfers between devices with their start and end apart: 36, of which 15 were waited for; matrix products, arithmetic and copies ran while one was open for 1% of the time, Pallas kernels for 0%

profile of v1, /device:TPU:16, one launch (start us, length us, event | category | flops | bytes accessed | tf_op | source)
XLA Modules:
  0.0 167.3 jit_solution(3093895487324138919)
XLA Ops:
  0.6 0.0 copy-start.3
  0.7 0.8 copy_bitcast_fusion
  1.5 4.7 %collective-permute-start.6 = (bf16[2,32,128]{2,1,0:T(8,128)(2,1)S(1)}, bf16[2,32,128]{2,1,0:T(8,128)(2,1)S(1)}, u32[]{:S(2)}, u32[]{:S(2)}) collective-permute-start(bf16[2,32,128]{2,1,0:T(8,128)(2,1)S(1)} %get-tuple-element.33), channel_id=1, source_target_pairs={{0,0},{1,64},{2,128},{3,192},{64,1},{65,65},{66,129},{67,193},{128... | collective-permute-start | bytes 49160 | tf_op jit(solution)/shard_map/ppermute | solution.py:259
  6.3 2.7 %collective-permute-start.7 = (bf16[2,32,128]{2,1,0:T(8,128)(2,1)S(1)}, bf16[2,32,128]{2,1,0:T(8,128)(2,1)S(1)}, u32[]{:S(2)}, u32[]{:S(2)}) collective-permute-start(bf16[2,32,128]{2,1,0:T(8,128)(2,1)S(1)} %get-tuple-element.34), channel_id=1, source_target_pairs={{0,1},{1,65},{2,129},{3,193},{64,2},{65,66},{66,130},{67,194},{128... | collective-permute-start | bytes 49160 | tf_op jit(solution)/shard_map/ppermute | solution.py:259
  9.0 4.3 %collective-permute-start = (bf16[1024,128]{1,0:T(8,128)(2,1)S(1)}, bf16[1024,128]{1,0:T(8,128)(2,1)S(1)}, u32[]{:S(2)}, u32[]{:S(2)}) collective-permute-start(bf16[1024,128]{1,0:T(8,128)(2,1)S(1)} %bitcast.109), channel_id=1, source_target_pairs={{64,0},{128,64},{192,128},{0,192},{65,1},{129,65},{193,129},{1,193... | collective-permute-start | bytes 786440 | tf_op jit(solution)/shard_map/ppermute | solution.py:246
  13.3 0.2 collective-permute-start.4
  13.5 0.7 collective-permute-done.8
  14.2 1.0 collective-permute-done.9
  15.3 6.4 %collective-permute-start.15 = (bf16[4,2,32,128]{3,2,1,0:T(8,128)(2,1)S(1)}, bf16[4,2,32,128]{3,2,1,0:T(8,128)(2,1)S(1)}, u32[]{:S(2)}, u32[]{:S(2)}) collective-permute-start(bf16[4,2,32,128]{3,2,1,0:T(8,128)(2,1)S(1)} %pad_maximum_fusion), channel_id=1, source_target_pairs={{16,0},{24,8},{32,16},{40,24},{48,32},{56,40},{0,48},{8,56},{17,1}... | collective-permute-start | bytes 196616 | tf_op jit(solution)/shard_map/ppermute | solution.py:246
  21.6 1.0 collective-permute-start.14
  22.6 1.9 %collective-permute-start.10 = (bf16[4,2,32,128]{3,2,1,0:T(8,128)(2,1)S(1)}, bf16[4,2,32,128]{3,2,1,0:T(8,128)(2,1)S(1)}, u32[]{:S(2)}, u32[]{:S(2)}) collective-permute-start(bf16[4,2,32,128]{3,2,1,0:T(8,128)(2,1)S(1)} %pad_maximum_fusion), channel_id=1, source_target_pairs={{56,0},{0,8},{8,16},{16,24},{24,32},{32,40},{40,48},{48,56},{57,1}... | collective-permute-start | bytes 196616 | tf_op jit(solution)/shard_map/ppermute | solution.py:246
  24.6 3.6 %collective-permute-done.10 = bf16[4,2,32,128]{3,2,1,0:T(8,128)(2,1)S(1)} collective-permute-done((bf16[4,2,32,128]{3,2,1,0:T(8,128)(2,1)S(1)}, bf16[4,2,32,128]{3,2,1,0:T(8,128)(2,1)S(1)}, u32[]{:S(2)}, u32[]{:S(2)}) %collective-permute-start.10) | collective-permute-done | bytes 65568 | tf_op jit(solution)/shard_map/ppermute | solution.py:246
  28.1 2.0 %collective-permute-start.11 = (bf16[4,2,32,128]{3,2,1,0:T(8,128)(2,1)S(1)}, bf16[4,2,32,128]{3,2,1,0:T(8,128)(2,1)S(1)}, u32[]{:S(2)}, u32[]{:S(2)}) collective-permute-start(bf16[4,2,32,128]{3,2,1,0:T(8,128)(2,1)S(1)} %pad_maximum_fusion), channel_id=1, source_target_pairs={{48,0},{56,8},{0,16},{8,24},{16,32},{24,40},{32,48},{40,56},{49,1}... | collective-permute-start | bytes 196616 | tf_op jit(solution)/shard_map/ppermute | solution.py:246
  30.2 4.4 %collective-permute-done.11 = bf16[4,2,32,128]{3,2,1,0:T(8,128)(2,1)S(1)} collective-permute-done((bf16[4,2,32,128]{3,2,1,0:T(8,128)(2,1)S(1)}, bf16[4,2,32,128]{3,2,1,0:T(8,128)(2,1)S(1)}, u32[]{:S(2)}, u32[]{:S(2)}) %collective-permute-start.11) | collective-permute-done | bytes 65568 | tf_op jit(solution)/shard_map/ppermute | solution.py:246
  34.6 0.4 collective-permute-start.12
  35.0 6.9 %collective-permute-done.12 = bf16[4,2,32,128]{3,2,1,0:T(8,128)(2,1)S(1)} collective-permute-done((bf16[4,2,32,128]{3,2,1,0:T(8,128)(2,1)S(1)}, bf16[4,2,32,128]{3,2,1,0:T(8,128)(2,1)S(1)}, u32[]{:S(2)}, u32[]{:S(2)}) %collective-permute-start.12) | collective-permute-done | bytes 65568 | tf_op jit(solution)/shard_map/ppermute | solution.py:246
  41.9 6.5 %collective-permute-start.13 = (bf16[4,2,32,128]{3,2,1,0:T(8,128)(2,1)S(1)}, bf16[4,2,32,128]{3,2,1,0:T(8,128)(2,1)S(1)}, u32[]{:S(2)}, u32[]{:S(2)}) collective-permute-start(bf16[4,2,32,128]{3,2,1,0:T(8,128)(2,1)S(1)} %pad_maximum_fusion), channel_id=1, source_target_pairs={{32,0},{40,8},{48,16},{56,24},{0,32},{8,40},{16,48},{24,56},{33,1}... | collective-permute-start | bytes 196616 | tf_op jit(solution)/shard_map/ppermute | solution.py:246
  48.4 2.2 %collective-permute-done.13 = bf16[4,2,32,128]{3,2,1,0:T(8,128)(2,1)S(1)} collective-permute-done((bf16[4,2,32,128]{3,2,1,0:T(8,128)(2,1)S(1)}, bf16[4,2,32,128]{3,2,1,0:T(8,128)(2,1)S(1)}, u32[]{:S(2)}, u32[]{:S(2)}) %collective-permute-start.13) | collective-permute-done | bytes 65568 | tf_op jit(solution)/shard_map/ppermute | solution.py:246
  50.6 3.5 %collective-permute-start.16 = (bf16[4,2,32,128]{3,2,1,0:T(8,128)(2,1)S(1)}, bf16[4,2,32,128]{3,2,1,0:T(8,128)(2,1)S(1)}, u32[]{:S(2)}, u32[]{:S(2)}) collective-permute-start(bf16[4,2,32,128]{3,2,1,0:T(8,128)(2,1)S(1)} %pad_maximum_fusion), channel_id=1, source_target_pairs={{8,0},{16,8},{24,16},{32,24},{40,32},{48,40},{56,48},{0,56},{9,1},... | collective-permute-start | bytes 196616 | tf_op jit(solution)/shard_map/ppermute | solution.py:246
  54.1 2.7 %collective-permute-done.16 = bf16[4,2,32,128]{3,2,1,0:T(8,128)(2,1)S(1)} collective-permute-done((bf16[4,2,32,128]{3,2,1,0:T(8,128)(2,1)S(1)}, bf16[4,2,32,128]{3,2,1,0:T(8,128)(2,1)S(1)}, u32[]{:S(2)}, u32[]{:S(2)}) %collective-permute-start.16) | collective-permute-done | bytes 65568 | tf_op jit(solution)/shard_map/ppermute | solution.py:246
  56.8 0.1 collective-permute-start.17
  56.9 1.1 collective-permute-start.2
  58.0 1.7 collective-permute-start.3
  59.6 1.9 %collective-permute-start.1 = (bf16[1024,128]{1,0:T(8,128)(2,1)S(1)}, bf16[1024,128]{1,0:T(8,128)(2,1)S(1)}, u32[]{:S(2)}, u32[]{:S(2)}) collective-permute-start(bf16[1024,128]{1,0:T(8,128)(2,1)S(1)} %collective-permute-done.refs_1_), channel_id=1, source_target_pairs={{64,0},{128,64},{192,128},{0,192},{65,1},{129,65},{193,129},{1,193... | collective-permute-start | bytes 786440 | tf_op jit(solution)/shard_map/ppermute | solution.py:246
  61.6 0.1 collective-permute-start.5
  61.7 0.7 pad_add_fusion.where
  62.3 4.4 %collective-permute-done.2.refs_3_ = bf16[1024,128]{1,0:T(8,128)(2,1)S(1)} collective-permute-done((bf16[1024,128]{1,0:T(8,128)(2,1)S(1)}, bf16[1024,128]{1,0:T(8,128)(2,1)S(1)}, u32[]{:S(2)}, u32[]{:S(2)}) %collective-permute-start.2) | collective-permute-done | bytes 262176 | tf_op jit(solution)/shard_map/ppermute | solution.py:246
  66.7 1.0 collective-permute-done.3.refs_5_
  67.7 5.1 %collective-permute-done.1.refs_2_ = bf16[1024,128]{1,0:T(8,128)(2,1)S(1)} collective-permute-done((bf16[1024,128]{1,0:T(8,128)(2,1)S(1)}, bf16[1024,128]{1,0:T(8,128)(2,1)S(1)}, u32[]{:S(2)}, u32[]{:S(2)}) %collective-permute-start.1) | collective-permute-done | bytes 262176 | tf_op jit(solution)/shard_map/ppermute | solution.py:246
  72.8 0.7 copy-done.9
  73.5 0.1 copy-done.10
  73.6 0.8 copy-done.1
  74.4 12.7 %stats.1.refs_8_ = f32[4,3,1024]{2,1,0:T(4,128)} custom-call(s32[4]{0:T(128)} %pad_add_fusion.where, s32[32]{0:T(128)} %seg_blocks.3, s32[32]{0:T(128)} %seg_audio.3, bf16[1024,128]{1,0:T(8,128)(2,1)} %bitcast.107, bf16[1024,128]{1,0:T(8,128)(2,1)} %copy-done.5, bf16[1024,128]{1,0:T(8,128)(2,1)} %copy-done.9, bf16[1024,128]{1,0:T(8,128)(2,1)} %copy-done.7, ...), custom_call_target="tpu_custom_call" | custom-call | tf_op jit(solution)/shard_map/stats/pallas_call | solution.py:211
  87.1 3.0 %collective-permute-start.20 = (f32[4,3,1024]{2,1,0:T(4,128)}, f32[4,3,1024]{2,1,0:T(4,128)S(1)}, u32[]{:S(2)}, u32[]{:S(2)}) collective-permute-start(f32[4,3,1024]{2,1,0:T(4,128)} %stats.1.refs_8_), channel_id=1, source_target_pairs={{192,0},{0,64},{64,128},{128,192},{193,1},{1,65},{65,129},{129,193... | collective-permute-start | bytes 147464 | tf_op jit(solution)/shard_map/ppermute | solution.py:246
  90.1 1.9 %collective-permute-start.18 = (f32[4,3,1024]{2,1,0:T(4,128)}, f32[4,3,1024]{2,1,0:T(4,128)S(1)}, u32[]{:S(2)}, u32[]{:S(2)}) collective-permute-start(f32[4,3,1024]{2,1,0:T(4,128)} %stats.1.refs_8_), channel_id=1, source_target_pairs={{64,0},{128,64},{192,128},{0,192},{65,1},{129,65},{193,129},{1,193... | collective-permute-start | bytes 147464 | tf_op jit(solution)/shard_map/ppermute | solution.py:246
  92.0 0.3 collective-permute-done.20.refs_11_
  92.3 3.8 %collective-permute-done.19.refs_10_ = f32[4,3,1024]{2,1,0:T(4,128)S(1)} collective-permute-done((f32[4,3,1024]{2,1,0:T(4,128)}, f32[4,3,1024]{2,1,0:T(4,128)S(1)}, u32[]{:S(2)}, u32[]{:S(2)}) %collective-permute-start.19) | collective-permute-done | bytes 49184 | tf_op jit(solution)/shard_map/ppermute | solution.py:246
  96.1 0.6 copy-done.12
  96.7 0.6 copy-done.13
  97.3 22.3 %grads.1 = (bf16[4,1024,128]{2,1,0:T(8,128)(2,1)}, f32[8,4,2,32,128]{4,3,2,1,0:T(8,128)}, f32[8,4,2,32,128]{4,3,2,1,0:T(8,128)}) custom-call(s32[4]{0:T(128)} %pad_add_fusion.where, s32[32]{0:T(128)} %seg_blocks.3, s32[32]{0:T(128)} %seg_audio.3, bf16[1024,128]{1,0:T(8,128)(2,1)} %bitcast.108, bf16[1024,128]{1,0:T(8,128)(2,1)} %copy-done.5, ...), custom_call_target="tpu_custom_call" | custom-call | tf_op jit(solution)/shard_map/grads/pallas_call | solution.py:226
  119.6 0.1 collective-permute-start.24
  119.7 2.9 %collective-permute-done.24 = f32[8,4,2,32,128]{4,3,2,1,0:T(8,128)S(1)} collective-permute-done((f32[8,4,2,32,128]{4,3,2,1,0:T(8,128)}, f32[8,4,2,32,128]{4,3,2,1,0:T(8,128)S(1)}, u32[]{:S(2)}, u32[]{:S(2)}) %collective-permute-start.24) | collective-permute-done | bytes 1048608 | tf_op jit(solution)/shard_map/ppermute | solution.py:246
  122.6 1.5 fusion.20
  124.2 2.1 %collective-permute-start.25 = (bf16[4,2,32,128]{3,2,1,0:T(8,128)(2,1)S(1)}, bf16[4,2,32,128]{3,2,1,0:T(8,128)(2,1)S(1)}, u32[]{:S(2)}, u32[]{:S(2)}) collective-permute-start(bf16[4,2,32,128]{3,2,1,0:T(8,128)(2,1)S(1)} %get-tuple-element.20), channel_id=1, source_target_pairs={{56,0},{0,8},{8,16},{16,24},{24,32},{32,40},{40,48},{48,56},{57,1}... | collective-permute-start | bytes 196616 | tf_op jit(solution)/shard_map/ppermute | solution.py:246
  126.3 1.3 collective-permute-start.31
  127.6 1.2 collective-permute-start.30
  128.7 1.4 collective-permute-start.29
  130.1 5.1 %collective-permute-start.28 = (bf16[4,2,32,128]{3,2,1,0:T(8,128)(2,1)S(1)}, bf16[4,2,32,128]{3,2,1,0:T(8,128)(2,1)S(1)}, u32[]{:S(2)}, u32[]{:S(2)}) collective-permute-start(bf16[4,2,32,128]{3,2,1,0:T(8,128)(2,1)S(1)} %get-tuple-element.24), channel_id=1, source_target_pairs={{32,0},{40,8},{48,16},{56,24},{0,32},{8,40},{16,48},{24,56},{33,1}... | collective-permute-start | bytes 196616 | tf_op jit(solution)/shard_map/ppermute | solution.py:246
  135.2 0.2 collective-permute-start.27
  135.4 2.6 %collective-permute-start.26 = (bf16[4,2,32,128]{3,2,1,0:T(8,128)(2,1)S(1)}, bf16[4,2,32,128]{3,2,1,0:T(8,128)(2,1)S(1)}, u32[]{:S(2)}, u32[]{:S(2)}) collective-permute-start(bf16[4,2,32,128]{3,2,1,0:T(8,128)(2,1)S(1)} %get-tuple-element.26), channel_id=1, source_target_pairs={{48,0},{56,8},{0,16},{8,24},{16,32},{24,40},{32,48},{40,56},{49,1}... | collective-permute-start | bytes 196616 | tf_op jit(solution)/shard_map/ppermute | solution.py:246
  138.1 0.1 slice_bitcast_fusion.2
  138.1 1.4 collective-permute-start.21
  139.6 0.7 collective-permute-start.23
  140.2 2.6 %collective-permute-start.22 = (bf16[1024,128]{1,0:T(8,128)(2,1)S(1)}, bf16[1024,128]{1,0:T(8,128)(2,1)S(1)}, u32[]{:S(2)}, u32[]{:S(2)}) collective-permute-start(bf16[1024,128]{1,0:T(8,128)(2,1)S(1)} %get-tuple-element.19), channel_id=1, source_target_pairs={{128,0},{192,64},{0,128},{64,192},{129,1},{193,65},{1,129},{65,193... | collective-permute-start | bytes 786440 | tf_op jit(solution)/shard_map/ppermute | solution.py:246
  142.9 2.5 %collective-permute-done.27 = bf16[4,2,32,128]{3,2,1,0:T(8,128)(2,1)S(1)} collective-permute-done((bf16[4,2,32,128]{3,2,1,0:T(8,128)(2,1)S(1)}, bf16[4,2,32,128]{3,2,1,0:T(8,128)(2,1)S(1)}, u32[]{:S(2)}, u32[]{:S(2)}) %collective-permute-start.27) | collective-permute-done | bytes 65568 | tf_op jit(solution)/shard_map/ppermute | solution.py:246
  145.4 0.1 fusion.11
  145.5 6.6 %collective-permute-start.32 = (bf16[2,32,128]{2,1,0:T(8,128)(2,1)S(1)}, bf16[2,32,128]{2,1,0:T(8,128)(2,1)S(1)}, u32[]{:S(2)}, u32[]{:S(2)}) collective-permute-start(bf16[2,32,128]{2,1,0:T(8,128)(2,1)S(1)} %get-tuple-element.32), channel_id=1, source_target_pairs={{0,0},{64,1},{128,2},{192,3},{1,64},{65,65},{129,66},{193,67},{2,1... | collective-permute-start | bytes 49160 | tf_op jit(solution)/shard_map/ppermute | solution.py:288
  152.1 0.9 fusion.3
  153.0 3.9 %collective-permute-start.35 = (bf16[2,32,128]{2,1,0:T(8,128)(2,1)S(1)}, bf16[2,32,128]{2,1,0:T(8,128)(2,1)S(1)}, u32[]{:S(2)}, u32[]{:S(2)}) collective-permute-start(bf16[2,32,128]{2,1,0:T(8,128)(2,1)S(1)} %get-tuple-element.29), channel_id=1, source_target_pairs={{3,0},{67,1},{131,2},{195,3},{0,64},{64,65},{128,66},{192,67},{1,1... | collective-permute-start | bytes 49160 | tf_op jit(solution)/shard_map/ppermute | solution.py:288
  156.8 1.7 %collective-permute-start.34 = (bf16[2,32,128]{2,1,0:T(8,128)(2,1)S(1)}, bf16[2,32,128]{2,1,0:T(8,128)(2,1)S(1)}, u32[]{:S(2)}, u32[]{:S(2)}) collective-permute-start(bf16[2,32,128]{2,1,0:T(8,128)(2,1)S(1)} %get-tuple-element.30), channel_id=1, source_target_pairs={{2,0},{66,1},{130,2},{194,3},{3,64},{67,65},{131,66},{195,67},{0,1... | collective-permute-start | bytes 49160 | tf_op jit(solution)/shard_map/ppermute | solution.py:288
  158.5 0.2 collective-permute-start.33
  158.7 7.2 %collective-permute-done.33 = bf16[2,32,128]{2,1,0:T(8,128)(2,1)S(1)} collective-permute-done((bf16[2,32,128]{2,1,0:T(8,128)(2,1)S(1)}, bf16[2,32,128]{2,1,0:T(8,128)(2,1)S(1)}, u32[]{:S(2)}, u32[]{:S(2)}) %collective-permute-start.33) | collective-permute-done | bytes 16416 | tf_op jit(solution)/shard_map/ppermute | solution.py:288
  166.0 0.6 copy.14
  166.6 0.6 copy.13
  (68 shorter events, 0.4 us)
Async XLA Ops:
  0.6 8.4 %copy-start.3 = (bf16[128,8,128]{2,1,0:T(8,128)(2,1)S(1)}, bf16[128,8,128]{2,1,0:T(8,128)(2,1)}, u32[]{:S(2)}) copy-start(bf16[128,8,128]{2,1,0:T(8,128)(2,1)} %param.6) | copy-start | bytes 786436
  1.5 11.8 %collective-permute-start.6 = (bf16[2,32,128]{2,1,0:T(8,128)(2,1)S(1)}, bf16[2,32,128]{2,1,0:T(8,128)(2,1)S(1)}, u32[]{:S(2)}, u32[]{:S(2)}) collective-permute-start(bf16[2,32,128]{2,1,0:T(8,128)(2,1)S(1)} %get-tuple-element.33), channel_id=1, source_target_pairs={{0,0},{1,64},{2,128},{3,192},{64,1},{65,65},{66,129},{67,193},{128... | collective-permute-start | bytes 49160 | tf_op jit(solution)/shard_map/ppermute | solution.py:259
  6.3 7.3 %collective-permute-start.7 = (bf16[2,32,128]{2,1,0:T(8,128)(2,1)S(1)}, bf16[2,32,128]{2,1,0:T(8,128)(2,1)S(1)}, u32[]{:S(2)}, u32[]{:S(2)}) collective-permute-start(bf16[2,32,128]{2,1,0:T(8,128)(2,1)S(1)} %get-tuple-element.34), channel_id=1, source_target_pairs={{0,1},{1,65},{2,129},{3,193},{64,2},{65,66},{66,130},{67,194},{128... | collective-permute-start | bytes 49160 | tf_op jit(solution)/shard_map/ppermute | solution.py:259
  9.0 5.2 %collective-permute-start.8 = (bf16[2,32,128]{2,1,0:T(8,128)(2,1)S(1)}, bf16[2,32,128]{2,1,0:T(8,128)(2,1)S(1)}, u32[]{:S(2)}, u32[]{:S(2)}) collective-permute-start(bf16[2,32,128]{2,1,0:T(8,128)(2,1)S(1)} %get-tuple-element.35), channel_id=1, source_target_pairs={{0,2},{1,66},{2,130},{3,194},{64,3},{65,67},{66,131},{67,195},{128... | collective-permute-start | bytes 49160 | tf_op jit(solution)/shard_map/ppermute | solution.py:259
  9.0 6.2 %collective-permute-start.9 = (bf16[2,32,128]{2,1,0:T(8,128)(2,1)S(1)}, bf16[2,32,128]{2,1,0:T(8,128)(2,1)S(1)}, u32[]{:S(2)}, u32[]{:S(2)}) collective-permute-start(bf16[2,32,128]{2,1,0:T(8,128)(2,1)S(1)} %get-tuple-element.36), channel_id=1, source_target_pairs={{0,3},{1,67},{2,131},{3,195},{64,0},{65,64},{66,128},{67,192},{128... | collective-permute-start | bytes 49160 | tf_op jit(solution)/shard_map/ppermute | solution.py:259
  9.0 50.6 %collective-permute-start = (bf16[1024,128]{1,0:T(8,128)(2,1)S(1)}, bf16[1024,128]{1,0:T(8,128)(2,1)S(1)}, u32[]{:S(2)}, u32[]{:S(2)}) collective-permute-start(bf16[1024,128]{1,0:T(8,128)(2,1)S(1)} %bitcast.109), channel_id=1, source_target_pairs={{64,0},{128,64},{192,128},{0,192},{65,1},{129,65},{193,129},{1,193... | collective-permute-start | bytes 786440 | tf_op jit(solution)/shard_map/ppermute | solution.py:246
  13.3 48.3 %collective-permute-start.4 = (bf16[1024,128]{1,0:T(8,128)(2,1)}, bf16[1024,128]{1,0:T(8,128)(2,1)S(1)}, u32[]{:S(2)}, u32[]{:S(2)}) collective-permute-start(bf16[1024,128]{1,0:T(8,128)(2,1)} %bitcast.111), channel_id=1, source_target_pairs={{192,0},{0,64},{64,128},{128,192},{193,1},{1,65},{65,129},{129,193... | collective-permute-start | bytes 786440 | tf_op jit(solution)/shard_map/ppermute | solution.py:246
  15.3 38.8 %collective-permute-start.15 = (bf16[4,2,32,128]{3,2,1,0:T(8,128)(2,1)S(1)}, bf16[4,2,32,128]{3,2,1,0:T(8,128)(2,1)S(1)}, u32[]{:S(2)}, u32[]{:S(2)}) collective-permute-start(bf16[4,2,32,128]{3,2,1,0:T(8,128)(2,1)S(1)} %pad_maximum_fusion), channel_id=1, source_target_pairs={{16,0},{24,8},{32,16},{40,24},{48,32},{56,40},{0,48},{8,56},{17,1}... | collective-permute-start | bytes 196616 | tf_op jit(solution)/shard_map/ppermute | solution.py:246
  21.6 32.4 %collective-permute-start.14 = (bf16[4,2,32,128]{3,2,1,0:T(8,128)(2,1)S(1)}, bf16[4,2,32,128]{3,2,1,0:T(8,128)(2,1)S(1)}, u32[]{:S(2)}, u32[]{:S(2)}) collective-permute-start(bf16[4,2,32,128]{3,2,1,0:T(8,128)(2,1)S(1)} %pad_maximum_fusion), channel_id=1, source_target_pairs={{24,0},{32,8},{40,16},{48,24},{56,32},{0,40},{8,48},{16,56},{25,1}... | collective-permute-start | bytes 196616 | tf_op jit(solution)/shard_map/ppermute | solution.py:246
  22.6 5.5 %collective-permute-start.10 = (bf16[4,2,32,128]{3,2,1,0:T(8,128)(2,1)S(1)}, bf16[4,2,32,128]{3,2,1,0:T(8,128)(2,1)S(1)}, u32[]{:S(2)}, u32[]{:S(2)}) collective-permute-start(bf16[4,2,32,128]{3,2,1,0:T(8,128)(2,1)S(1)} %pad_maximum_fusion), channel_id=1, source_target_pairs={{56,0},{0,8},{8,16},{16,24},{24,32},{32,40},{40,48},{48,56},{57,1}... | collective-permute-start | bytes 196616 | tf_op jit(solution)/shard_map/ppermute | solution.py:246
  28.1 6.5 %collective-permute-start.11 = (bf16[4,2,32,128]{3,2,1,0:T(8,128)(2,1)S(1)}, bf16[4,2,32,128]{3,2,1,0:T(8,128)(2,1)S(1)}, u32[]{:S(2)}, u32[]{:S(2)}) collective-permute-start(bf16[4,2,32,128]{3,2,1,0:T(8,128)(2,1)S(1)} %pad_maximum_fusion), channel_id=1, source_target_pairs={{48,0},{56,8},{0,16},{8,24},{16,32},{24,40},{32,48},{40,56},{49,1}... | collective-permute-start | bytes 196616 | tf_op jit(solution)/shard_map/ppermute | solution.py:246
  34.6 7.3 %collective-permute-start.12 = (bf16[4,2,32,128]{3,2,1,0:T(8,128)(2,1)S(1)}, bf16[4,2,32,128]{3,2,1,0:T(8,128)(2,1)S(1)}, u32[]{:S(2)}, u32[]{:S(2)}) collective-permute-start(bf16[4,2,32,128]{3,2,1,0:T(8,128)(2,1)S(1)} %pad_maximum_fusion), channel_id=1, source_target_pairs={{40,0},{48,8},{56,16},{0,24},{8,32},{16,40},{24,48},{32,56},{41,1}... | collective-permute-start | bytes 196616 | tf_op jit(solution)/shard_map/ppermute | solution.py:246
  41.9 8.7 %collective-permute-start.13 = (bf16[4,2,32,128]{3,2,1,0:T(8,128)(2,1)S(1)}, bf16[4,2,32,128]{3,2,1,0:T(8,128)(2,1)S(1)}, u32[]{:S(2)}, u32[]{:S(2)}) collective-permute-start(bf16[4,2,32,128]{3,2,1,0:T(8,128)(2,1)S(1)} %pad_maximum_fusion), channel_id=1, source_target_pairs={{32,0},{40,8},{48,16},{56,24},{0,32},{8,40},{16,48},{24,56},{33,1}... | collective-permute-start | bytes 196616 | tf_op jit(solution)/shard_map/ppermute | solution.py:246
  48.4 9.6 %copy-start.4 = (bf16[128,8,128]{2,1,0:T(8,128)(2,1)S(1)}, bf16[128,8,128]{2,1,0:T(8,128)(2,1)}, u32[]{:S(2)}) copy-start(bf16[128,8,128]{2,1,0:T(8,128)(2,1)} %param.9) | copy-start | bytes 786436
  50.6 6.2 %collective-permute-start.16 = (bf16[4,2,32,128]{3,2,1,0:T(8,128)(2,1)S(1)}, bf16[4,2,32,128]{3,2,1,0:T(8,128)(2,1)S(1)}, u32[]{:S(2)}, u32[]{:S(2)}) collective-permute-start(bf16[4,2,32,128]{3,2,1,0:T(8,128)(2,1)S(1)} %pad_maximum_fusion), channel_id=1, source_target_pairs={{8,0},{16,8},{24,16},{32,24},{40,32},{48,40},{56,48},{0,56},{9,1},... | collective-permute-start | bytes 196616 | tf_op jit(solution)/shard_map/ppermute | solution.py:246
  56.8 15.9 %copy-start = (bf16[8,4,2,32,128]{4,3,2,1,0:T(8,128)(2,1)}, bf16[8,4,2,32,128]{4,3,2,1,0:T(8,128)(2,1)S(1)}, u32[]{:S(2)}) copy-start(bf16[8,4,2,32,128]{4,3,2,1,0:T(8,128)(2,1)S(1)} %bitcast_dynamic-update-slice_fusion.refs_8_.refs_12_) | copy-start | bytes 1572868
  56.8 15.9 %collective-permute-start.17 = (bf16[8,4,2,32,128]{4,3,2,1,0:T(8,128)(2,1)S(1)}, bf16[8,4,2,32,128]{4,3,2,1,0:T(8,128)(2,1)S(1)}, u32[]{:S(2)}, u32[]{:S(2)}) collective-permute-start(bf16[8,4,2,32,128]{4,3,2,1,0:T(8,128)(2,1)S(1)} %bitcast_dynamic-update-slice_fusion.refs_8_.refs_12_), channel_id=1, source_target_pairs={{4,0},{0,4},{5,1},{1,5},{6,2},{2,6},{7,3},{3,7},{12,8},{8,12},{13,... | collective-permute-start | bytes 1572872 | tf_op jit(solution)/shard_map/ppermute | solution.py:246
  56.9 9.8 %collective-permute-start.2 = (bf16[1024,128]{1,0:T(8,128)(2,1)S(1)}, bf16[1024,128]{1,0:T(8,128)(2,1)S(1)}, u32[]{:S(2)}, u32[]{:S(2)}) collective-permute-start(bf16[1024,128]{1,0:T(8,128)(2,1)S(1)} %bitcast.110), channel_id=1, source_target_pairs={{192,0},{0,64},{64,128},{128,192},{193,1},{1,65},{65,129},{129,193... | collective-permute-start | bytes 786440 | tf_op jit(solution)/shard_map/ppermute | solution.py:246
  58.0 9.7 %collective-permute-start.3 = (bf16[1024,128]{1,0:T(8,128)(2,1)S(1)}, bf16[1024,128]{1,0:T(8,128)(2,1)S(1)}, u32[]{:S(2)}, u32[]{:S(2)}) collective-permute-start(bf16[1024,128]{1,0:T(8,128)(2,1)S(1)} %bitcast.114), channel_id=1, source_target_pairs={{64,0},{128,64},{192,128},{0,192},{65,1},{129,65},{193,129},{1,193... | collective-permute-start | bytes 786440 | tf_op jit(solution)/shard_map/ppermute | solution.py:246
  59.6 13.1 %copy-start.5 = (bf16[1024,128]{1,0:T(8,128)(2,1)}, bf16[1024,128]{1,0:T(8,128)(2,1)S(1)}, u32[]{:S(2)}) copy-start(bf16[1024,128]{1,0:T(8,128)(2,1)S(1)} %collective-permute-done.refs_1_) | copy-start | bytes 786436
  59.6 13.1 %collective-permute-start.1 = (bf16[1024,128]{1,0:T(8,128)(2,1)S(1)}, bf16[1024,128]{1,0:T(8,128)(2,1)S(1)}, u32[]{:S(2)}, u32[]{:S(2)}) collective-permute-start(bf16[1024,128]{1,0:T(8,128)(2,1)S(1)} %collective-permute-done.refs_1_), channel_id=1, source_target_pairs={{64,0},{128,64},{192,128},{0,192},{65,1},{129,65},{193,129},{1,193... | collective-permute-start | bytes 786440 | tf_op jit(solution)/shard_map/ppermute | solution.py:246
  61.6 11.2 %copy-start.6 = (bf16[1024,128]{1,0:T(8,128)(2,1)}, bf16[1024,128]{1,0:T(8,128)(2,1)S(1)}, u32[]{:S(2)}) copy-start(bf16[1024,128]{1,0:T(8,128)(2,1)S(1)} %collective-permute-done.4.refs_7_) | copy-start | bytes 786436
  61.6 11.2 %collective-permute-start.5 = (bf16[1024,128]{1,0:T(8,128)(2,1)S(1)}, bf16[1024,128]{1,0:T(8,128)(2,1)S(1)}, u32[]{:S(2)}, u32[]{:S(2)}) collective-permute-start(bf16[1024,128]{1,0:T(8,128)(2,1)S(1)} %collective-permute-done.4.refs_7_), channel_id=1, source_target_pairs={{192,0},{0,64},{64,128},{128,192},{193,1},{1,65},{65,129},{129,193... | collective-permute-start | bytes 786440 | tf_op jit(solution)/shard_map/ppermute | solution.py:246
  66.7 6.1 %copy-start.7 = (bf16[1024,128]{1,0:T(8,128)(2,1)}, bf16[1024,128]{1,0:T(8,128)(2,1)S(1)}, u32[]{:S(2)}) copy-start(bf16[1024,128]{1,0:T(8,128)(2,1)S(1)} %collective-permute-done.2.refs_3_) | copy-start | bytes 786436
  67.7 5.1 %copy-start.8 = (bf16[1024,128]{1,0:T(8,128)(2,1)}, bf16[1024,128]{1,0:T(8,128)(2,1)S(1)}, u32[]{:S(2)}) copy-start(bf16[1024,128]{1,0:T(8,128)(2,1)S(1)} %collective-permute-done.3.refs_5_) | copy-start | bytes 786436
  72.7 0.7 copy-start.9
  72.7 0.8 copy-start.10
  73.6 0.8 copy-start.1
  87.1 5.2 %collective-permute-start.20 = (f32[4,3,1024]{2,1,0:T(4,128)}, f32[4,3,1024]{2,1,0:T(4,128)S(1)}, u32[]{:S(2)}, u32[]{:S(2)}) collective-permute-start(f32[4,3,1024]{2,1,0:T(4,128)} %stats.1.refs_8_), channel_id=1, source_target_pairs={{192,0},{0,64},{64,128},{128,192},{193,1},{1,65},{65,129},{129,193... | collective-permute-start | bytes 147464 | tf_op jit(solution)/shard_map/ppermute | solution.py:246
  90.1 6.0 %collective-permute-start.19 = (f32[4,3,1024]{2,1,0:T(4,128)}, f32[4,3,1024]{2,1,0:T(4,128)S(1)}, u32[]{:S(2)}, u32[]{:S(2)}) collective-permute-start(f32[4,3,1024]{2,1,0:T(4,128)} %stats.1.refs_8_), channel_id=1, source_target_pairs={{128,0},{192,64},{0,128},{64,192},{129,1},{193,65},{1,129},{65,193... | collective-permute-start | bytes 147464 | tf_op jit(solution)/shard_map/ppermute | solution.py:246
  90.1 6.0 %collective-permute-start.18 = (f32[4,3,1024]{2,1,0:T(4,128)}, f32[4,3,1024]{2,1,0:T(4,128)S(1)}, u32[]{:S(2)}, u32[]{:S(2)}) collective-permute-start(f32[4,3,1024]{2,1,0:T(4,128)} %stats.1.refs_8_), channel_id=1, source_target_pairs={{64,0},{128,64},{192,128},{0,192},{65,1},{129,65},{193,129},{1,193... | collective-permute-start | bytes 147464 | tf_op jit(solution)/shard_map/ppermute | solution.py:246
  92.3 3.8 %copy-start.11 = (f32[4,3,1024]{2,1,0:T(4,128)}, f32[4,3,1024]{2,1,0:T(4,128)S(1)}, u32[]{:S(2)}) copy-start(f32[4,3,1024]{2,1,0:T(4,128)S(1)} %collective-permute-done.20.refs_11_) | copy-start | bytes 147460
  96.1 0.6 copy-start.12
  96.7 0.6 copy-start.13
  119.6 3.0 %collective-permute-start.24 = (f32[8,4,2,32,128]{4,3,2,1,0:T(8,128)}, f32[8,4,2,32,128]{4,3,2,1,0:T(8,128)S(1)}, u32[]{:S(2)}, u32[]{:S(2)}) collective-permute-start(f32[8,4,2,32,128]{4,3,2,1,0:T(8,128)} %get-tuple-element.8), channel_id=1, source_target_pairs={{4,0},{0,4},{5,1},{1,5},{6,2},{2,6},{7,3},{3,7},{12,8},{8,12},{13,... | collective-permute-start | bytes 3145736 | tf_op jit(solution)/shard_map/ppermute | solution.py:246
  122.6 15.5 %copy-start.2 = (bf16[4,1024,128]{2,1,0:T(8,128)(2,1)S(1)}, bf16[4,1024,128]{2,1,0:T(8,128)(2,1)}, u32[]{:S(2)}) copy-start(bf16[4,1024,128]{2,1,0:T(8,128)(2,1)} %get-tuple-element.6) | copy-start | bytes 3145732
  124.2 11.0 %collective-permute-start.25 = (bf16[4,2,32,128]{3,2,1,0:T(8,128)(2,1)S(1)}, bf16[4,2,32,128]{3,2,1,0:T(8,128)(2,1)S(1)}, u32[]{:S(2)}, u32[]{:S(2)}) collective-permute-start(bf16[4,2,32,128]{3,2,1,0:T(8,128)(2,1)S(1)} %get-tuple-element.20), channel_id=1, source_target_pairs={{56,0},{0,8},{8,16},{16,24},{24,32},{32,40},{40,48},{48,56},{57,1}... | collective-permute-start | bytes 196616 | tf_op jit(solution)/shard_map/ppermute | solution.py:246
  126.3 9.2 %collective-permute-start.31 = (bf16[4,2,32,128]{3,2,1,0:T(8,128)(2,1)S(1)}, bf16[4,2,32,128]{3,2,1,0:T(8,128)(2,1)S(1)}, u32[]{:S(2)}, u32[]{:S(2)}) collective-permute-start(bf16[4,2,32,128]{3,2,1,0:T(8,128)(2,1)S(1)} %get-tuple-element.21), channel_id=1, source_target_pairs={{8,0},{16,8},{24,16},{32,24},{40,32},{48,40},{56,48},{0,56},{9,1},... | collective-permute-start | bytes 196616 | tf_op jit(solution)/shard_map/ppermute | solution.py:246
  127.6 10.6 %collective-permute-start.30 = (bf16[4,2,32,128]{3,2,1,0:T(8,128)(2,1)S(1)}, bf16[4,2,32,128]{3,2,1,0:T(8,128)(2,1)S(1)}, u32[]{:S(2)}, u32[]{:S(2)}) collective-permute-start(bf16[4,2,32,128]{3,2,1,0:T(8,128)(2,1)S(1)} %get-tuple-element.22), channel_id=1, source_target_pairs={{16,0},{24,8},{32,16},{40,24},{48,32},{56,40},{0,48},{8,56},{17,1}... | collective-permute-start | bytes 196616 | tf_op jit(solution)/shard_map/ppermute | solution.py:246
  128.7 10.9 %collective-permute-start.29 = (bf16[4,2,32,128]{3,2,1,0:T(8,128)(2,1)S(1)}, bf16[4,2,32,128]{3,2,1,0:T(8,128)(2,1)S(1)}, u32[]{:S(2)}, u32[]{:S(2)}) collective-permute-start(bf16[4,2,32,128]{3,2,1,0:T(8,128)(2,1)S(1)} %get-tuple-element.23), channel_id=1, source_target_pairs={{24,0},{32,8},{40,16},{48,24},{56,32},{0,40},{8,48},{16,56},{25,1}... | collective-permute-start | bytes 196616 | tf_op jit(solution)/shard_map/ppermute | solution.py:246
  130.1 10.1 %collective-permute-start.28 = (bf16[4,2,32,128]{3,2,1,0:T(8,128)(2,1)S(1)}, bf16[4,2,32,128]{3,2,1,0:T(8,128)(2,1)S(1)}, u32[]{:S(2)}, u32[]{:S(2)}) collective-permute-start(bf16[4,2,32,128]{3,2,1,0:T(8,128)(2,1)S(1)} %get-tuple-element.24), channel_id=1, source_target_pairs={{32,0},{40,8},{48,16},{56,24},{0,32},{8,40},{16,48},{24,56},{33,1}... | collective-permute-start | bytes 196616 | tf_op jit(solution)/shard_map/ppermute | solution.py:246
  135.2 10.2 %collective-permute-start.27 = (bf16[4,2,32,128]{3,2,1,0:T(8,128)(2,1)S(1)}, bf16[4,2,32,128]{3,2,1,0:T(8,128)(2,1)S(1)}, u32[]{:S(2)}, u32[]{:S(2)}) collective-permute-start(bf16[4,2,32,128]{3,2,1,0:T(8,128)(2,1)S(1)} %get-tuple-element.25), channel_id=1, source_target_pairs={{40,0},{48,8},{56,16},{0,24},{8,32},{16,40},{24,48},{32,56},{41,1}... | collective-permute-start | bytes 196616 | tf_op jit(solution)/shard_map/ppermute | solution.py:246
  135.4 9.9 %collective-permute-start.26 = (bf16[4,2,32,128]{3,2,1,0:T(8,128)(2,1)S(1)}, bf16[4,2,32,128]{3,2,1,0:T(8,128)(2,1)S(1)}, u32[]{:S(2)}, u32[]{:S(2)}) collective-permute-start(bf16[4,2,32,128]{3,2,1,0:T(8,128)(2,1)S(1)} %get-tuple-element.26), channel_id=1, source_target_pairs={{48,0},{56,8},{0,16},{8,24},{16,32},{24,40},{32,48},{40,56},{49,1}... | collective-permute-start | bytes 196616 | tf_op jit(solution)/shard_map/ppermute | solution.py:246
  138.1 13.9 %collective-permute-start.21 = (bf16[1024,128]{1,0:T(8,128)(2,1)S(1)}, bf16[1024,128]{1,0:T(8,128)(2,1)S(1)}, u32[]{:S(2)}, u32[]{:S(2)}) collective-permute-start(bf16[1024,128]{1,0:T(8,128)(2,1)S(1)} %get-tuple-element.17), channel_id=1, source_target_pairs={{192,0},{0,64},{64,128},{128,192},{193,1},{1,65},{65,129},{129,193... | collective-permute-start | bytes 786440 | tf_op jit(solution)/shard_map/ppermute | solution.py:246
  139.6 12.5 %collective-permute-start.23 = (bf16[1024,128]{1,0:T(8,128)(2,1)S(1)}, bf16[1024,128]{1,0:T(8,128)(2,1)S(1)}, u32[]{:S(2)}, u32[]{:S(2)}) collective-permute-start(bf16[1024,128]{1,0:T(8,128)(2,1)S(1)} %get-tuple-element.18), channel_id=1, source_target_pairs={{64,0},{128,64},{192,128},{0,192},{65,1},{129,65},{193,129},{1,193... | collective-permute-start | bytes 786440 | tf_op jit(solution)/shard_map/ppermute | solution.py:246
  140.2 11.8 %collective-permute-start.22 = (bf16[1024,128]{1,0:T(8,128)(2,1)S(1)}, bf16[1024,128]{1,0:T(8,128)(2,1)S(1)}, u32[]{:S(2)}, u32[]{:S(2)}) collective-permute-start(bf16[1024,128]{1,0:T(8,128)(2,1)S(1)} %get-tuple-element.19), channel_id=1, source_target_pairs={{128,0},{192,64},{0,128},{64,192},{129,1},{193,65},{1,129},{65,193... | collective-permute-start | bytes 786440 | tf_op jit(solution)/shard_map/ppermute | solution.py:246
  145.5 13.2 %collective-permute-start.32 = (bf16[2,32,128]{2,1,0:T(8,128)(2,1)S(1)}, bf16[2,32,128]{2,1,0:T(8,128)(2,1)S(1)}, u32[]{:S(2)}, u32[]{:S(2)}) collective-permute-start(bf16[2,32,128]{2,1,0:T(8,128)(2,1)S(1)} %get-tuple-element.32), channel_id=1, source_target_pairs={{0,0},{64,1},{128,2},{192,3},{1,64},{65,65},{129,66},{193,67},{2,1... | collective-permute-start | bytes 49160 | tf_op jit(solution)/shard_map/ppermute | solution.py:288
  153.0 12.9 %collective-permute-start.35 = (bf16[2,32,128]{2,1,0:T(8,128)(2,1)S(1)}, bf16[2,32,128]{2,1,0:T(8,128)(2,1)S(1)}, u32[]{:S(2)}, u32[]{:S(2)}) collective-permute-start(bf16[2,32,128]{2,1,0:T(8,128)(2,1)S(1)} %get-tuple-element.29), channel_id=1, source_target_pairs={{3,0},{67,1},{131,2},{195,3},{0,64},{64,65},{128,66},{192,67},{1,1... | collective-permute-start | bytes 49160 | tf_op jit(solution)/shard_map/ppermute | solution.py:288
  156.8 9.1 %collective-permute-start.34 = (bf16[2,32,128]{2,1,0:T(8,128)(2,1)S(1)}, bf16[2,32,128]{2,1,0:T(8,128)(2,1)S(1)}, u32[]{:S(2)}, u32[]{:S(2)}) collective-permute-start(bf16[2,32,128]{2,1,0:T(8,128)(2,1)S(1)} %get-tuple-element.30), channel_id=1, source_target_pairs={{2,0},{66,1},{130,2},{194,3},{3,64},{67,65},{131,66},{195,67},{0,1... | collective-permute-start | bytes 49160 | tf_op jit(solution)/shard_map/ppermute | solution.py:288
  158.5 7.4 %collective-permute-start.33 = (bf16[2,32,128]{2,1,0:T(8,128)(2,1)S(1)}, bf16[2,32,128]{2,1,0:T(8,128)(2,1)S(1)}, u32[]{:S(2)}, u32[]{:S(2)}) collective-permute-start(bf16[2,32,128]{2,1,0:T(8,128)(2,1)S(1)} %get-tuple-element.31), channel_id=1, source_target_pairs={{1,0},{65,1},{129,2},{193,3},{2,64},{66,65},{130,66},{194,67},{3,1... | collective-permute-start | bytes 49160 | tf_op jit(solution)/shard_map/ppermute | solution.py:288

commit v2 on v1

--- a/solution.py
+++ b/solution.py
@@ -6,6 +6,7 @@
 from jax.experimental import pallas as pl
 from jax.experimental.pallas import tpu as pltpu
 from jax.sharding import Mesh, PartitionSpec as P
+
 
 DH = 128
 GROUP = 8
@@ -18,7 +19,7 @@
 NEG = -1e30
 SCALE = 1.0 / math.sqrt(DH)
 SCALE2 = SCALE * math.log2(math.e)
-RB = 512
+RB = 1024
 CROSS = 4 * SLICE
 BF, F32 = jnp.bfloat16, jnp.float32
 VM = pl.BlockSpec(memory_space=pltpu.VMEM)
@@ -61,25 +62,30 @@
     return out
 
 
+def place():
+    return tuple(lax.axis_index(name).astype(jnp.int32) for name in ("y", "z", "c", "x"))
+
+
 def load_all(where, q_refs, o_refs, z_ref, c_ref, q_buf, o_buf, kv_buf, sem):
-    y, z, c, x = (where[n] for n in range(4))
-    copies = []
+    y, _, c, x = where
+    for r in range(NX):
+        j = lax.rem(x + NX - r, NX)
+        for e, ref in enumerate((z_ref, c_ref)):
+            for d in range(NZ):
+                block = d * NC + (c if e == 0 else 1 - c)
+                pltpu.make_async_copy(
+                    ref.at[d, r], kv_buf.at[:, j, block], sem.at[NY + j]
+                ).start()
     for d in range(NY):
         i = lax.rem(y + d, NY)
-        copies.append(pltpu.make_async_copy(q_refs[d], q_buf.at[i], sem.at[0]))
-        copies.append(pltpu.make_async_copy(o_refs[d], o_buf.at[i], sem.at[0]))
-    for e, ref in enumerate((z_ref, c_ref)):
-        for d in range(NZ):
-            block = lax.rem(z + NZ - d, NZ) * NC + (c if e == 0 else 1 - c)
-            for r in range(NX):
-                j = lax.rem(x + NX - r, NX)
-                copies.append(
-                    pltpu.make_async_copy(ref.at[d, r], kv_buf.at[:, j, block], sem.at[0])
-                )
-    for copy in copies:
-        copy.start()
-    for copy in copies:
-        copy.wait()
+        pltpu.make_async_copy(q_refs[d], q_buf.at[i], sem.at[i]).start()
+        pltpu.make_async_copy(o_refs[d], o_buf.at[i], sem.at[i]).start()
+
+
+def wait_for(i, q_buf, o_buf, kv_buf, sem):
+    pltpu.make_async_copy(q_buf.at[i], q_buf.at[i], sem.at[i]).wait()
+    pltpu.make_async_copy(o_buf.at[i], o_buf.at[i], sem.at[i]).wait()
+    pltpu.make_async_copy(kv_buf.at[:, i], kv_buf.at[:, i], sem.at[NY + i]).wait()
 
 
 def visible(where, ends, j, i, count, rows_from, rows):
@@ -90,20 +96,21 @@
     return key_pos < jnp.maximum(query_pos + 1, pick(i, ends))
 
 
-def each_pair(ends, pair):
+def each_pair(ends, pair, ready):
     def full(p, carry):
         i = 1 + (p >= 1).astype(jnp.int32) + (p >= 3).astype(jnp.int32)
-        pair(p - i * (i - 1) // 2, i, COL, False)
+        pair(p - i * (i - 1) // 2, i, COL, False, False)
         return carry
 
     def diagonal(i, carry):
-        pair(i, i, COL, True)
+        ready(i)
+        pair(i, i, COL, True, True)
         return carry
 
     def crossing(i, carry):
         @pl.when(pick(i, ends) > (i + 1) * NZ * NC * BLK)
         def _():
-            pair(i + 1, i, CROSS, True)
+            pair(i + 1, i, CROSS, True, False)
 
         return carry
 
@@ -112,16 +119,17 @@
     lax.fori_loop(0, NY - 1, crossing, 0)
 
 
-def stats_kernel(where, seg_blocks, seg_audio, *refs):
+def stats_kernel(seg_blocks, seg_audio, *refs):
     q_refs, o_refs = refs[:NY], refs[NY : 2 * NY]
     z_ref, c_ref, out, q_buf, o_buf, kv_buf, high, total, weighted, sem = refs[2 * NY :]
+    where = place()
     load_all(where, q_refs, o_refs, z_ref, c_ref, q_buf, o_buf, kv_buf, sem)
     ends = span_ends(where, seg_blocks, seg_audio)
     high[...] = jnp.full_like(high, NEG)
     total[...] = jnp.zeros_like(total)
     weighted[...] = jnp.zeros_like(weighted)
 
-    def pair(j, i, count, masked):
+    def pair(j, i, count, masked, first):
         k = kv_buf[0, j].reshape(COL, DH)[:count]
         v = kv_buf[1, j].reshape(COL, DH)[:count]
         for r in range(0, ROWS, RB):
@@ -142,7 +150,7 @@
             total[i, :, rows] = total[i, :, rows] * fix + jnp.sum(p, axis=0)
             weighted[i, :, rows] = weighted[i, :, rows] * fix + jnp.sum(p * dp, axis=0)
 
-    each_pair(ends, pair)
+    each_pair(ends, pair, lambda i: wait_for(i, q_buf, o_buf, kv_buf, sem))
     top = jnp.max(high[...], axis=1, keepdims=True)
     fix = jnp.exp2(high[...] - top)
     out[:, 0:1, :] = top
@@ -150,24 +158,24 @@
     out[:, 2:3, :] = jnp.sum(weighted[...] * fix, axis=1, keepdims=True)
 
 
-def grad_kernel(where, seg_blocks, seg_audio, *refs):
+def grad_kernel(seg_blocks, seg_audio, *refs):
     q_refs, o_refs, st_refs = refs[:NY], refs[NY : 2 * NY], refs[2 * NY : 3 * NY]
-    (z_ref, c_ref, dq_out, own_out, other_out, q_buf, o_buf, kv_buf, lse, delta, dq, dk, dv, sem) = (
-        refs[3 * NY :]
-    )
+    z_ref, c_ref = refs[3 * NY : 3 * NY + 2]
+    dq_outs, (own_out, other_out) = refs[3 * NY + 2 : 4 * NY + 2], refs[4 * NY + 2 : 4 * NY + 4]
+    q_buf, o_buf, kv_buf, st_buf, lse, delta, dq, dk, dv, sem, st_sem = refs[4 * NY + 4 :]
+    for d in range(NY):
+        pltpu.make_async_copy(st_refs[d], st_buf.at[d], st_sem.at[0]).start()
+    where = place()
     load_all(where, q_refs, o_refs, z_ref, c_ref, q_buf, o_buf, kv_buf, sem)
     ends = span_ends(where, seg_blocks, seg_audio)
-    tops = [ref[:, 0:1, :] for ref in st_refs]
-    top = jnp.maximum(jnp.maximum(tops[0], tops[1]), jnp.maximum(tops[2], tops[3]))
-    fixes = [jnp.exp2(t - top) for t in tops]
-    total = sum(f * ref[:, 1:2, :] for f, ref in zip(fixes, st_refs))
+    pltpu.make_async_copy(st_buf, st_buf, st_sem.at[0]).wait()
+    top = jnp.max(st_buf[:, :, 0:1, :], axis=0)
+    fix = jnp.exp2(st_buf[:, :, 0:1, :] - top[None])
+    total = jnp.sum(fix * st_buf[:, :, 1:2, :], axis=0)
     lse[...] = top + jnp.log2(total)
-    delta[...] = sum(f * ref[:, 2:3, :] for f, ref in zip(fixes, st_refs)) / total
-    dq[...] = jnp.zeros_like(dq)
-    dk[...] = jnp.zeros_like(dk)
-    dv[...] = jnp.zeros_like(dv)
-
-    def pair(j, i, count, masked):
+    delta[...] = jnp.sum(fix * st_buf[:, :, 2:3, :], axis=0) / total
+
+    def pair(j, i, count, masked, first):
         k = kv_buf[0, j].reshape(COL, DH)[:count]
         v = kv_buf[1, j].reshape(COL, DH)[:count]
         p_parts, ds_parts = [], []
@@ -179,16 +187,25 @@
                 p = jnp.where(visible(where, ends, j, i, count, r, RB), p, 0.0)
             dp = dot_nt(v, o_buf[i, rows, :])
             ds = (p * (dp - delta[i, :, rows])).astype(BF)
-            dq[i, :, rows] += dot_tn(k, ds)
+            if first:
+                dq[i, :, rows] = dot_tn(k, ds)
+            else:
+                dq[i, :, rows] += dot_tn(k, ds)
             p_parts.append(p.astype(BF))
             ds_parts.append(ds)
-        dv[j, :count, :] += dot_nn(jnp.concatenate(p_parts, axis=1), o_buf[i])
-        dk[j, :count, :] += dot_nn(jnp.concatenate(ds_parts, axis=1), q_buf[i])
-
-    each_pair(ends, pair)
-    y, z, c, x = (where[n] for n in range(4))
+        dv_part = dot_nn(jnp.concatenate(p_parts, axis=1), o_buf[i])
+        dk_part = dot_nn(jnp.concatenate(ds_parts, axis=1), q_buf[i])
+        if first:
+            dv[j, :count, :] = dv_part
+            dk[j, :count, :] = dk_part
+        else:
+            dv[j, :count, :] += dv_part
+            dk[j, :count, :] += dk_part
+
+    each_pair(ends, pair, lambda i: wait_for(i, q_buf, o_buf, kv_buf, sem))
+    y, z, c, x = where
     for d in range(NY):
-        dq_out[d] = (dq[lax.rem(y + d, NY)].T * SCALE).astype(BF)
+        dq_outs[d][...] = (dq[lax.rem(y + d, NY)].T * SCALE).astype(BF)
     for d in range(NZ):
         first = lax.rem(z + d, NZ) * NC
         for r in range(NX):
@@ -207,48 +224,49 @@
     ]
 
 
-def stats_call(where, seg_blocks, seg_audio, q, o, z_all, c_all):
+def stats_call(seg_blocks, seg_audio, q, o, z_all, c_all):
     return pl.pallas_call(
         stats_kernel,
         out_shape=jax.ShapeDtypeStruct((NY, 3, ROWS), F32),
-        in_specs=[SM] * 3 + [HB] * (2 * NY + 2),
+        in_specs=[SM] * 2 + [HB] * (2 * NY + 2),
         out_specs=VM,
         scratch_shapes=buffers()
         + [pltpu.VMEM((NY, 8, ROWS), F32)] * 3
-        + [pltpu.SemaphoreType.DMA((1,))],
+        + [pltpu.SemaphoreType.DMA((2 * NY,))],
         compiler_params=pltpu.CompilerParams(vmem_limit_bytes=56 << 20),
         name="stats",
-    )(where, seg_blocks, seg_audio, *q, *o, z_all, c_all)
-
-
-def grad_call(where, seg_blocks, seg_audio, q, o, st, z_all, c_all):
+    )(seg_blocks, seg_audio, *q, *o, z_all, c_all)
+
+
+def grad_call(seg_blocks, seg_audio, q, o, st, z_all, c_all):
     part = jax.ShapeDtypeStruct((NZ, NX, 2, SLICE, DH), F32)
     return pl.pallas_call(
         grad_kernel,
-        out_shape=(jax.ShapeDtypeStruct((NY, ROWS, DH), BF), part, part),
-        in_specs=[SM] * 3 + [HB] * (2 * NY) + [VM] * NY + [HB] * 2,
-        out_specs=(VM,) * 3,
+        out_shape=(jax.ShapeDtypeStruct((ROWS, DH), BF),) * NY + (part, part),
+        in_specs=[SM] * 2 + [HB] * (3 * NY + 2),
+        out_specs=(VM,) * (NY + 2),
         scratch_shapes=buffers()
         + [
+            pltpu.VMEM((NY, NY, 3, ROWS), F32),
             pltpu.VMEM((NY, 1, ROWS), F32),
             pltpu.VMEM((NY, 1, ROWS), F32),
             pltpu.VMEM((NY, DH, ROWS), F32),
             pltpu.VMEM((NY, COL, DH), F32),
             pltpu.VMEM((NY, COL, DH), F32),
+            pltpu.SemaphoreType.DMA((2 * NY,)),
             pltpu.SemaphoreType.DMA((1,)),
         ],
         compiler_params=pltpu.CompilerParams(vmem_limit_bytes=56 << 20),
         name="grads",
-    )(where, seg_blocks, seg_audio, *q, *o, *st, z_all, c_all)
+    )(seg_blocks, seg_audio, *q, *o, *st, z_all, c_all)
 
 
 def shift(value, axis, size, by):
     return lax.ppermute(value, axis, [((n + by) % size, n) for n in range(size)])
 
 
-def body(query, key, value, d_out, seg_blocks, seg_audio):
-    y, z, c, x = (lax.axis_index(name).astype(jnp.int32) for name in ("y", "z", "c", "x"))
-    where = jnp.stack([y, z, c, x])
+def steps(query, key, value, d_out, seg_blocks, seg_audio):
+    y, _, _, _ = (lax.axis_index(name).astype(jnp.int32) for name in ("y", "z", "c", "x"))
     heads = jnp.stack([key, value]).transpose(2, 0, 1, 3)
     rounds = []
     for r in range(NX):
@@ -262,13 +280,13 @@
     q1, q3 = shift(q0, "y", NY, 1), shift(q0, "y", NY, -1)
     o1, o3 = shift(o0, "y", NY, 1), shift(o0, "y", NY, -1)
     q2, o2 = shift(q1, "y", NY, 1), shift(o3, "y", NY, -1)
-    z_all = jnp.stack([own] + [shift(own, "z", NZ, -d) for d in range(1, NZ)])
+    z_all = lax.all_to_all(jnp.broadcast_to(own[None], (NZ,) + own.shape), "z", 0, 0)
     c_all = shift(z_all, "c", NC, 1)
     q, o = (q0, q1, q2, q3), (o0, o1, o2, o3)
-    st = stats_call(where, seg_blocks, seg_audio, q, o, z_all, c_all)
+    st = stats_call(seg_blocks, seg_audio, q, o, z_all, c_all)
     sts = (st,) + tuple(shift(st, "y", NY, d) for d in range(1, NY))
-    dq, own_part, other_part = grad_call(
-        where, seg_blocks, seg_audio, q, o, sts, z_all, c_all
+    *dq, own_part, other_part = grad_call(
+        seg_blocks, seg_audio, q, o, sts, z_all, c_all
     )
     dq_sum = dq[0].astype(F32)
     for d in range(1, NY):
@@ -297,7 +315,7 @@
     ctx = ("y", "z", "c")
     rows, tokens = P(ctx, "x", None), P(("y", "z", "c", "x"), None, None)
     return jax.shard_map(
-        body,
+        steps,
         mesh=fine,
         in_specs=(rows, tokens, tokens, rows, P(), P()),
         out_specs=(rows, tokens, tokens),

time: 168 us -> 145 us (0.86)
  starting transfers between devices: 74.4 us -> 53.9 us
  Pallas kernels: 35 us -> 31.8 us
    ppermute x28 -> x21, starting transfers between devices: 54.6 us -> 26.4 us  [shift(): lax.ppermute(value, axis, [((n + by) % size, n) for n in range(size)])]
    ppermute x28 -> x21, waiting for transfers between devices: 39.6 us -> 22.6 us  [shift(): lax.ppermute(value, axis, [((n + by) % size, n) for n in range(size)])]
    all_to_all x0 -> x1, waiting for transfers between devices: none -> 13.7 us  [steps(): lax.all_to_all(jnp.broadcast_to(own[None], (NZ,) + own.shape), 'z', 0, 0)]
    all_to_all x0 -> x1, starting transfers between devices: none -> 8.6 us  [steps(): lax.all_to_all(jnp.broadcast_to(own[None], (NZ,) + own.shape), 'z', 0, 0)]
    ppermute x8, waiting for transfers between devices: 8.92 us -> 12.7 us  [the longest x4 6.56 us: steps(): back.append(lax.ppermute(kv_low[r], ('y', 'x'), perm))]
    pallas_call x1, Pallas kernels: 22.3 us -> 19.6 us  [grad_call(): pl.pallas_call(grad_kernel, out_shape=(jax.ShapeDtypeStruct((ROWS, DH), B...]
    unnamed x43 -> x47, local copies, waits for them, and re-layouts: 4.22 us -> 4.87 us
  transfers between devices with their start and end apart: 36 -> 30, of which waited for: 15 -> 15; matrix products, arithmetic and copies ran while one was open for 1% -> 1% of each run, Pallas kernels for 0% -> 0%
where the time goes in v2:
time: 145 us; the launch traced here: 144 us
  starting transfers between devices  53.9 us (37%)
  waiting for transfers between devices  49 us (34%)
  Pallas kernels  31.8 us (22%)
  local copies, waits for them, and re-layouts  5.89 us (4%)
  other arithmetic  2.41 us (2%)
    ppermute x21, starting transfers between devices, shift(): lax.ppermute(value, axis, [((n + by) % size, n) for n in range(size)])  26.4 us
    ppermute x21, waiting for transfers between devices, shift(): lax.ppermute(value, axis, [((n + by) % size, n) for n in range(size)])  22.6 us
    pallas_call x1, Pallas kernels, grad_call(): pl.pallas_call(grad_kernel, out_shape=(jax.ShapeDtypeStruct((ROWS, DH), B...  19.6 us
    all_to_all x1, waiting for transfers between devices, steps(): lax.all_to_all(jnp.broadcast_to(own[None], (NZ,) + own.shape), 'z', 0, 0)  13.7 us
    pallas_call x1, Pallas kernels, stats_call(): pl.pallas_call(stats_kernel, out_shape=jax.ShapeDtypeStruct((NY, 3, ROWS)...  12.2 us
    ppermute x4, starting transfers between devices, steps(): back.append(lax.ppermute(kv_low[r], ('y', 'x'), perm))  11.5 us
    all_to_all x1, starting transfers between devices, steps(): lax.all_to_all(jnp.broadcast_to(own[None], (NZ,) + own.shape), 'z', 0, 0)  8.6 us
    ppermute x4, starting transfers between devices, steps(): rounds.append(lax.ppermute(piece, ('y', 'x'), perm))  7.45 us
  transfers between devices with their start and end apart: 30, of which 15 were waited for; matrix products, arithmetic and copies ran while one was open for 1% of the time, Pallas kernels for 0%

profile of v2, /device:TPU:16, one launch (start us, length us, event | category | flops | bytes accessed | tf_op | source)
XLA Modules:
  0.0 143.9 jit_solution(3038831205112017496)
XLA Ops:
  0.7 0.7 copy-done.15
  1.4 0.0 copy-done.14
  1.5 4.7 %collective-permute-start.6 = (bf16[2,32,128]{2,1,0:T(8,128)(2,1)S(1)}, bf16[2,32,128]{2,1,0:T(8,128)(2,1)S(1)}, u32[]{:S(2)}, u32[]{:S(2)}) collective-permute-start(bf16[2,32,128]{2,1,0:T(8,128)(2,1)S(1)} %get-tuple-element.36), channel_id=1, source_target_pairs={{0,0},{1,64},{2,128},{3,192},{64,1},{65,65},{66,129},{67,193},{128... | collective-permute-start | bytes 49160 | tf_op jit(solution)/shard_map/ppermute | solution.py:277
  6.2 2.7 %collective-permute-start.7 = (bf16[2,32,128]{2,1,0:T(8,128)(2,1)S(1)}, bf16[2,32,128]{2,1,0:T(8,128)(2,1)S(1)}, u32[]{:S(2)}, u32[]{:S(2)}) collective-permute-start(bf16[2,32,128]{2,1,0:T(8,128)(2,1)S(1)} %get-tuple-element.37), channel_id=1, source_target_pairs={{0,1},{1,65},{2,129},{3,193},{64,2},{65,66},{66,130},{67,194},{128... | collective-permute-start | bytes 49160 | tf_op jit(solution)/shard_map/ppermute | solution.py:277
  8.9 0.0 collective-permute-start.8
  8.9 0.0 collective-permute-start.9
  8.9 2.1 %collective-permute-done.6 = bf16[2,32,128]{2,1,0:T(8,128)(2,1)S(1)} collective-permute-done((bf16[2,32,128]{2,1,0:T(8,128)(2,1)S(1)}, bf16[2,32,128]{2,1,0:T(8,128)(2,1)S(1)}, u32[]{:S(2)}, u32[]{:S(2)}) %collective-permute-start.6) | collective-permute-done | bytes 16416 | tf_op jit(solution)/shard_map/ppermute | solution.py:277
  11.0 1.4 collective-permute-done.7
  12.4 1.8 %collective-permute-done.8 = bf16[2,32,128]{2,1,0:T(8,128)(2,1)S(1)} collective-permute-done((bf16[2,32,128]{2,1,0:T(8,128)(2,1)S(1)}, bf16[2,32,128]{2,1,0:T(8,128)(2,1)S(1)}, u32[]{:S(2)}, u32[]{:S(2)}) %collective-permute-start.8) | collective-permute-done | bytes 16416 | tf_op jit(solution)/shard_map/ppermute | solution.py:277
  14.2 0.9 collective-permute-done.9
  15.1 0.9 broadcast_in_dim.2
  16.0 8.6 %all-to-all-start = ((bf16[8,4,2,32,128]{4,3,2,1,0:T(8,128)(2,1)}), bf16[8,4,2,32,128]{4,3,2,1,0:T(8,128)(2,1)S(1)}, u32[]{:S(2)}, u32[]{:S(2)}) async-start(bf16[8,4,2,32,128]{4,3,2,1,0:T(8,128)(2,1)} %broadcast_in_dim.2), calls=%async_computation | async-start | bytes 1048576 | tf_op jit(solution)/shard_map/all_to_all | solution.py:283
  24.6 2.0 %collective-permute-start = (bf16[1024,128]{1,0:T(8,128)(2,1)S(1)}, bf16[1024,128]{1,0:T(8,128)(2,1)S(1)}, u32[]{:S(2)}, u32[]{:S(2)}) collective-permute-start(bf16[1024,128]{1,0:T(8,128)(2,1)S(1)} %bitcast.80), channel_id=1, source_target_pairs={{64,0},{128,64},{192,128},{0,192},{65,1},{129,65},{193,129},{1,193... | collective-permute-start | bytes 786440 | tf_op jit(solution)/shard_map/ppermute | solution.py:265
  26.6 0.1 collective-permute-start.4
  26.7 13.7 %all-to-all-done.refs_8_.refs_12_ = bf16[8,4,2,32,128]{4,3,2,1,0:T(8,128)(2,1)S(1)} async-done(((bf16[8,4,2,32,128]{4,3,2,1,0:T(8,128)(2,1)}), bf16[8,4,2,32,128]{4,3,2,1,0:T(8,128)(2,1)S(1)}, u32[]{:S(2)}, u32[]{:S(2)}) %all-to-all-start) | async-done | bytes 524320 | tf_op jit(solution)/shard_map/all_to_all | solution.py:283
  40.4 0.0 collective-permute-start.10
  40.4 0.0 collective-permute-start.2
  40.4 2.0 %collective-permute-start.3 = (bf16[1024,128]{1,0:T(8,128)(2,1)S(1)}, bf16[1024,128]{1,0:T(8,128)(2,1)S(1)}, u32[]{:S(2)}, u32[]{:S(2)}) collective-permute-start(bf16[1024,128]{1,0:T(8,128)(2,1)S(1)} %bitcast.85), channel_id=1, source_target_pairs={{64,0},{128,64},{192,128},{0,192},{65,1},{129,65},{193,129},{1,193... | collective-permute-start | bytes 786440 | tf_op jit(solution)/shard_map/ppermute | solution.py:265
  42.4 0.0 collective-permute-done.refs_1_
  42.4 1.6 %collective-permute-start.1 = (bf16[1024,128]{1,0:T(8,128)(2,1)S(1)}, bf16[1024,128]{1,0:T(8,128)(2,1)S(1)}, u32[]{:S(2)}, u32[]{:S(2)}) collective-permute-start(bf16[1024,128]{1,0:T(8,128)(2,1)S(1)} %collective-permute-done.refs_1_), channel_id=1, source_target_pairs={{64,0},{128,64},{192,128},{0,192},{65,1},{129,65},{193,129},{1,193... | collective-permute-start | bytes 786440 | tf_op jit(solution)/shard_map/ppermute | solution.py:265
  44.0 0.0 collective-permute-done.4.refs_7_
  44.0 0.4 collective-permute-start.5
  44.5 5.1 %collective-permute-done.2.refs_3_ = bf16[1024,128]{1,0:T(8,128)(2,1)S(1)} collective-permute-done((bf16[1024,128]{1,0:T(8,128)(2,1)S(1)}, bf16[1024,128]{1,0:T(8,128)(2,1)S(1)}, u32[]{:S(2)}, u32[]{:S(2)}) %collective-permute-start.2) | collective-permute-done | bytes 262176 | tf_op jit(solution)/shard_map/ppermute | solution.py:265
  49.6 0.5 collective-permute-done.3.refs_5_
  50.1 5.2 %collective-permute-done.1.refs_2_ = bf16[1024,128]{1,0:T(8,128)(2,1)S(1)} collective-permute-done((bf16[1024,128]{1,0:T(8,128)(2,1)S(1)}, bf16[1024,128]{1,0:T(8,128)(2,1)S(1)}, u32[]{:S(2)}, u32[]{:S(2)}) %collective-permute-start.1) | collective-permute-done | bytes 262176 | tf_op jit(solution)/shard_map/ppermute | solution.py:265
  55.3 0.6 copy-done.8
  55.9 0.1 copy-done.9
  56.0 0.8 copy-done.1
  56.8 12.2 %stats.1.refs_8_ = f32[4,3,1024]{2,1,0:T(4,128)} custom-call(s32[32]{0:T(128)} %seg_blocks.3, s32[32]{0:T(128)} %seg_audio.3, bf16[1024,128]{1,0:T(8,128)(2,1)} %bitcast.78, bf16[1024,128]{1,0:T(8,128)(2,1)} %copy-done.4, bf16[1024,128]{1,0:T(8,128)(2,1)} %copy-done.8, bf16[1024,128]{1,0:T(8,128)(2,1)} %copy-done.6, bf16[1024,128]{1,0:T(8,128)(2,1)} %bitcast.82, ...), custom_call_target="tpu_custom_call" | custom-call | tf_op jit(solution)/shard_map/stats/pallas_call | solution.py:228
  69.0 2.9 %collective-permute-start.13 = (f32[4,3,1024]{2,1,0:T(4,128)}, f32[4,3,1024]{2,1,0:T(4,128)S(1)}, u32[]{:S(2)}, u32[]{:S(2)}) collective-permute-start(f32[4,3,1024]{2,1,0:T(4,128)} %stats.1.refs_8_), channel_id=1, source_target_pairs={{192,0},{0,64},{64,128},{128,192},{193,1},{1,65},{65,129},{129,193... | collective-permute-start | bytes 147464 | tf_op jit(solution)/shard_map/ppermute | solution.py:265
  71.9 0.1 collective-permute-start.12
  72.0 1.7 %collective-permute-start.11 = (f32[4,3,1024]{2,1,0:T(4,128)}, f32[4,3,1024]{2,1,0:T(4,128)S(1)}, u32[]{:S(2)}, u32[]{:S(2)}) collective-permute-start(f32[4,3,1024]{2,1,0:T(4,128)} %stats.1.refs_8_), channel_id=1, source_target_pairs={{64,0},{128,64},{192,128},{0,192},{65,1},{129,65},{193,129},{1,193... | collective-permute-start | bytes 147464 | tf_op jit(solution)/shard_map/ppermute | solution.py:265
  73.7 0.4 collective-permute-done.13.refs_11_
  74.1 3.8 %collective-permute-done.12.refs_10_ = f32[4,3,1024]{2,1,0:T(4,128)S(1)} collective-permute-done((f32[4,3,1024]{2,1,0:T(4,128)}, f32[4,3,1024]{2,1,0:T(4,128)S(1)}, u32[]{:S(2)}, u32[]{:S(2)}) %collective-permute-start.12) | collective-permute-done | bytes 49184 | tf_op jit(solution)/shard_map/ppermute | solution.py:265
  77.9 0.0 collective-permute-done.11.refs_9_
  77.9 0.6 copy-done.12
  78.5 0.6 copy-done.13
  79.1 19.6 %grads.1 = (bf16[1024,128]{1,0:T(8,128)(2,1)}, bf16[1024,128]{1,0:T(8,128)(2,1)}, bf16[1024,128]{1,0:T(8,128)(2,1)}, bf16[1024,128]{1,0:T(8,128)(2,1)}, f32[8,4,...) custom-call(s32[32]{0:T(128)} %seg_blocks.3, s32[32]{0:T(128)} %seg_audio.3, bf16[1024,128]{1,0:T(8,128)(2,1)} %bitcast.79, ...), custom_call_target="tpu_custom_call" | custom-call | tf_op jit(solution)/shard_map/grads/pallas_call | solution.py:243
  98.7 0.1 collective-permute-start.17
  98.8 2.9 %collective-permute-done.17 = f32[8,4,2,32,128]{4,3,2,1,0:T(8,128)S(1)} collective-permute-done((f32[8,4,2,32,128]{4,3,2,1,0:T(8,128)}, f32[8,4,2,32,128]{4,3,2,1,0:T(8,128)S(1)}, u32[]{:S(2)}, u32[]{:S(2)}) %collective-permute-start.17) | collective-permute-done | bytes 1048608 | tf_op jit(solution)/shard_map/ppermute | solution.py:265
  101.7 1.5 %fusion.17 = (bf16[8,4,2,32,128]{4,3,2,1,0:T(8,128)(2,1)S(1)}, f32[8,4,2,32,128]{4,3,2,1,0:T(8,128)S(1)}) fusion(f32[8,4,2,32,128]{4,3,2,1,0:T(8,128)} %get-tuple-element.13, f32[8,4,2,32,128]{4,3,2,1,0:T(8,128)S(1)} %collective-permute-done.17), kind=kLoop, calls=%fused_computation.52 | loop fusion | flops 524288 | bytes 3670016 | tf_op jit(solution)/shard_map/convert_element_type | solution.py:296
  103.2 0.6 collective-permute-start.18
  103.8 2.7 %collective-permute-start.24 = (bf16[4,2,32,128]{3,2,1,0:T(8,128)(2,1)S(1)}, bf16[4,2,32,128]{3,2,1,0:T(8,128)(2,1)S(1)}, u32[]{:S(2)}, u32[]{:S(2)}) collective-permute-start(bf16[4,2,32,128]{3,2,1,0:T(8,128)(2,1)S(1)} %get-tuple-element.24), channel_id=1, source_target_pairs={{8,0},{16,8},{24,16},{32,24},{40,32},{48,40},{56,48},{0,56},{9,1},... | collective-permute-start | bytes 196616 | tf_op jit(solution)/shard_map/ppermute | solution.py:265
  106.5 0.0 collective-permute-start.23
  106.5 1.4 collective-permute-start.22
  107.9 4.5 %collective-permute-start.21 = (bf16[4,2,32,128]{3,2,1,0:T(8,128)(2,1)S(1)}, bf16[4,2,32,128]{3,2,1,0:T(8,128)(2,1)S(1)}, u32[]{:S(2)}, u32[]{:S(2)}) collective-permute-start(bf16[4,2,32,128]{3,2,1,0:T(8,128)(2,1)S(1)} %get-tuple-element.27), channel_id=1, source_target_pairs={{32,0},{40,8},{48,16},{56,24},{0,32},{8,40},{16,48},{24,56},{33,1}... | collective-permute-start | bytes 196616 | tf_op jit(solution)/shard_map/ppermute | solution.py:265
  112.5 0.3 collective-permute-start.20
  112.8 0.0 collective-permute-done.24
  112.8 2.3 %collective-permute-start.19 = (bf16[4,2,32,128]{3,2,1,0:T(8,128)(2,1)S(1)}, bf16[4,2,32,128]{3,2,1,0:T(8,128)(2,1)S(1)}, u32[]{:S(2)}, u32[]{:S(2)}) collective-permute-start(bf16[4,2,32,128]{3,2,1,0:T(8,128)(2,1)S(1)} %get-tuple-element.29), channel_id=1, source_target_pairs={{48,0},{56,8},{0,16},{8,24},{16,32},{24,40},{32,48},{40,56},{49,1}... | collective-permute-start | bytes 196616 | tf_op jit(solution)/shard_map/ppermute | solution.py:265
  115.1 1.2 collective-permute-done.23
  116.3 1.0 collective-permute-start.14
  117.3 0.5 collective-permute-done.22
  117.8 1.4 collective-permute-start.15
  119.2 1.2 collective-permute-start.16
  120.3 3.1 %collective-permute-done.20 = bf16[4,2,32,128]{3,2,1,0:T(8,128)(2,1)S(1)} collective-permute-done((bf16[4,2,32,128]{3,2,1,0:T(8,128)(2,1)S(1)}, bf16[4,2,32,128]{3,2,1,0:T(8,128)(2,1)S(1)}, u32[]{:S(2)}, u32[]{:S(2)}) %collective-permute-start.20) | collective-permute-done | bytes 65568 | tf_op jit(solution)/shard_map/ppermute | solution.py:265
  123.5 0.1 fusion.8
  123.6 6.2 %collective-permute-start.25 = (bf16[2,32,128]{2,1,0:T(8,128)(2,1)S(1)}, bf16[2,32,128]{2,1,0:T(8,128)(2,1)S(1)}, u32[]{:S(2)}, u32[]{:S(2)}) collective-permute-start(bf16[2,32,128]{2,1,0:T(8,128)(2,1)S(1)} %get-tuple-element.35), channel_id=1, source_target_pairs={{0,0},{64,1},{128,2},{192,3},{1,64},{65,65},{129,66},{193,67},{2,1... | collective-permute-start | bytes 49160 | tf_op jit(solution)/shard_map/ppermute | solution.py:306
  129.8 0.8 fusion
  130.7 3.7 %collective-permute-start.28 = (bf16[2,32,128]{2,1,0:T(8,128)(2,1)S(1)}, bf16[2,32,128]{2,1,0:T(8,128)(2,1)S(1)}, u32[]{:S(2)}, u32[]{:S(2)}) collective-permute-start(bf16[2,32,128]{2,1,0:T(8,128)(2,1)S(1)} %get-tuple-element.32), channel_id=1, source_target_pairs={{3,0},{67,1},{131,2},{195,3},{0,64},{64,65},{128,66},{192,67},{1,1... | collective-permute-start | bytes 49160 | tf_op jit(solution)/shard_map/ppermute | solution.py:306
  134.4 0.8 collective-permute-start.27
  135.2 0.8 collective-permute-start.26
  136.0 6.5 %collective-permute-done.26 = bf16[2,32,128]{2,1,0:T(8,128)(2,1)S(1)} collective-permute-done((bf16[2,32,128]{2,1,0:T(8,128)(2,1)S(1)}, bf16[2,32,128]{2,1,0:T(8,128)(2,1)S(1)}, u32[]{:S(2)}, u32[]{:S(2)}) %collective-permute-start.26) | collective-permute-done | bytes 16416 | tf_op jit(solution)/shard_map/ppermute | solution.py:306
  142.6 0.6 copy.14
  143.3 0.6 copy.13
  (57 shorter events, 0.3 us)
Async XLA Ops:
  0.7 0.8 copy-start.15
  0.7 0.8 copy-start.14
  1.5 9.5 %collective-permute-start.6 = (bf16[2,32,128]{2,1,0:T(8,128)(2,1)S(1)}, bf16[2,32,128]{2,1,0:T(8,128)(2,1)S(1)}, u32[]{:S(2)}, u32[]{:S(2)}) collective-permute-start(bf16[2,32,128]{2,1,0:T(8,128)(2,1)S(1)} %get-tuple-element.36), channel_id=1, source_target_pairs={{0,0},{1,64},{2,128},{3,192},{64,1},{65,65},{66,129},{67,193},{128... | collective-permute-start | bytes 49160 | tf_op jit(solution)/shard_map/ppermute | solution.py:277
  6.2 6.2 %collective-permute-start.7 = (bf16[2,32,128]{2,1,0:T(8,128)(2,1)S(1)}, bf16[2,32,128]{2,1,0:T(8,128)(2,1)S(1)}, u32[]{:S(2)}, u32[]{:S(2)}) collective-permute-start(bf16[2,32,128]{2,1,0:T(8,128)(2,1)S(1)} %get-tuple-element.37), channel_id=1, source_target_pairs={{0,1},{1,65},{2,129},{3,193},{64,2},{65,66},{66,130},{67,194},{128... | collective-permute-start | bytes 49160 | tf_op jit(solution)/shard_map/ppermute | solution.py:277
  8.9 5.2 %collective-permute-start.8 = (bf16[2,32,128]{2,1,0:T(8,128)(2,1)S(1)}, bf16[2,32,128]{2,1,0:T(8,128)(2,1)S(1)}, u32[]{:S(2)}, u32[]{:S(2)}) collective-permute-start(bf16[2,32,128]{2,1,0:T(8,128)(2,1)S(1)} %get-tuple-element.38), channel_id=1, source_target_pairs={{0,2},{1,66},{2,130},{3,194},{64,3},{65,67},{66,131},{67,195},{128... | collective-permute-start | bytes 49160 | tf_op jit(solution)/shard_map/ppermute | solution.py:277
  8.9 6.1 %collective-permute-start.9 = (bf16[2,32,128]{2,1,0:T(8,128)(2,1)S(1)}, bf16[2,32,128]{2,1,0:T(8,128)(2,1)S(1)}, u32[]{:S(2)}, u32[]{:S(2)}) collective-permute-start(bf16[2,32,128]{2,1,0:T(8,128)(2,1)S(1)} %get-tuple-element.39), channel_id=1, source_target_pairs={{0,3},{1,67},{2,131},{3,195},{64,0},{65,64},{66,128},{67,192},{128... | collective-permute-start | bytes 49160 | tf_op jit(solution)/shard_map/ppermute | solution.py:277
  16.0 8.6 %copy-start.2 = (bf16[128,8,128]{2,1,0:T(8,128)(2,1)S(1)}, bf16[128,8,128]{2,1,0:T(8,128)(2,1)}, u32[]{:S(2)}) copy-start(bf16[128,8,128]{2,1,0:T(8,128)(2,1)} %param.6) | copy-start | bytes 786436
  16.0 10.6 %copy-start.3 = (bf16[128,8,128]{2,1,0:T(8,128)(2,1)S(1)}, bf16[128,8,128]{2,1,0:T(8,128)(2,1)}, u32[]{:S(2)}) copy-start(bf16[128,8,128]{2,1,0:T(8,128)(2,1)} %param.9) | copy-start | bytes 786436
  16.0 24.4 %all-to-all-start = ((bf16[8,4,2,32,128]{4,3,2,1,0:T(8,128)(2,1)}), bf16[8,4,2,32,128]{4,3,2,1,0:T(8,128)(2,1)S(1)}, u32[]{:S(2)}, u32[]{:S(2)}) async-start(bf16[8,4,2,32,128]{4,3,2,1,0:T(8,128)(2,1)} %broadcast_in_dim.2), calls=%async_computation | async-start | bytes 1048576 | tf_op jit(solution)/shard_map/all_to_all | solution.py:283
  24.6 17.8 %collective-permute-start = (bf16[1024,128]{1,0:T(8,128)(2,1)S(1)}, bf16[1024,128]{1,0:T(8,128)(2,1)S(1)}, u32[]{:S(2)}, u32[]{:S(2)}) collective-permute-start(bf16[1024,128]{1,0:T(8,128)(2,1)S(1)} %bitcast.80), channel_id=1, source_target_pairs={{64,0},{128,64},{192,128},{0,192},{65,1},{129,65},{193,129},{1,193... | collective-permute-start | bytes 786440 | tf_op jit(solution)/shard_map/ppermute | solution.py:265
  26.6 17.5 %collective-permute-start.4 = (bf16[1024,128]{1,0:T(8,128)(2,1)S(1)}, bf16[1024,128]{1,0:T(8,128)(2,1)S(1)}, u32[]{:S(2)}, u32[]{:S(2)}) collective-permute-start(bf16[1024,128]{1,0:T(8,128)(2,1)S(1)} %bitcast.84), channel_id=1, source_target_pairs={{192,0},{0,64},{64,128},{128,192},{193,1},{1,65},{65,129},{129,193... | collective-permute-start | bytes 786440 | tf_op jit(solution)/shard_map/ppermute | solution.py:265
  40.4 14.8 %copy-start = (bf16[8,4,2,32,128]{4,3,2,1,0:T(8,128)(2,1)}, bf16[8,4,2,32,128]{4,3,2,1,0:T(8,128)(2,1)S(1)}, u32[]{:S(2)}) copy-start(bf16[8,4,2,32,128]{4,3,2,1,0:T(8,128)(2,1)S(1)} %all-to-all-done.refs_8_.refs_12_) | copy-start | bytes 1572868
  40.4 14.8 %collective-permute-start.10 = (bf16[8,4,2,32,128]{4,3,2,1,0:T(8,128)(2,1)S(1)}, bf16[8,4,2,32,128]{4,3,2,1,0:T(8,128)(2,1)S(1)}, u32[]{:S(2)}, u32[]{:S(2)}) collective-permute-start(bf16[8,4,2,32,128]{4,3,2,1,0:T(8,128)(2,1)S(1)} %all-to-all-done.refs_8_.refs_12_), channel_id=1, source_target_pairs={{4,0},{0,4},{5,1},{1,5},{6,2},{2,6},{7,3},{3,7},{12,8},{8,12},{13,... | collective-permute-start | bytes 1572872 | tf_op jit(solution)/shard_map/ppermute | solution.py:265
  40.4 9.2 %collective-permute-start.2 = (bf16[1024,128]{1,0:T(8,128)(2,1)S(1)}, bf16[1024,128]{1,0:T(8,128)(2,1)S(1)}, u32[]{:S(2)}, u32[]{:S(2)}) collective-permute-start(bf16[1024,128]{1,0:T(8,128)(2,1)S(1)} %bitcast.81), channel_id=1, source_target_pairs={{192,0},{0,64},{64,128},{128,192},{193,1},{1,65},{65,129},{129,193... | collective-permute-start | bytes 786440 | tf_op jit(solution)/shard_map/ppermute | solution.py:265
  40.4 9.6 %collective-permute-start.3 = (bf16[1024,128]{1,0:T(8,128)(2,1)S(1)}, bf16[1024,128]{1,0:T(8,128)(2,1)S(1)}, u32[]{:S(2)}, u32[]{:S(2)}) collective-permute-start(bf16[1024,128]{1,0:T(8,128)(2,1)S(1)} %bitcast.85), channel_id=1, source_target_pairs={{64,0},{128,64},{192,128},{0,192},{65,1},{129,65},{193,129},{1,193... | collective-permute-start | bytes 786440 | tf_op jit(solution)/shard_map/ppermute | solution.py:265
  42.4 12.8 %copy-start.4 = (bf16[1024,128]{1,0:T(8,128)(2,1)}, bf16[1024,128]{1,0:T(8,128)(2,1)S(1)}, u32[]{:S(2)}) copy-start(bf16[1024,128]{1,0:T(8,128)(2,1)S(1)} %collective-permute-done.refs_1_) | copy-start | bytes 786436
  42.4 12.8 %collective-permute-start.1 = (bf16[1024,128]{1,0:T(8,128)(2,1)S(1)}, bf16[1024,128]{1,0:T(8,128)(2,1)S(1)}, u32[]{:S(2)}, u32[]{:S(2)}) collective-permute-start(bf16[1024,128]{1,0:T(8,128)(2,1)S(1)} %collective-permute-done.refs_1_), channel_id=1, source_target_pairs={{64,0},{128,64},{192,128},{0,192},{65,1},{129,65},{193,129},{1,193... | collective-permute-start | bytes 786440 | tf_op jit(solution)/shard_map/ppermute | solution.py:265
  44.0 11.2 %copy-start.5 = (bf16[1024,128]{1,0:T(8,128)(2,1)}, bf16[1024,128]{1,0:T(8,128)(2,1)S(1)}, u32[]{:S(2)}) copy-start(bf16[1024,128]{1,0:T(8,128)(2,1)S(1)} %collective-permute-done.4.refs_7_) | copy-start | bytes 786436
  44.0 11.2 %collective-permute-start.5 = (bf16[1024,128]{1,0:T(8,128)(2,1)S(1)}, bf16[1024,128]{1,0:T(8,128)(2,1)S(1)}, u32[]{:S(2)}, u32[]{:S(2)}) collective-permute-start(bf16[1024,128]{1,0:T(8,128)(2,1)S(1)} %collective-permute-done.4.refs_7_), channel_id=1, source_target_pairs={{192,0},{0,64},{64,128},{128,192},{193,1},{1,65},{65,129},{129,193... | collective-permute-start | bytes 786440 | tf_op jit(solution)/shard_map/ppermute | solution.py:265
  49.6 5.7 %copy-start.6 = (bf16[1024,128]{1,0:T(8,128)(2,1)}, bf16[1024,128]{1,0:T(8,128)(2,1)S(1)}, u32[]{:S(2)}) copy-start(bf16[1024,128]{1,0:T(8,128)(2,1)S(1)} %collective-permute-done.2.refs_3_) | copy-start | bytes 786436
  50.1 5.2 %copy-start.7 = (bf16[1024,128]{1,0:T(8,128)(2,1)}, bf16[1024,128]{1,0:T(8,128)(2,1)S(1)}, u32[]{:S(2)}) copy-start(bf16[1024,128]{1,0:T(8,128)(2,1)S(1)} %collective-permute-done.3.refs_5_) | copy-start | bytes 786436
  55.2 0.7 copy-start.8
  55.2 0.8 copy-start.9
  56.0 0.8 copy-start.1
  69.0 5.1 %collective-permute-start.13 = (f32[4,3,1024]{2,1,0:T(4,128)}, f32[4,3,1024]{2,1,0:T(4,128)S(1)}, u32[]{:S(2)}, u32[]{:S(2)}) collective-permute-start(f32[4,3,1024]{2,1,0:T(4,128)} %stats.1.refs_8_), channel_id=1, source_target_pairs={{192,0},{0,64},{64,128},{128,192},{193,1},{1,65},{65,129},{129,193... | collective-permute-start | bytes 147464 | tf_op jit(solution)/shard_map/ppermute | solution.py:265
  71.9 6.0 %collective-permute-start.12 = (f32[4,3,1024]{2,1,0:T(4,128)}, f32[4,3,1024]{2,1,0:T(4,128)S(1)}, u32[]{:S(2)}, u32[]{:S(2)}) collective-permute-start(f32[4,3,1024]{2,1,0:T(4,128)} %stats.1.refs_8_), channel_id=1, source_target_pairs={{128,0},{192,64},{0,128},{64,192},{129,1},{193,65},{1,129},{65,193... | collective-permute-start | bytes 147464 | tf_op jit(solution)/shard_map/ppermute | solution.py:265
  72.0 5.9 %collective-permute-start.11 = (f32[4,3,1024]{2,1,0:T(4,128)}, f32[4,3,1024]{2,1,0:T(4,128)S(1)}, u32[]{:S(2)}, u32[]{:S(2)}) collective-permute-start(f32[4,3,1024]{2,1,0:T(4,128)} %stats.1.refs_8_), channel_id=1, source_target_pairs={{64,0},{128,64},{192,128},{0,192},{65,1},{129,65},{193,129},{1,193... | collective-permute-start | bytes 147464 | tf_op jit(solution)/shard_map/ppermute | solution.py:265
  74.1 3.8 %copy-start.11 = (f32[4,3,1024]{2,1,0:T(4,128)}, f32[4,3,1024]{2,1,0:T(4,128)S(1)}, u32[]{:S(2)}) copy-start(f32[4,3,1024]{2,1,0:T(4,128)S(1)} %collective-permute-done.13.refs_11_) | copy-start | bytes 147460
  77.9 0.6 copy-start.12
  78.5 0.6 copy-start.13
  98.7 3.0 %collective-permute-start.17 = (f32[8,4,2,32,128]{4,3,2,1,0:T(8,128)}, f32[8,4,2,32,128]{4,3,2,1,0:T(8,128)S(1)}, u32[]{:S(2)}, u32[]{:S(2)}) collective-permute-start(f32[8,4,2,32,128]{4,3,2,1,0:T(8,128)} %get-tuple-element.14), channel_id=1, source_target_pairs={{4,0},{0,4},{5,1},{1,5},{6,2},{2,6},{7,3},{3,7},{12,8},{8,12},{13,... | collective-permute-start | bytes 3145736 | tf_op jit(solution)/shard_map/ppermute | solution.py:265
  103.1 13.1 %copy-start.18 = (bf16[1024,128]{1,0:T(8,128)(2,1)S(1)}, bf16[1024,128]{1,0:T(8,128)(2,1)}, u32[]{:S(2)}) copy-start(bf16[1024,128]{1,0:T(8,128)(2,1)} %get-tuple-element.10) | copy-start | bytes 786436
  103.1 14.6 %copy-start.17 = (bf16[1024,128]{1,0:T(8,128)(2,1)S(1)}, bf16[1024,128]{1,0:T(8,128)(2,1)}, u32[]{:S(2)}) copy-start(bf16[1024,128]{1,0:T(8,128)(2,1)} %get-tuple-element.11) | copy-start | bytes 786436
  103.2 16.0 %copy-start.16 = (bf16[1024,128]{1,0:T(8,128)(2,1)S(1)}, bf16[1024,128]{1,0:T(8,128)(2,1)}, u32[]{:S(2)}) copy-start(bf16[1024,128]{1,0:T(8,128)(2,1)} %get-tuple-element.12) | copy-start | bytes 786436
  103.2 9.3 %collective-permute-start.18 = (bf16[4,2,32,128]{3,2,1,0:T(8,128)(2,1)S(1)}, bf16[4,2,32,128]{3,2,1,0:T(8,128)(2,1)S(1)}, u32[]{:S(2)}, u32[]{:S(2)}) collective-permute-start(bf16[4,2,32,128]{3,2,1,0:T(8,128)(2,1)S(1)} %get-tuple-element.23), channel_id=1, source_target_pairs={{56,0},{0,8},{8,16},{16,24},{24,32},{32,40},{40,48},{48,56},{57,1}... | collective-permute-start | bytes 196616 | tf_op jit(solution)/shard_map/ppermute | solution.py:265
  103.8 9.0 %collective-permute-start.24 = (bf16[4,2,32,128]{3,2,1,0:T(8,128)(2,1)S(1)}, bf16[4,2,32,128]{3,2,1,0:T(8,128)(2,1)S(1)}, u32[]{:S(2)}, u32[]{:S(2)}) collective-permute-start(bf16[4,2,32,128]{3,2,1,0:T(8,128)(2,1)S(1)} %get-tuple-element.24), channel_id=1, source_target_pairs={{8,0},{16,8},{24,16},{32,24},{40,32},{48,40},{56,48},{0,56},{9,1},... | collective-permute-start | bytes 196616 | tf_op jit(solution)/shard_map/ppermute | solution.py:265
  106.5 9.8 %collective-permute-start.23 = (bf16[4,2,32,128]{3,2,1,0:T(8,128)(2,1)S(1)}, bf16[4,2,32,128]{3,2,1,0:T(8,128)(2,1)S(1)}, u32[]{:S(2)}, u32[]{:S(2)}) collective-permute-start(bf16[4,2,32,128]{3,2,1,0:T(8,128)(2,1)S(1)} %get-tuple-element.25), channel_id=1, source_target_pairs={{16,0},{24,8},{32,16},{40,24},{48,32},{56,40},{0,48},{8,56},{17,1}... | collective-permute-start | bytes 196616 | tf_op jit(solution)/shard_map/ppermute | solution.py:265
  106.5 11.2 %collective-permute-start.22 = (bf16[4,2,32,128]{3,2,1,0:T(8,128)(2,1)S(1)}, bf16[4,2,32,128]{3,2,1,0:T(8,128)(2,1)S(1)}, u32[]{:S(2)}, u32[]{:S(2)}) collective-permute-start(bf16[4,2,32,128]{3,2,1,0:T(8,128)(2,1)S(1)} %get-tuple-element.26), channel_id=1, source_target_pairs={{24,0},{32,8},{40,16},{48,24},{56,32},{0,40},{8,48},{16,56},{25,1}... | collective-permute-start | bytes 196616 | tf_op jit(solution)/shard_map/ppermute | solution.py:265
  107.9 11.2 %collective-permute-start.21 = (bf16[4,2,32,128]{3,2,1,0:T(8,128)(2,1)S(1)}, bf16[4,2,32,128]{3,2,1,0:T(8,128)(2,1)S(1)}, u32[]{:S(2)}, u32[]{:S(2)}) collective-permute-start(bf16[4,2,32,128]{3,2,1,0:T(8,128)(2,1)S(1)} %get-tuple-element.27), channel_id=1, source_target_pairs={{32,0},{40,8},{48,16},{56,24},{0,32},{8,40},{16,48},{24,56},{33,1}... | collective-permute-start | bytes 196616 | tf_op jit(solution)/shard_map/ppermute | solution.py:265
  112.5 11.0 %collective-permute-start.20 = (bf16[4,2,32,128]{3,2,1,0:T(8,128)(2,1)S(1)}, bf16[4,2,32,128]{3,2,1,0:T(8,128)(2,1)S(1)}, u32[]{:S(2)}, u32[]{:S(2)}) collective-permute-start(bf16[4,2,32,128]{3,2,1,0:T(8,128)(2,1)S(1)} %get-tuple-element.28), channel_id=1, source_target_pairs={{40,0},{48,8},{56,16},{0,24},{8,32},{16,40},{24,48},{32,56},{41,1}... | collective-permute-start | bytes 196616 | tf_op jit(solution)/shard_map/ppermute | solution.py:265
  112.8 10.7 %collective-permute-start.19 = (bf16[4,2,32,128]{3,2,1,0:T(8,128)(2,1)S(1)}, bf16[4,2,32,128]{3,2,1,0:T(8,128)(2,1)S(1)}, u32[]{:S(2)}, u32[]{:S(2)}) collective-permute-start(bf16[4,2,32,128]{3,2,1,0:T(8,128)(2,1)S(1)} %get-tuple-element.29), channel_id=1, source_target_pairs={{48,0},{56,8},{0,16},{8,24},{16,32},{24,40},{32,48},{40,56},{49,1}... | collective-permute-start | bytes 196616 | tf_op jit(solution)/shard_map/ppermute | solution.py:265
  116.3 13.5 %collective-permute-start.14 = (bf16[1024,128]{1,0:T(8,128)(2,1)S(1)}, bf16[1024,128]{1,0:T(8,128)(2,1)S(1)}, u32[]{:S(2)}, u32[]{:S(2)}) collective-permute-start(bf16[1024,128]{1,0:T(8,128)(2,1)S(1)} %copy-done.18), channel_id=1, source_target_pairs={{192,0},{0,64},{64,128},{128,192},{193,1},{1,65},{65,129},{129,193... | collective-permute-start | bytes 786440 | tf_op jit(solution)/shard_map/ppermute | solution.py:265
  117.8 12.1 %collective-permute-start.15 = (bf16[1024,128]{1,0:T(8,128)(2,1)S(1)}, bf16[1024,128]{1,0:T(8,128)(2,1)S(1)}, u32[]{:S(2)}, u32[]{:S(2)}) collective-permute-start(bf16[1024,128]{1,0:T(8,128)(2,1)S(1)} %copy-done.17), channel_id=1, source_target_pairs={{128,0},{192,64},{0,128},{64,192},{129,1},{193,65},{1,129},{65,193... | collective-permute-start | bytes 786440 | tf_op jit(solution)/shard_map/ppermute | solution.py:265
  119.2 10.6 %collective-permute-start.16 = (bf16[1024,128]{1,0:T(8,128)(2,1)S(1)}, bf16[1024,128]{1,0:T(8,128)(2,1)S(1)}, u32[]{:S(2)}, u32[]{:S(2)}) collective-permute-start(bf16[1024,128]{1,0:T(8,128)(2,1)S(1)} %copy-done.16), channel_id=1, source_target_pairs={{64,0},{128,64},{192,128},{0,192},{65,1},{129,65},{193,129},{1,193... | collective-permute-start | bytes 786440 | tf_op jit(solution)/shard_map/ppermute | solution.py:265
  123.5 6.3 %copy-start.10 = (bf16[1024,128]{1,0:T(8,128)(2,1)S(1)}, bf16[1024,128]{1,0:T(8,128)(2,1)}, u32[]{:S(2)}) copy-start(bf16[1024,128]{1,0:T(8,128)(2,1)} %get-tuple-element.9) | copy-start | bytes 786436
  123.6 12.4 %collective-permute-start.25 = (bf16[2,32,128]{2,1,0:T(8,128)(2,1)S(1)}, bf16[2,32,128]{2,1,0:T(8,128)(2,1)S(1)}, u32[]{:S(2)}, u32[]{:S(2)}) collective-permute-start(bf16[2,32,128]{2,1,0:T(8,128)(2,1)S(1)} %get-tuple-element.35), channel_id=1, source_target_pairs={{0,0},{64,1},{128,2},{192,3},{1,64},{65,65},{129,66},{193,67},{2,1... | collective-permute-start | bytes 49160 | tf_op jit(solution)/shard_map/ppermute | solution.py:306
  130.7 11.9 %collective-permute-start.28 = (bf16[2,32,128]{2,1,0:T(8,128)(2,1)S(1)}, bf16[2,32,128]{2,1,0:T(8,128)(2,1)S(1)}, u32[]{:S(2)}, u32[]{:S(2)}) collective-permute-start(bf16[2,32,128]{2,1,0:T(8,128)(2,1)S(1)} %get-tuple-element.32), channel_id=1, source_target_pairs={{3,0},{67,1},{131,2},{195,3},{0,64},{64,65},{128,66},{192,67},{1,1... | collective-permute-start | bytes 49160 | tf_op jit(solution)/shard_map/ppermute | solution.py:306
  134.4 8.1 %collective-permute-start.27 = (bf16[2,32,128]{2,1,0:T(8,128)(2,1)S(1)}, bf16[2,32,128]{2,1,0:T(8,128)(2,1)S(1)}, u32[]{:S(2)}, u32[]{:S(2)}) collective-permute-start(bf16[2,32,128]{2,1,0:T(8,128)(2,1)S(1)} %get-tuple-element.33), channel_id=1, source_target_pairs={{2,0},{66,1},{130,2},{194,3},{3,64},{67,65},{131,66},{195,67},{0,1... | collective-permute-start | bytes 49160 | tf_op jit(solution)/shard_map/ppermute | solution.py:306
  135.2 7.4 %collective-permute-start.26 = (bf16[2,32,128]{2,1,0:T(8,128)(2,1)S(1)}, bf16[2,32,128]{2,1,0:T(8,128)(2,1)S(1)}, u32[]{:S(2)}, u32[]{:S(2)}) collective-permute-start(bf16[2,32,128]{2,1,0:T(8,128)(2,1)S(1)} %get-tuple-element.34), channel_id=1, source_target_pairs={{1,0},{65,1},{129,2},{193,3},{2,64},{66,65},{130,66},{194,67},{3,1... | collective-permute-start | bytes 49160 | tf_op jit(solution)/shard_map/ppermute | solution.py:306

commit v3 on v2

--- a/solution.py
+++ b/solution.py
@@ -224,25 +224,29 @@
     ]
 
 
+def near(value):
+    return pltpu.with_memory_space_constraint(value, pltpu.VMEM)
+
+
 def stats_call(seg_blocks, seg_audio, q, o, z_all, c_all):
     return pl.pallas_call(
         stats_kernel,
-        out_shape=jax.ShapeDtypeStruct((NY, 3, ROWS), F32),
+        out_shape=pltpu.VMEM((NY, 3, ROWS), F32),
         in_specs=[SM] * 2 + [HB] * (2 * NY + 2),
         out_specs=VM,
         scratch_shapes=buffers()
         + [pltpu.VMEM((NY, 8, ROWS), F32)] * 3
         + [pltpu.SemaphoreType.DMA((2 * NY,))],
-        compiler_params=pltpu.CompilerParams(vmem_limit_bytes=56 << 20),
+        compiler_params=pltpu.CompilerParams(vmem_limit_bytes=24 << 20),
         name="stats",
-    )(seg_blocks, seg_audio, *q, *o, z_all, c_all)
+    )(seg_blocks, seg_audio, *map(near, (*q, *o, z_all, c_all)))
 
 
 def grad_call(seg_blocks, seg_audio, q, o, st, z_all, c_all):
-    part = jax.ShapeDtypeStruct((NZ, NX, 2, SLICE, DH), F32)
+    part = pltpu.VMEM((NZ, NX, 2, SLICE, DH), F32)
     return pl.pallas_call(
         grad_kernel,
-        out_shape=(jax.ShapeDtypeStruct((ROWS, DH), BF),) * NY + (part, part),
+        out_shape=(pltpu.VMEM((ROWS, DH), BF),) * NY + (part, part),
         in_specs=[SM] * 2 + [HB] * (3 * NY + 2),
         out_specs=(VM,) * (NY + 2),
         scratch_shapes=buffers()
@@ -256,9 +260,9 @@
             pltpu.SemaphoreType.DMA((2 * NY,)),
             pltpu.SemaphoreType.DMA((1,)),
         ],
-        compiler_params=pltpu.CompilerParams(vmem_limit_bytes=56 << 20),
+        compiler_params=pltpu.CompilerParams(vmem_limit_bytes=24 << 20),
         name="grads",
-    )(seg_blocks, seg_audio, *q, *o, *st, z_all, c_all)
+    )(seg_blocks, seg_audio, *map(near, (*q, *o, *st, z_all, c_all)))
 
 
 def shift(value, axis, size, by):
@@ -288,14 +292,17 @@
     *dq, own_part, other_part = grad_call(
         seg_blocks, seg_audio, q, o, sts, z_all, c_all
     )
+    dq_parts = [shift(dq[d], "y", NY, -d) for d in range(1, NY)]
     dq_sum = dq[0].astype(F32)
-    for d in range(1, NY):
-        dq_sum = dq_sum + shift(dq[d], "y", NY, -d).astype(F32)
+    for part in dq_parts:
+        dq_sum = dq_sum + part.astype(F32)
     d_query = dq_sum.astype(BF).reshape(BLK, GROUP, DH)
     both = own_part + shift(other_part, "c", NC, 1)
     low = both.astype(BF)
-    kv_sum = both[0]
-    for d in range(1, NZ):
+    carried = shift(low[4], "z", NZ, -1)
+    third = (both[3] + carried.astype(F32)).astype(BF)
+    kv_sum = both[0] + shift(third, "z", NZ, -3).astype(F32)
+    for d in (1, 2, 5, 6, 7):
         kv_sum = kv_sum + shift(low[d], "z", NZ, -d).astype(F32)
     kv_low = kv_sum.astype(BF)
     back = []

time: 145 us -> 138 us (0.952)
  starting transfers between devices: 53.9 us -> 56.9 us
  local copies, waits for them, and re-layouts: 5.89 us -> 3.04 us
  Pallas kernels: 31.8 us -> 29 us
  waiting for transfers between devices: 49 us -> 46.2 us
    ppermute x21, waiting for transfers between devices: 22.6 us -> 19.8 us  [shift(): lax.ppermute(value, axis, [((n + by) % size, n) for n in range(size)])]
    unnamed x47 -> x21, local copies, waits for them, and re-layouts: 4.87 us -> 2.06 us
    pallas_call x2, Pallas kernels: 31.8 us -> 29 us  [the longest x1 18 us: grad_call(): pl.pallas_call(grad_kernel, out_shape=(pltpu.VMEM((ROWS, DH), BF),) * NY...]
    ppermute x4, starting transfers between devices: 11.5 us -> 13.5 us  [steps(): back.append(lax.ppermute(kv_low[r], ('y', 'x'), perm))]
  transfers between devices with their start and end apart: 30 -> 30, of which waited for: 15 -> 13; matrix products, arithmetic and copies ran while one was open for 1% -> 1% of each run, Pallas kernels for 0% -> 0%
where the time goes in v3:
time: 138 us; the launch traced here: 137 us
  starting transfers between devices  56.9 us (41%)
  waiting for transfers between devices  46.2 us (33%)
  Pallas kernels  29 us (21%)
  local copies, waits for them, and re-layouts  3.04 us (2%)
    ppermute x21, starting transfers between devices, shift(): lax.ppermute(value, axis, [((n + by) % size, n) for n in range(size)])  27.3 us
    ppermute x21, waiting for transfers between devices, shift(): lax.ppermute(value, axis, [((n + by) % size, n) for n in range(size)])  19.8 us
    pallas_call x1, Pallas kernels, grad_call(): pl.pallas_call(grad_kernel, out_shape=(pltpu.VMEM((ROWS, DH), BF),) * NY...  18 us
    all_to_all x1, waiting for transfers between devices, steps(): lax.all_to_all(jnp.broadcast_to(own[None], (NZ,) + own.shape), 'z', 0, 0)  13.6 us
    ppermute x4, starting transfers between devices, steps(): back.append(lax.ppermute(kv_low[r], ('y', 'x'), perm))  13.5 us
    pallas_call x1, Pallas kernels, stats_call(): pl.pallas_call(stats_kernel, out_shape=pltpu.VMEM((NY, 3, ROWS), F32), in...  11 us
    all_to_all x1, starting transfers between devices, steps(): lax.all_to_all(jnp.broadcast_to(own[None], (NZ,) + own.shape), 'z', 0, 0)  8.6 us
    ppermute x4, starting transfers between devices, steps(): rounds.append(lax.ppermute(piece, ('y', 'x'), perm))  7.45 us
  transfers between devices with their start and end apart: 30, of which 13 were waited for; matrix products, arithmetic and copies ran while one was open for 1% of the time, Pallas kernels for 0%

profile of v3, /device:TPU:16, one launch (start us, length us, event | category | flops | bytes accessed | tf_op | source)
XLA Modules:
  0.0 137.2 jit_solution(5645398885862252277)
XLA Ops:
  0.7 0.7 copy-done.5
  1.4 0.0 copy-done.4
  1.5 4.7 %collective-permute-start.6 = (bf16[2,32,128]{2,1,0:T(8,128)(2,1)S(1)}, bf16[2,32,128]{2,1,0:T(8,128)(2,1)S(1)}, u32[]{:S(2)}, u32[]{:S(2)}) collective-permute-start(bf16[2,32,128]{2,1,0:T(8,128)(2,1)S(1)} %get-tuple-element.35), channel_id=1, source_target_pairs={{0,0},{1,64},{2,128},{3,192},{64,1},{65,65},{66,129},{67,193},{128... | collective-permute-start | bytes 49160 | tf_op jit(solution)/shard_map/ppermute | solution.py:281
  6.2 2.7 %collective-permute-start.7 = (bf16[2,32,128]{2,1,0:T(8,128)(2,1)S(1)}, bf16[2,32,128]{2,1,0:T(8,128)(2,1)S(1)}, u32[]{:S(2)}, u32[]{:S(2)}) collective-permute-start(bf16[2,32,128]{2,1,0:T(8,128)(2,1)S(1)} %get-tuple-element.36), channel_id=1, source_target_pairs={{0,1},{1,65},{2,129},{3,193},{64,2},{65,66},{66,130},{67,194},{128... | collective-permute-start | bytes 49160 | tf_op jit(solution)/shard_map/ppermute | solution.py:281
  8.9 0.0 collective-permute-start.8
  8.9 0.0 collective-permute-start.9
  8.9 2.1 %collective-permute-done.6 = bf16[2,32,128]{2,1,0:T(8,128)(2,1)S(1)} collective-permute-done((bf16[2,32,128]{2,1,0:T(8,128)(2,1)S(1)}, bf16[2,32,128]{2,1,0:T(8,128)(2,1)S(1)}, u32[]{:S(2)}, u32[]{:S(2)}) %collective-permute-start.6) | collective-permute-done | bytes 16416 | tf_op jit(solution)/shard_map/ppermute | solution.py:281
  11.0 1.4 %collective-permute-done.7 = bf16[2,32,128]{2,1,0:T(8,128)(2,1)S(1)} collective-permute-done((bf16[2,32,128]{2,1,0:T(8,128)(2,1)S(1)}, bf16[2,32,128]{2,1,0:T(8,128)(2,1)S(1)}, u32[]{:S(2)}, u32[]{:S(2)}) %collective-permute-start.7) | collective-permute-done | bytes 16416 | tf_op jit(solution)/shard_map/ppermute | solution.py:281
  12.4 1.8 %collective-permute-done.8 = bf16[2,32,128]{2,1,0:T(8,128)(2,1)S(1)} collective-permute-done((bf16[2,32,128]{2,1,0:T(8,128)(2,1)S(1)}, bf16[2,32,128]{2,1,0:T(8,128)(2,1)S(1)}, u32[]{:S(2)}, u32[]{:S(2)}) %collective-permute-start.8) | collective-permute-done | bytes 16416 | tf_op jit(solution)/shard_map/ppermute | solution.py:281
  14.2 0.9 collective-permute-done.9
  15.1 0.9 broadcast_in_dim.2
  16.0 8.6 %all-to-all-start = ((bf16[8,4,2,32,128]{4,3,2,1,0:T(8,128)(2,1)}), bf16[8,4,2,32,128]{4,3,2,1,0:T(8,128)(2,1)S(1)}, u32[]{:S(2)}, u32[]{:S(2)}) async-start(bf16[8,4,2,32,128]{4,3,2,1,0:T(8,128)(2,1)} %broadcast_in_dim.2), calls=%async_computation | async-start | bytes 1048576 | tf_op jit(solution)/shard_map/all_to_all | solution.py:287
  24.6 0.0 copy-start.2
  24.6 0.0 copy-start.3
  24.6 2.0 %collective-permute-start = (bf16[1024,128]{1,0:T(8,128)(2,1)S(1)}, bf16[1024,128]{1,0:T(8,128)(2,1)S(1)}, u32[]{:S(2)}, u32[]{:S(2)}) collective-permute-start(bf16[1024,128]{1,0:T(8,128)(2,1)S(1)} %bitcast.80), channel_id=1, source_target_pairs={{64,0},{128,64},{192,128},{0,192},{65,1},{129,65},{193,129},{1,193... | collective-permute-start | bytes 786440 | tf_op jit(solution)/shard_map/ppermute | solution.py:269
  26.6 0.1 collective-permute-start.4
  26.7 13.6 %all-to-all-done.refs_8_.refs_12_ = bf16[8,4,2,32,128]{4,3,2,1,0:T(8,128)(2,1)S(1)} async-done(((bf16[8,4,2,32,128]{4,3,2,1,0:T(8,128)(2,1)}), bf16[8,4,2,32,128]{4,3,2,1,0:T(8,128)(2,1)S(1)}, u32[]{:S(2)}, u32[]{:S(2)}) %all-to-all-start) | async-done | bytes 524320 | tf_op jit(solution)/shard_map/all_to_all | solution.py:287
  40.4 0.0 collective-permute-start.10
  40.4 0.0 collective-permute-start.2
  40.4 2.0 %collective-permute-start.3 = (bf16[1024,128]{1,0:T(8,128)(2,1)S(1)}, bf16[1024,128]{1,0:T(8,128)(2,1)S(1)}, u32[]{:S(2)}, u32[]{:S(2)}) collective-permute-start(bf16[1024,128]{1,0:T(8,128)(2,1)S(1)} %bitcast.85), channel_id=1, source_target_pairs={{64,0},{128,64},{192,128},{0,192},{65,1},{129,65},{193,129},{1,193... | collective-permute-start | bytes 786440 | tf_op jit(solution)/shard_map/ppermute | solution.py:269
  42.4 0.0 collective-permute-done.refs_1_
  42.4 1.6 %collective-permute-start.1 = (bf16[1024,128]{1,0:T(8,128)(2,1)S(1)}, bf16[1024,128]{1,0:T(8,128)(2,1)S(1)}, u32[]{:S(2)}, u32[]{:S(2)}) collective-permute-start(bf16[1024,128]{1,0:T(8,128)(2,1)S(1)} %collective-permute-done.refs_1_), channel_id=1, source_target_pairs={{64,0},{128,64},{192,128},{0,192},{65,1},{129,65},{193,129},{1,193... | collective-permute-start | bytes 786440 | tf_op jit(solution)/shard_map/ppermute | solution.py:269
  44.0 0.0 collective-permute-done.4.refs_7_
  44.0 0.4 collective-permute-start.5
  44.4 5.1 %collective-permute-done.2.refs_3_ = bf16[1024,128]{1,0:T(8,128)(2,1)S(1)} collective-permute-done((bf16[1024,128]{1,0:T(8,128)(2,1)S(1)}, bf16[1024,128]{1,0:T(8,128)(2,1)S(1)}, u32[]{:S(2)}, u32[]{:S(2)}) %collective-permute-start.2) | collective-permute-done | bytes 262176 | tf_op jit(solution)/shard_map/ppermute | solution.py:269
  49.6 0.5 collective-permute-done.3.refs_5_
  50.0 5.2 %collective-permute-done.1.refs_2_ = bf16[1024,128]{1,0:T(8,128)(2,1)S(1)} collective-permute-done((bf16[1024,128]{1,0:T(8,128)(2,1)S(1)}, bf16[1024,128]{1,0:T(8,128)(2,1)S(1)}, u32[]{:S(2)}, u32[]{:S(2)}) %collective-permute-start.1) | collective-permute-done | bytes 262176 | tf_op jit(solution)/shard_map/ppermute | solution.py:269
  55.2 0.0 collective-permute-done.5.refs_6_
  55.2 11.0 %stats.1.refs_8_ = f32[4,3,1024]{2,1,0:T(4,128)S(1)} custom-call(s32[32]{0:T(128)S(1)} %copy-done.2, s32[32]{0:T(128)S(1)} %copy-done.3, bf16[1024,128]{1,0:T(8,128)(2,1)S(1)} %bitcast.82, bf16[1024,128]{1,0:T(8,128)(2,1)S(1)} %collective-permute-done.refs_1_, bf16[1024,128]{1,0:T(8,128)(2,1)S(1)} %collective-permute-done.1.refs_2_, ...), custom_call_target="tpu_custom_call" | custom-call | tf_op jit(solution)/shard_map/stats/pallas_call | solution.py:232
  66.3 3.0 %collective-permute-start.13 = (f32[4,3,1024]{2,1,0:T(4,128)S(1)}, f32[4,3,1024]{2,1,0:T(4,128)S(1)}, u32[]{:S(2)}, u32[]{:S(2)}) collective-permute-start(f32[4,3,1024]{2,1,0:T(4,128)S(1)} %stats.1.refs_8_), channel_id=1, source_target_pairs={{192,0},{0,64},{64,128},{128,192},{193,1},{1,65},{65,129},{129,193... | collective-permute-start | bytes 147464 | tf_op jit(solution)/shard_map/ppermute | solution.py:269
  69.3 0.0 collective-permute-start.12
  69.3 2.0 %collective-permute-start.11 = (f32[4,3,1024]{2,1,0:T(4,128)S(1)}, f32[4,3,1024]{2,1,0:T(4,128)S(1)}, u32[]{:S(2)}, u32[]{:S(2)}) collective-permute-start(f32[4,3,1024]{2,1,0:T(4,128)S(1)} %stats.1.refs_8_), channel_id=1, source_target_pairs={{64,0},{128,64},{192,128},{0,192},{65,1},{129,65},{193,129},{1,193... | collective-permute-start | bytes 147464 | tf_op jit(solution)/shard_map/ppermute | solution.py:269
  71.3 0.0 collective-permute-done.13.refs_11_
  71.3 3.8 %collective-permute-done.12.refs_10_ = f32[4,3,1024]{2,1,0:T(4,128)S(1)} collective-permute-done((f32[4,3,1024]{2,1,0:T(4,128)S(1)}, f32[4,3,1024]{2,1,0:T(4,128)S(1)}, u32[]{:S(2)}, u32[]{:S(2)}) %collective-permute-start.12) | collective-permute-done | bytes 49184 | tf_op jit(solution)/shard_map/ppermute | solution.py:269
  75.1 0.0 collective-permute-done.11.refs_9_
  75.1 18.0 %grads.1 = (bf16[1024,128]{1,0:T(8,128)(2,1)S(1)}, bf16[1024,128]{1,0:T(8,128)(2,1)S(1)}, bf16[1024,128]{1,0:T(8,128)(2,1)S(1)}, bf16[1024,128]{1,0:T(8,128)(2,1...) custom-call(s32[32]{0:T(128)S(1)} %copy-done.2, s32[32]{0:T(128)S(1)} %copy-done.3, ...), custom_call_target="tpu_custom_call" | custom-call | tf_op jit(solution)/shard_map/grads/pallas_call | solution.py:247
  93.0 0.1 collective-permute-start.17
  93.2 2.6 %collective-permute-done.17 = f32[8,4,2,32,128]{4,3,2,1,0:T(8,128)S(1)} collective-permute-done((f32[8,4,2,32,128]{4,3,2,1,0:T(8,128)S(1)}, f32[8,4,2,32,128]{4,3,2,1,0:T(8,128)S(1)}, u32[]{:S(2)}, u32[]{:S(2)}) %collective-permute-start.17) | collective-permute-done | bytes 1048608 | tf_op jit(solution)/shard_map/ppermute | solution.py:269
  95.8 0.2 fusion.18
  96.1 0.6 collective-permute-start.18
  96.7 2.7 %collective-permute-start.24 = (bf16[4,2,32,128]{3,2,1,0:T(8,128)(2,1)S(1)}, bf16[4,2,32,128]{3,2,1,0:T(8,128)(2,1)S(1)}, u32[]{:S(2)}, u32[]{:S(2)}) collective-permute-start(bf16[4,2,32,128]{3,2,1,0:T(8,128)(2,1)S(1)} %get-tuple-element.24), channel_id=1, source_target_pairs={{8,0},{16,8},{24,16},{32,24},{40,32},{48,40},{56,48},{0,56},{9,1},... | collective-permute-start | bytes 196616 | tf_op jit(solution)/shard_map/ppermute | solution.py:269
  99.4 1.4 %collective-permute-start.22 = (bf16[4,2,32,128]{3,2,1,0:T(8,128)(2,1)S(1)}, bf16[4,2,32,128]{3,2,1,0:T(8,128)(2,1)S(1)}, u32[]{:S(2)}, u32[]{:S(2)}) collective-permute-start(bf16[4,2,32,128]{3,2,1,0:T(8,128)(2,1)S(1)} %get-tuple-element.26), channel_id=1, source_target_pairs={{24,0},{32,8},{40,16},{48,24},{56,32},{0,40},{8,48},{16,56},{25,1}... | collective-permute-start | bytes 196616 | tf_op jit(solution)/shard_map/ppermute | solution.py:269
  100.8 1.5 %collective-permute-start.21 = (bf16[4,2,32,128]{3,2,1,0:T(8,128)(2,1)S(1)}, bf16[4,2,32,128]{3,2,1,0:T(8,128)(2,1)S(1)}, u32[]{:S(2)}, u32[]{:S(2)}) collective-permute-start(bf16[4,2,32,128]{3,2,1,0:T(8,128)(2,1)S(1)} %get-tuple-element.27), channel_id=1, source_target_pairs={{48,0},{56,8},{0,16},{8,24},{16,32},{24,40},{32,48},{40,56},{49,1}... | collective-permute-start | bytes 196616 | tf_op jit(solution)/shard_map/ppermute | solution.py:269
  102.3 1.5 %collective-permute-start.20 = (bf16[4,2,32,128]{3,2,1,0:T(8,128)(2,1)S(1)}, bf16[4,2,32,128]{3,2,1,0:T(8,128)(2,1)S(1)}, u32[]{:S(2)}, u32[]{:S(2)}) collective-permute-start(bf16[4,2,32,128]{3,2,1,0:T(8,128)(2,1)S(1)} %get-tuple-element.28), channel_id=1, source_target_pairs={{56,0},{0,8},{8,16},{16,24},{24,32},{32,40},{40,48},{48,56},{57,1}... | collective-permute-start | bytes 196616 | tf_op jit(solution)/shard_map/ppermute | solution.py:269
  103.8 3.6 %collective-permute-start.19 = (bf16[4,2,32,128]{3,2,1,0:T(8,128)(2,1)S(1)}, bf16[4,2,32,128]{3,2,1,0:T(8,128)(2,1)S(1)}, u32[]{:S(2)}, u32[]{:S(2)}) collective-permute-start(bf16[4,2,32,128]{3,2,1,0:T(8,128)(2,1)S(1)} %fusion.2), channel_id=1, source_target_pairs={{40,0},{48,8},{56,16},{0,24},{8,32},{16,40},{24,48},{32,56},{41,1}... | collective-permute-start | bytes 196616 | tf_op jit(solution)/shard_map/ppermute | solution.py:269
  107.5 1.6 %collective-permute-start.14 = (bf16[1024,128]{1,0:T(8,128)(2,1)S(1)}, bf16[1024,128]{1,0:T(8,128)(2,1)S(1)}, u32[]{:S(2)}, u32[]{:S(2)}) collective-permute-start(bf16[1024,128]{1,0:T(8,128)(2,1)S(1)} %get-tuple-element.10), channel_id=1, source_target_pairs={{192,0},{0,64},{64,128},{128,192},{193,1},{1,65},{65,129},{129,193... | collective-permute-start | bytes 786440 | tf_op jit(solution)/shard_map/ppermute | solution.py:269
  109.0 0.0 collective-permute-done.22
  109.0 0.8 collective-permute-start.15
  109.8 0.0 collective-permute-done.21
  109.8 2.3 %collective-permute-start.16 = (bf16[1024,128]{1,0:T(8,128)(2,1)S(1)}, bf16[1024,128]{1,0:T(8,128)(2,1)S(1)}, u32[]{:S(2)}, u32[]{:S(2)}) collective-permute-start(bf16[1024,128]{1,0:T(8,128)(2,1)S(1)} %get-tuple-element.12), channel_id=1, source_target_pairs={{64,0},{128,64},{192,128},{0,192},{65,1},{129,65},{193,129},{1,193... | collective-permute-start | bytes 786440 | tf_op jit(solution)/shard_map/ppermute | solution.py:269
  112.1 0.0 collective-permute-done.20
  112.1 0.0 collective-permute-done.19
  112.1 0.1 fusion.9
  112.2 6.8 %collective-permute-start.25 = (bf16[2,32,128]{2,1,0:T(8,128)(2,1)S(1)}, bf16[2,32,128]{2,1,0:T(8,128)(2,1)S(1)}, u32[]{:S(2)}, u32[]{:S(2)}) collective-permute-start(bf16[2,32,128]{2,1,0:T(8,128)(2,1)S(1)} %get-tuple-element.34), channel_id=1, source_target_pairs={{0,0},{64,1},{128,2},{192,3},{1,64},{65,65},{129,66},{193,67},{2,1... | collective-permute-start | bytes 49160 | tf_op jit(solution)/shard_map/ppermute | solution.py:313
  119.0 1.6 %collective-permute-done.15 = bf16[1024,128]{1,0:T(8,128)(2,1)S(1)} collective-permute-done((bf16[1024,128]{1,0:T(8,128)(2,1)S(1)}, bf16[1024,128]{1,0:T(8,128)(2,1)S(1)}, u32[]{:S(2)}, u32[]{:S(2)}) %collective-permute-start.15) | collective-permute-done | bytes 262176 | tf_op jit(solution)/shard_map/ppermute | solution.py:269
  120.6 1.0 collective-permute-done.16
  121.6 0.9 fusion
  122.4 4.6 %collective-permute-start.28 = (bf16[2,32,128]{2,1,0:T(8,128)(2,1)S(1)}, bf16[2,32,128]{2,1,0:T(8,128)(2,1)S(1)}, u32[]{:S(2)}, u32[]{:S(2)}) collective-permute-start(bf16[2,32,128]{2,1,0:T(8,128)(2,1)S(1)} %get-tuple-element.31), channel_id=1, source_target_pairs={{3,0},{67,1},{131,2},{195,3},{0,64},{64,65},{128,66},{192,67},{1,1... | collective-permute-start | bytes 49160 | tf_op jit(solution)/shard_map/ppermute | solution.py:313
  127.1 1.4 %collective-permute-start.27 = (bf16[2,32,128]{2,1,0:T(8,128)(2,1)S(1)}, bf16[2,32,128]{2,1,0:T(8,128)(2,1)S(1)}, u32[]{:S(2)}, u32[]{:S(2)}) collective-permute-start(bf16[2,32,128]{2,1,0:T(8,128)(2,1)S(1)} %get-tuple-element.32), channel_id=1, source_target_pairs={{2,0},{66,1},{130,2},{194,3},{3,64},{67,65},{131,66},{195,67},{0,1... | collective-permute-start | bytes 49160 | tf_op jit(solution)/shard_map/ppermute | solution.py:313
  128.5 0.7 collective-permute-start.26
  129.2 0.0 collective-permute-done.25
  129.2 6.6 %collective-permute-done.26 = bf16[2,32,128]{2,1,0:T(8,128)(2,1)S(1)} collective-permute-done((bf16[2,32,128]{2,1,0:T(8,128)(2,1)S(1)}, bf16[2,32,128]{2,1,0:T(8,128)(2,1)S(1)}, u32[]{:S(2)}, u32[]{:S(2)}) %collective-permute-start.26) | collective-permute-done | bytes 16416 | tf_op jit(solution)/shard_map/ppermute | solution.py:313
  136.0 0.6 copy.14
  136.6 0.6 copy.13
  (32 shorter events, 0.2 us)
Async XLA Ops:
  0.7 0.8 copy-start.5
  0.7 0.8 copy-start.4
  1.5 9.5 %collective-permute-start.6 = (bf16[2,32,128]{2,1,0:T(8,128)(2,1)S(1)}, bf16[2,32,128]{2,1,0:T(8,128)(2,1)S(1)}, u32[]{:S(2)}, u32[]{:S(2)}) collective-permute-start(bf16[2,32,128]{2,1,0:T(8,128)(2,1)S(1)} %get-tuple-element.35), channel_id=1, source_target_pairs={{0,0},{1,64},{2,128},{3,192},{64,1},{65,65},{66,129},{67,193},{128... | collective-permute-start | bytes 49160 | tf_op jit(solution)/shard_map/ppermute | solution.py:281
  6.2 6.2 %collective-permute-start.7 = (bf16[2,32,128]{2,1,0:T(8,128)(2,1)S(1)}, bf16[2,32,128]{2,1,0:T(8,128)(2,1)S(1)}, u32[]{:S(2)}, u32[]{:S(2)}) collective-permute-start(bf16[2,32,128]{2,1,0:T(8,128)(2,1)S(1)} %get-tuple-element.36), channel_id=1, source_target_pairs={{0,1},{1,65},{2,129},{3,193},{64,2},{65,66},{66,130},{67,194},{128... | collective-permute-start | bytes 49160 | tf_op jit(solution)/shard_map/ppermute | solution.py:281
  8.9 5.2 %collective-permute-start.8 = (bf16[2,32,128]{2,1,0:T(8,128)(2,1)S(1)}, bf16[2,32,128]{2,1,0:T(8,128)(2,1)S(1)}, u32[]{:S(2)}, u32[]{:S(2)}) collective-permute-start(bf16[2,32,128]{2,1,0:T(8,128)(2,1)S(1)} %get-tuple-element.37), channel_id=1, source_target_pairs={{0,2},{1,66},{2,130},{3,194},{64,3},{65,67},{66,131},{67,195},{128... | collective-permute-start | bytes 49160 | tf_op jit(solution)/shard_map/ppermute | solution.py:281
  8.9 6.1 %collective-permute-start.9 = (bf16[2,32,128]{2,1,0:T(8,128)(2,1)S(1)}, bf16[2,32,128]{2,1,0:T(8,128)(2,1)S(1)}, u32[]{:S(2)}, u32[]{:S(2)}) collective-permute-start(bf16[2,32,128]{2,1,0:T(8,128)(2,1)S(1)} %get-tuple-element.38), channel_id=1, source_target_pairs={{0,3},{1,67},{2,131},{3,195},{64,0},{65,64},{66,128},{67,192},{128... | collective-permute-start | bytes 49160 | tf_op jit(solution)/shard_map/ppermute | solution.py:281
  16.0 8.6 %copy-start = (bf16[128,8,128]{2,1,0:T(8,128)(2,1)S(1)}, bf16[128,8,128]{2,1,0:T(8,128)(2,1)}, u32[]{:S(2)}) copy-start(bf16[128,8,128]{2,1,0:T(8,128)(2,1)} %param.6) | copy-start | bytes 786436
  16.0 10.6 %copy-start.1 = (bf16[128,8,128]{2,1,0:T(8,128)(2,1)S(1)}, bf16[128,8,128]{2,1,0:T(8,128)(2,1)}, u32[]{:S(2)}) copy-start(bf16[128,8,128]{2,1,0:T(8,128)(2,1)} %param.9) | copy-start | bytes 786436
  16.0 24.4 %all-to-all-start = ((bf16[8,4,2,32,128]{4,3,2,1,0:T(8,128)(2,1)}), bf16[8,4,2,32,128]{4,3,2,1,0:T(8,128)(2,1)S(1)}, u32[]{:S(2)}, u32[]{:S(2)}) async-start(bf16[8,4,2,32,128]{4,3,2,1,0:T(8,128)(2,1)} %broadcast_in_dim.2), calls=%async_computation | async-start | bytes 1048576 | tf_op jit(solution)/shard_map/all_to_all | solution.py:287
  24.6 30.6 %copy-start.2 = (s32[32]{0:T(128)S(1)}, s32[32]{0:T(128)}, u32[]{:S(2)}) copy-start(s32[32]{0:T(128)} %seg_blocks.3) | copy-start | bytes 388
  24.6 30.6 %copy-start.3 = (s32[32]{0:T(128)S(1)}, s32[32]{0:T(128)}, u32[]{:S(2)}) copy-start(s32[32]{0:T(128)} %seg_audio.3) | copy-start | bytes 388
  24.6 17.8 %collective-permute-start = (bf16[1024,128]{1,0:T(8,128)(2,1)S(1)}, bf16[1024,128]{1,0:T(8,128)(2,1)S(1)}, u32[]{:S(2)}, u32[]{:S(2)}) collective-permute-start(bf16[1024,128]{1,0:T(8,128)(2,1)S(1)} %bitcast.80), channel_id=1, source_target_pairs={{64,0},{128,64},{192,128},{0,192},{65,1},{129,65},{193,129},{1,193... | collective-permute-start | bytes 786440 | tf_op jit(solution)/shard_map/ppermute | solution.py:269
  26.6 17.4 %collective-permute-start.4 = (bf16[1024,128]{1,0:T(8,128)(2,1)S(1)}, bf16[1024,128]{1,0:T(8,128)(2,1)S(1)}, u32[]{:S(2)}, u32[]{:S(2)}) collective-permute-start(bf16[1024,128]{1,0:T(8,128)(2,1)S(1)} %bitcast.84), channel_id=1, source_target_pairs={{192,0},{0,64},{64,128},{128,192},{193,1},{1,65},{65,129},{129,193... | collective-permute-start | bytes 786440 | tf_op jit(solution)/shard_map/ppermute | solution.py:269
  40.4 14.8 %collective-permute-start.10 = (bf16[8,4,2,32,128]{4,3,2,1,0:T(8,128)(2,1)S(1)}, bf16[8,4,2,32,128]{4,3,2,1,0:T(8,128)(2,1)S(1)}, u32[]{:S(2)}, u32[]{:S(2)}) collective-permute-start(bf16[8,4,2,32,128]{4,3,2,1,0:T(8,128)(2,1)S(1)} %all-to-all-done.refs_8_.refs_12_), channel_id=1, source_target_pairs={{4,0},{0,4},{5,1},{1,5},{6,2},{2,6},{7,3},{3,7},{12,8},{8,12},{13,... | collective-permute-start | bytes 1572872 | tf_op jit(solution)/shard_map/ppermute | solution.py:269
  40.4 9.2 %collective-permute-start.2 = (bf16[1024,128]{1,0:T(8,128)(2,1)S(1)}, bf16[1024,128]{1,0:T(8,128)(2,1)S(1)}, u32[]{:S(2)}, u32[]{:S(2)}) collective-permute-start(bf16[1024,128]{1,0:T(8,128)(2,1)S(1)} %bitcast.81), channel_id=1, source_target_pairs={{192,0},{0,64},{64,128},{128,192},{193,1},{1,65},{65,129},{129,193... | collective-permute-start | bytes 786440 | tf_op jit(solution)/shard_map/ppermute | solution.py:269
  40.4 9.6 %collective-permute-start.3 = (bf16[1024,128]{1,0:T(8,128)(2,1)S(1)}, bf16[1024,128]{1,0:T(8,128)(2,1)S(1)}, u32[]{:S(2)}, u32[]{:S(2)}) collective-permute-start(bf16[1024,128]{1,0:T(8,128)(2,1)S(1)} %bitcast.85), channel_id=1, source_target_pairs={{64,0},{128,64},{192,128},{0,192},{65,1},{129,65},{193,129},{1,193... | collective-permute-start | bytes 786440 | tf_op jit(solution)/shard_map/ppermute | solution.py:269
  42.4 12.8 %collective-permute-start.1 = (bf16[1024,128]{1,0:T(8,128)(2,1)S(1)}, bf16[1024,128]{1,0:T(8,128)(2,1)S(1)}, u32[]{:S(2)}, u32[]{:S(2)}) collective-permute-start(bf16[1024,128]{1,0:T(8,128)(2,1)S(1)} %collective-permute-done.refs_1_), channel_id=1, source_target_pairs={{64,0},{128,64},{192,128},{0,192},{65,1},{129,65},{193,129},{1,193... | collective-permute-start | bytes 786440 | tf_op jit(solution)/shard_map/ppermute | solution.py:269
  44.0 11.2 %collective-permute-start.5 = (bf16[1024,128]{1,0:T(8,128)(2,1)S(1)}, bf16[1024,128]{1,0:T(8,128)(2,1)S(1)}, u32[]{:S(2)}, u32[]{:S(2)}) collective-permute-start(bf16[1024,128]{1,0:T(8,128)(2,1)S(1)} %collective-permute-done.4.refs_7_), channel_id=1, source_target_pairs={{192,0},{0,64},{64,128},{128,192},{193,1},{1,65},{65,129},{129,193... | collective-permute-start | bytes 786440 | tf_op jit(solution)/shard_map/ppermute | solution.py:269
  66.3 5.0 %collective-permute-start.13 = (f32[4,3,1024]{2,1,0:T(4,128)S(1)}, f32[4,3,1024]{2,1,0:T(4,128)S(1)}, u32[]{:S(2)}, u32[]{:S(2)}) collective-permute-start(f32[4,3,1024]{2,1,0:T(4,128)S(1)} %stats.1.refs_8_), channel_id=1, source_target_pairs={{192,0},{0,64},{64,128},{128,192},{193,1},{1,65},{65,129},{129,193... | collective-permute-start | bytes 147464 | tf_op jit(solution)/shard_map/ppermute | solution.py:269
  69.3 5.8 %collective-permute-start.12 = (f32[4,3,1024]{2,1,0:T(4,128)S(1)}, f32[4,3,1024]{2,1,0:T(4,128)S(1)}, u32[]{:S(2)}, u32[]{:S(2)}) collective-permute-start(f32[4,3,1024]{2,1,0:T(4,128)S(1)} %stats.1.refs_8_), channel_id=1, source_target_pairs={{128,0},{192,64},{0,128},{64,192},{129,1},{193,65},{1,129},{65,193... | collective-permute-start | bytes 147464 | tf_op jit(solution)/shard_map/ppermute | solution.py:269
  69.3 5.8 %collective-permute-start.11 = (f32[4,3,1024]{2,1,0:T(4,128)S(1)}, f32[4,3,1024]{2,1,0:T(4,128)S(1)}, u32[]{:S(2)}, u32[]{:S(2)}) collective-permute-start(f32[4,3,1024]{2,1,0:T(4,128)S(1)} %stats.1.refs_8_), channel_id=1, source_target_pairs={{64,0},{128,64},{192,128},{0,192},{65,1},{129,65},{193,129},{1,193... | collective-permute-start | bytes 147464 | tf_op jit(solution)/shard_map/ppermute | solution.py:269
  93.0 2.7 %collective-permute-start.17 = (f32[8,4,2,32,128]{4,3,2,1,0:T(8,128)S(1)}, f32[8,4,2,32,128]{4,3,2,1,0:T(8,128)S(1)}, u32[]{:S(2)}, u32[]{:S(2)}) collective-permute-start(f32[8,4,2,32,128]{4,3,2,1,0:T(8,128)S(1)} %get-tuple-element.14), channel_id=1, source_target_pairs={{4,0},{0,4},{5,1},{1,5},{6,2},{2,6},{7,3},{3,7},{12,8},{8,12},{13,... | collective-permute-start | bytes 3145736 | tf_op jit(solution)/shard_map/ppermute | solution.py:269
  96.1 6.2 %collective-permute-start.18 = (bf16[4,2,32,128]{3,2,1,0:T(8,128)(2,1)S(1)}, bf16[4,2,32,128]{3,2,1,0:T(8,128)(2,1)S(1)}, u32[]{:S(2)}, u32[]{:S(2)}) collective-permute-start(bf16[4,2,32,128]{3,2,1,0:T(8,128)(2,1)S(1)} %get-tuple-element.23), channel_id=1, source_target_pairs={{56,0},{0,8},{8,16},{16,24},{24,32},{32,40},{40,48},{48,56},{57,1}... | collective-permute-start | bytes 196616 | tf_op jit(solution)/shard_map/ppermute | solution.py:269
  96.7 7.1 %collective-permute-start.24 = (bf16[4,2,32,128]{3,2,1,0:T(8,128)(2,1)S(1)}, bf16[4,2,32,128]{3,2,1,0:T(8,128)(2,1)S(1)}, u32[]{:S(2)}, u32[]{:S(2)}) collective-permute-start(bf16[4,2,32,128]{3,2,1,0:T(8,128)(2,1)S(1)} %get-tuple-element.24), channel_id=1, source_target_pairs={{8,0},{16,8},{24,16},{32,24},{40,32},{48,40},{56,48},{0,56},{9,1},... | collective-permute-start | bytes 196616 | tf_op jit(solution)/shard_map/ppermute | solution.py:269
  99.4 8.1 %collective-permute-start.23 = (bf16[4,2,32,128]{3,2,1,0:T(8,128)(2,1)S(1)}, bf16[4,2,32,128]{3,2,1,0:T(8,128)(2,1)S(1)}, u32[]{:S(2)}, u32[]{:S(2)}) collective-permute-start(bf16[4,2,32,128]{3,2,1,0:T(8,128)(2,1)S(1)} %get-tuple-element.25), channel_id=1, source_target_pairs={{16,0},{24,8},{32,16},{40,24},{48,32},{56,40},{0,48},{8,56},{17,1}... | collective-permute-start | bytes 196616 | tf_op jit(solution)/shard_map/ppermute | solution.py:269
  99.4 9.6 %collective-permute-start.22 = (bf16[4,2,32,128]{3,2,1,0:T(8,128)(2,1)S(1)}, bf16[4,2,32,128]{3,2,1,0:T(8,128)(2,1)S(1)}, u32[]{:S(2)}, u32[]{:S(2)}) collective-permute-start(bf16[4,2,32,128]{3,2,1,0:T(8,128)(2,1)S(1)} %get-tuple-element.26), channel_id=1, source_target_pairs={{24,0},{32,8},{40,16},{48,24},{56,32},{0,40},{8,48},{16,56},{25,1}... | collective-permute-start | bytes 196616 | tf_op jit(solution)/shard_map/ppermute | solution.py:269
  100.8 9.0 %collective-permute-start.21 = (bf16[4,2,32,128]{3,2,1,0:T(8,128)(2,1)S(1)}, bf16[4,2,32,128]{3,2,1,0:T(8,128)(2,1)S(1)}, u32[]{:S(2)}, u32[]{:S(2)}) collective-permute-start(bf16[4,2,32,128]{3,2,1,0:T(8,128)(2,1)S(1)} %get-tuple-element.27), channel_id=1, source_target_pairs={{48,0},{56,8},{0,16},{8,24},{16,32},{24,40},{32,48},{40,56},{49,1}... | collective-permute-start | bytes 196616 | tf_op jit(solution)/shard_map/ppermute | solution.py:269
  102.3 9.8 %collective-permute-start.20 = (bf16[4,2,32,128]{3,2,1,0:T(8,128)(2,1)S(1)}, bf16[4,2,32,128]{3,2,1,0:T(8,128)(2,1)S(1)}, u32[]{:S(2)}, u32[]{:S(2)}) collective-permute-start(bf16[4,2,32,128]{3,2,1,0:T(8,128)(2,1)S(1)} %get-tuple-element.28), channel_id=1, source_target_pairs={{56,0},{0,8},{8,16},{16,24},{24,32},{32,40},{40,48},{48,56},{57,1}... | collective-permute-start | bytes 196616 | tf_op jit(solution)/shard_map/ppermute | solution.py:269
  103.8 8.3 %collective-permute-start.19 = (bf16[4,2,32,128]{3,2,1,0:T(8,128)(2,1)S(1)}, bf16[4,2,32,128]{3,2,1,0:T(8,128)(2,1)S(1)}, u32[]{:S(2)}, u32[]{:S(2)}) collective-permute-start(bf16[4,2,32,128]{3,2,1,0:T(8,128)(2,1)S(1)} %fusion.2), channel_id=1, source_target_pairs={{40,0},{48,8},{56,16},{0,24},{8,32},{16,40},{24,48},{32,56},{41,1}... | collective-permute-start | bytes 196616 | tf_op jit(solution)/shard_map/ppermute | solution.py:269
  107.5 11.5 %collective-permute-start.14 = (bf16[1024,128]{1,0:T(8,128)(2,1)S(1)}, bf16[1024,128]{1,0:T(8,128)(2,1)S(1)}, u32[]{:S(2)}, u32[]{:S(2)}) collective-permute-start(bf16[1024,128]{1,0:T(8,128)(2,1)S(1)} %get-tuple-element.10), channel_id=1, source_target_pairs={{192,0},{0,64},{64,128},{128,192},{193,1},{1,65},{65,129},{129,193... | collective-permute-start | bytes 786440 | tf_op jit(solution)/shard_map/ppermute | solution.py:269
  109.0 11.5 %collective-permute-start.15 = (bf16[1024,128]{1,0:T(8,128)(2,1)S(1)}, bf16[1024,128]{1,0:T(8,128)(2,1)S(1)}, u32[]{:S(2)}, u32[]{:S(2)}) collective-permute-start(bf16[1024,128]{1,0:T(8,128)(2,1)S(1)} %get-tuple-element.11), channel_id=1, source_target_pairs={{128,0},{192,64},{0,128},{64,192},{129,1},{193,65},{1,129},{65,193... | collective-permute-start | bytes 786440 | tf_op jit(solution)/shard_map/ppermute | solution.py:269
  109.8 11.7 %collective-permute-start.16 = (bf16[1024,128]{1,0:T(8,128)(2,1)S(1)}, bf16[1024,128]{1,0:T(8,128)(2,1)S(1)}, u32[]{:S(2)}, u32[]{:S(2)}) collective-permute-start(bf16[1024,128]{1,0:T(8,128)(2,1)S(1)} %get-tuple-element.12), channel_id=1, source_target_pairs={{64,0},{128,64},{192,128},{0,192},{65,1},{129,65},{193,129},{1,193... | collective-permute-start | bytes 786440 | tf_op jit(solution)/shard_map/ppermute | solution.py:269
  112.2 17.0 %collective-permute-start.25 = (bf16[2,32,128]{2,1,0:T(8,128)(2,1)S(1)}, bf16[2,32,128]{2,1,0:T(8,128)(2,1)S(1)}, u32[]{:S(2)}, u32[]{:S(2)}) collective-permute-start(bf16[2,32,128]{2,1,0:T(8,128)(2,1)S(1)} %get-tuple-element.34), channel_id=1, source_target_pairs={{0,0},{64,1},{128,2},{192,3},{1,64},{65,65},{129,66},{193,67},{2,1... | collective-permute-start | bytes 49160 | tf_op jit(solution)/shard_map/ppermute | solution.py:313
  122.4 13.4 %collective-permute-start.28 = (bf16[2,32,128]{2,1,0:T(8,128)(2,1)S(1)}, bf16[2,32,128]{2,1,0:T(8,128)(2,1)S(1)}, u32[]{:S(2)}, u32[]{:S(2)}) collective-permute-start(bf16[2,32,128]{2,1,0:T(8,128)(2,1)S(1)} %get-tuple-element.31), channel_id=1, source_target_pairs={{3,0},{67,1},{131,2},{195,3},{0,64},{64,65},{128,66},{192,67},{1,1... | collective-permute-start | bytes 49160 | tf_op jit(solution)/shard_map/ppermute | solution.py:313
  127.1 8.7 %collective-permute-start.27 = (bf16[2,32,128]{2,1,0:T(8,128)(2,1)S(1)}, bf16[2,32,128]{2,1,0:T(8,128)(2,1)S(1)}, u32[]{:S(2)}, u32[]{:S(2)}) collective-permute-start(bf16[2,32,128]{2,1,0:T(8,128)(2,1)S(1)} %get-tuple-element.32), channel_id=1, source_target_pairs={{2,0},{66,1},{130,2},{194,3},{3,64},{67,65},{131,66},{195,67},{0,1... | collective-permute-start | bytes 49160 | tf_op jit(solution)/shard_map/ppermute | solution.py:313
  128.5 7.4 %collective-permute-start.26 = (bf16[2,32,128]{2,1,0:T(8,128)(2,1)S(1)}, bf16[2,32,128]{2,1,0:T(8,128)(2,1)S(1)}, u32[]{:S(2)}, u32[]{:S(2)}) collective-permute-start(bf16[2,32,128]{2,1,0:T(8,128)(2,1)S(1)} %get-tuple-element.33), channel_id=1, source_target_pairs={{1,0},{65,1},{129,2},{193,3},{2,64},{66,65},{130,66},{194,67},{3,1... | collective-permute-start | bytes 49160 | tf_op jit(solution)/shard_map/ppermute | solution.py:313

commit v4 on v3

--- a/solution.py
+++ b/solution.py
@@ -222,6 +222,30 @@
         pltpu.VMEM((NY, ROWS, DH), BF),
         pltpu.VMEM((2, NY, NZ * NC, SLICE, DH), BF),
     ]
+
+
+def spread_kernel(b0, b1, b2, b3, key_out, value_out, wide):
+    y = lax.axis_index("y").astype(jnp.int32)
+    parts = [ref[...].astype(F32) for ref in (b0, b1, b2, b3)]
+    for h in range(NX):
+        piece = pick(lax.rem(h + NY - y, NX), parts)
+        for n in range(2):
+            wide[n, :, h, :] = piece[n]
+    key_out[...] = wide[0].astype(BF)
+    value_out[...] = wide[1].astype(BF)
+
+
+def spread_call(back):
+    out = jax.ShapeDtypeStruct((SLICE, NX, DH), BF)
+    return pl.pallas_call(
+        spread_kernel,
+        out_shape=(out, out),
+        in_specs=[VM] * NX,
+        out_specs=(VM, VM),
+        scratch_shapes=[pltpu.VMEM((2, SLICE, NX, DH), F32)],
+        compiler_params=pltpu.CompilerParams(vmem_limit_bytes=4 << 20),
+        name="spread",
+    )(*map(near, back))
 
 
 def near(value):
@@ -311,10 +335,8 @@
             (a * NX + (b + r) % NX, b * NX + a) for b in range(NY) for a in range(NX)
         ]
         back.append(lax.ppermute(kv_low[r], ("y", "x"), perm))
-    ring = jnp.stack(back + back)
-    ring = lax.dynamic_slice_in_dim(ring, (NX - y) % NX, NX, axis=0)
-    ring = ring.transpose(1, 2, 0, 3)
-    return (d_query, ring[0], ring[1])
+    d_key, d_value = spread_call(back)
+    return (d_query, d_key, d_value)
 
 
 def solution(mesh):

time: 138 us -> 136 us (0.986)
  the two profiles are of different devices: /device:TPU:16 before, /device:TPU:26 now
where the time goes in v4:
time: 136 us; the launch traced here: 135 us
  starting transfers between devices  57.5 us (42%)
  waiting for transfers between devices  44.4 us (33%)
  Pallas kernels  29.7 us (22%)
  local copies, waits for them, and re-layouts  1.69 us (1%)
    ppermute x21, starting transfers between devices, shift(): lax.ppermute(value, axis, [((n + by) % size, n) for n in range(size)])  25 us
    ppermute x21, waiting for transfers between devices, shift(): lax.ppermute(value, axis, [((n + by) % size, n) for n in range(size)])  20.8 us
    pallas_call x1, Pallas kernels, grad_call(): pl.pallas_call(grad_kernel, out_shape=(pltpu.VMEM((ROWS, DH), BF),) * NY...  18 us
    ppermute x4, starting transfers between devices, steps(): back.append(lax.ppermute(kv_low[r], ('y', 'x'), perm))  15.9 us
    all_to_all x1, waiting for transfers between devices, steps(): lax.all_to_all(jnp.broadcast_to(own[None], (NZ,) + own.shape), 'z', 0, 0)  12.4 us
    pallas_call x1, Pallas kernels, stats_call(): pl.pallas_call(stats_kernel, out_shape=pltpu.VMEM((NY, 3, ROWS), F32), in...  11 us
    all_to_all x1, starting transfers between devices, steps(): lax.all_to_all(jnp.broadcast_to(own[None], (NZ,) + own.shape), 'z', 0, 0)  8.6 us
    ppermute x4, starting transfers between devices, steps(): rounds.append(lax.ppermute(piece, ('y', 'x'), perm))  7.99 us
  transfers between devices with their start and end apart: 30, of which 13 were waited for; matrix products, arithmetic and copies ran while one was open for 1% of the time, Pallas kernels for 0%

profile of v4, /device:TPU:26, one launch (start us, length us, event | category | flops | bytes accessed | tf_op | source)
XLA Modules:
  0.0 135.4 jit_solution(15252013143202714425)
XLA Ops:
  0.7 0.7 copy-done.5
  1.4 0.0 copy-done.4
  1.5 4.7 %collective-permute-start.6 = (bf16[2,32,128]{2,1,0:T(8,128)(2,1)S(1)}, bf16[2,32,128]{2,1,0:T(8,128)(2,1)S(1)}, u32[]{:S(2)}, u32[]{:S(2)}) collective-permute-start(bf16[2,32,128]{2,1,0:T(8,128)(2,1)S(1)} %get-tuple-element.31), channel_id=1, source_target_pairs={{0,0},{1,64},{2,128},{3,192},{64,1},{65,65},{66,129},{67,193},{128... | collective-permute-start | bytes 49160 | tf_op jit(solution)/shard_map/ppermute | solution.py:305
  6.2 0.1 collective-permute-start.7
  6.3 1.5 %collective-permute-start.8 = (bf16[2,32,128]{2,1,0:T(8,128)(2,1)S(1)}, bf16[2,32,128]{2,1,0:T(8,128)(2,1)S(1)}, u32[]{:S(2)}, u32[]{:S(2)}) collective-permute-start(bf16[2,32,128]{2,1,0:T(8,128)(2,1)S(1)} %get-tuple-element.33), channel_id=1, source_target_pairs={{0,2},{1,66},{2,130},{3,194},{64,3},{65,67},{66,131},{67,195},{128... | collective-permute-start | bytes 49160 | tf_op jit(solution)/shard_map/ppermute | solution.py:305
  7.7 1.7 %collective-permute-start.9 = (bf16[2,32,128]{2,1,0:T(8,128)(2,1)S(1)}, bf16[2,32,128]{2,1,0:T(8,128)(2,1)S(1)}, u32[]{:S(2)}, u32[]{:S(2)}) collective-permute-start(bf16[2,32,128]{2,1,0:T(8,128)(2,1)S(1)} %get-tuple-element.34), channel_id=1, source_target_pairs={{0,3},{1,67},{2,131},{3,195},{64,0},{65,64},{66,128},{67,192},{128... | collective-permute-start | bytes 49160 | tf_op jit(solution)/shard_map/ppermute | solution.py:305
  9.5 1.5 %collective-permute-done.6 = bf16[2,32,128]{2,1,0:T(8,128)(2,1)S(1)} collective-permute-done((bf16[2,32,128]{2,1,0:T(8,128)(2,1)S(1)}, bf16[2,32,128]{2,1,0:T(8,128)(2,1)S(1)}, u32[]{:S(2)}, u32[]{:S(2)}) %collective-permute-start.6) | collective-permute-done | bytes 16416 | tf_op jit(solution)/shard_map/ppermute | solution.py:305
  11.0 2.6 %collective-permute-done.7 = bf16[2,32,128]{2,1,0:T(8,128)(2,1)S(1)} collective-permute-done((bf16[2,32,128]{2,1,0:T(8,128)(2,1)S(1)}, bf16[2,32,128]{2,1,0:T(8,128)(2,1)S(1)}, u32[]{:S(2)}, u32[]{:S(2)}) %collective-permute-start.7) | collective-permute-done | bytes 16416 | tf_op jit(solution)/shard_map/ppermute | solution.py:305
  13.6 0.0 collective-permute-done.8
  13.6 0.4 collective-permute-done.9
  14.0 0.9 broadcast_in_dim.2
  14.9 8.6 %all-to-all-start = ((bf16[8,4,2,32,128]{4,3,2,1,0:T(8,128)(2,1)}), bf16[8,4,2,32,128]{4,3,2,1,0:T(8,128)(2,1)S(1)}, u32[]{:S(2)}, u32[]{:S(2)}) async-start(bf16[8,4,2,32,128]{4,3,2,1,0:T(8,128)(2,1)} %broadcast_in_dim.2), calls=%async_computation | async-start | bytes 1048576 | tf_op jit(solution)/shard_map/all_to_all | solution.py:311
  23.5 0.0 copy-start.2
  23.5 0.0 copy-start.3
  23.5 0.7 collective-permute-start
  24.2 2.6 %collective-permute-start.4 = (bf16[1024,128]{1,0:T(8,128)(2,1)S(1)}, bf16[1024,128]{1,0:T(8,128)(2,1)S(1)}, u32[]{:S(2)}, u32[]{:S(2)}) collective-permute-start(bf16[1024,128]{1,0:T(8,128)(2,1)S(1)} %bitcast.66), channel_id=1, source_target_pairs={{192,0},{0,64},{64,128},{128,192},{193,1},{1,65},{65,129},{129,193... | collective-permute-start | bytes 786440 | tf_op jit(solution)/shard_map/ppermute | solution.py:293
  26.8 12.4 %all-to-all-done.refs_8_.refs_12_ = bf16[8,4,2,32,128]{4,3,2,1,0:T(8,128)(2,1)S(1)} async-done(((bf16[8,4,2,32,128]{4,3,2,1,0:T(8,128)(2,1)}), bf16[8,4,2,32,128]{4,3,2,1,0:T(8,128)(2,1)S(1)}, u32[]{:S(2)}, u32[]{:S(2)}) %all-to-all-start) | async-done | bytes 524320 | tf_op jit(solution)/shard_map/all_to_all | solution.py:311
  39.2 0.0 collective-permute-start.10
  39.2 0.4 collective-permute-start.2
  39.6 1.6 %collective-permute-start.3 = (bf16[1024,128]{1,0:T(8,128)(2,1)S(1)}, bf16[1024,128]{1,0:T(8,128)(2,1)S(1)}, u32[]{:S(2)}, u32[]{:S(2)}) collective-permute-start(bf16[1024,128]{1,0:T(8,128)(2,1)S(1)} %bitcast.67), channel_id=1, source_target_pairs={{64,0},{128,64},{192,128},{0,192},{65,1},{129,65},{193,129},{1,193... | collective-permute-start | bytes 786440 | tf_op jit(solution)/shard_map/ppermute | solution.py:293
  41.2 0.0 collective-permute-done.refs_1_
  41.2 0.4 collective-permute-start.1
  41.6 0.0 collective-permute-done.4.refs_7_
  41.7 2.8 %collective-permute-start.5 = (bf16[1024,128]{1,0:T(8,128)(2,1)S(1)}, bf16[1024,128]{1,0:T(8,128)(2,1)S(1)}, u32[]{:S(2)}, u32[]{:S(2)}) collective-permute-start(bf16[1024,128]{1,0:T(8,128)(2,1)S(1)} %collective-permute-done.4.refs_7_), channel_id=1, source_target_pairs={{192,0},{0,64},{64,128},{128,192},{193,1},{1,65},{65,129},{129,193... | collective-permute-start | bytes 786440 | tf_op jit(solution)/shard_map/ppermute | solution.py:293
  44.5 3.9 %collective-permute-done.2.refs_3_ = bf16[1024,128]{1,0:T(8,128)(2,1)S(1)} collective-permute-done((bf16[1024,128]{1,0:T(8,128)(2,1)S(1)}, bf16[1024,128]{1,0:T(8,128)(2,1)S(1)}, u32[]{:S(2)}, u32[]{:S(2)}) %collective-permute-start.2) | collective-permute-done | bytes 262176 | tf_op jit(solution)/shard_map/ppermute | solution.py:293
  48.4 1.6 %collective-permute-done.3.refs_5_ = bf16[1024,128]{1,0:T(8,128)(2,1)S(1)} collective-permute-done((bf16[1024,128]{1,0:T(8,128)(2,1)S(1)}, bf16[1024,128]{1,0:T(8,128)(2,1)S(1)}, u32[]{:S(2)}, u32[]{:S(2)}) %collective-permute-start.3) | collective-permute-done | bytes 262176 | tf_op jit(solution)/shard_map/ppermute | solution.py:293
  50.0 4.9 %collective-permute-done.1.refs_2_ = bf16[1024,128]{1,0:T(8,128)(2,1)S(1)} collective-permute-done((bf16[1024,128]{1,0:T(8,128)(2,1)S(1)}, bf16[1024,128]{1,0:T(8,128)(2,1)S(1)}, u32[]{:S(2)}, u32[]{:S(2)}) %collective-permute-start.1) | collective-permute-done | bytes 262176 | tf_op jit(solution)/shard_map/ppermute | solution.py:293
  54.9 0.0 collective-permute-done.5.refs_6_
  54.9 0.0 collective-permute-done.10.refs_9_.refs_13_
  54.9 11.0 %stats.1.refs_8_ = f32[4,3,1024]{2,1,0:T(4,128)S(1)} custom-call(s32[32]{0:T(128)S(1)} %copy-done.2, s32[32]{0:T(128)S(1)} %copy-done.3, bf16[1024,128]{1,0:T(8,128)(2,1)S(1)} %bitcast.64, bf16[1024,128]{1,0:T(8,128)(2,1)S(1)} %collective-permute-done.refs_1_, bf16[1024,128]{1,0:T(8,128)(2,1)S(1)} %collective-permute-done.1.refs_2_, ...), custom_call_target="tpu_custom_call" | custom-call | tf_op jit(solution)/shard_map/stats/pallas_call | solution.py:256
  65.9 1.1 collective-permute-start.13
  67.1 1.4 %collective-permute-start.12 = (f32[4,3,1024]{2,1,0:T(4,128)S(1)}, f32[4,3,1024]{2,1,0:T(4,128)S(1)}, u32[]{:S(2)}, u32[]{:S(2)}) collective-permute-start(f32[4,3,1024]{2,1,0:T(4,128)S(1)} %stats.1.refs_8_), channel_id=1, source_target_pairs={{128,0},{192,64},{0,128},{64,192},{129,1},{193,65},{1,129},{65,193... | collective-permute-start | bytes 147464 | tf_op jit(solution)/shard_map/ppermute | solution.py:293
  68.5 0.0 collective-permute-start.11
  68.5 1.8 %collective-permute-done.13.refs_11_ = f32[4,3,1024]{2,1,0:T(4,128)S(1)} collective-permute-done((f32[4,3,1024]{2,1,0:T(4,128)S(1)}, f32[4,3,1024]{2,1,0:T(4,128)S(1)}, u32[]{:S(2)}, u32[]{:S(2)}) %collective-permute-start.13) | collective-permute-done | bytes 49184 | tf_op jit(solution)/shard_map/ppermute | solution.py:293
  70.3 2.7 %collective-permute-done.12.refs_10_ = f32[4,3,1024]{2,1,0:T(4,128)S(1)} collective-permute-done((f32[4,3,1024]{2,1,0:T(4,128)S(1)}, f32[4,3,1024]{2,1,0:T(4,128)S(1)}, u32[]{:S(2)}, u32[]{:S(2)}) %collective-permute-start.12) | collective-permute-done | bytes 49184 | tf_op jit(solution)/shard_map/ppermute | solution.py:293
  73.0 1.0 collective-permute-done.11.refs_9_
  74.0 18.0 %grads.1 = (bf16[1024,128]{1,0:T(8,128)(2,1)S(1)}, bf16[1024,128]{1,0:T(8,128)(2,1)S(1)}, bf16[1024,128]{1,0:T(8,128)(2,1)S(1)}, bf16[1024,128]{1,0:T(8,128)(2,1...) custom-call(s32[32]{0:T(128)S(1)} %copy-done.2, s32[32]{0:T(128)S(1)} %copy-done.3, ...), custom_call_target="tpu_custom_call" | custom-call | tf_op jit(solution)/shard_map/grads/pallas_call | solution.py:271
  92.0 0.1 collective-permute-start.17
  92.1 2.6 %collective-permute-done.17 = f32[8,4,2,32,128]{4,3,2,1,0:T(8,128)S(1)} collective-permute-done((f32[8,4,2,32,128]{4,3,2,1,0:T(8,128)S(1)}, f32[8,4,2,32,128]{4,3,2,1,0:T(8,128)S(1)}, u32[]{:S(2)}, u32[]{:S(2)}) %collective-permute-start.17) | collective-permute-done | bytes 1048608 | tf_op jit(solution)/shard_map/ppermute | solution.py:293
  94.7 0.3 fusion.18
  95.0 0.6 collective-permute-start.18
  95.7 2.7 %collective-permute-start.24 = (bf16[4,2,32,128]{3,2,1,0:T(8,128)(2,1)S(1)}, bf16[4,2,32,128]{3,2,1,0:T(8,128)(2,1)S(1)}, u32[]{:S(2)}, u32[]{:S(2)}) collective-permute-start(bf16[4,2,32,128]{3,2,1,0:T(8,128)(2,1)S(1)} %get-tuple-element.22), channel_id=1, source_target_pairs={{8,0},{16,8},{24,16},{32,24},{40,32},{48,40},{56,48},{0,56},{9,1},... | collective-permute-start | bytes 196616 | tf_op jit(solution)/shard_map/ppermute | solution.py:293
  98.3 0.0 collective-permute-start.23
  98.3 1.4 %collective-permute-start.22 = (bf16[4,2,32,128]{3,2,1,0:T(8,128)(2,1)S(1)}, bf16[4,2,32,128]{3,2,1,0:T(8,128)(2,1)S(1)}, u32[]{:S(2)}, u32[]{:S(2)}) collective-permute-start(bf16[4,2,32,128]{3,2,1,0:T(8,128)(2,1)S(1)} %get-tuple-element.24), channel_id=1, source_target_pairs={{24,0},{32,8},{40,16},{48,24},{56,32},{0,40},{8,48},{16,56},{25,1}... | collective-permute-start | bytes 196616 | tf_op jit(solution)/shard_map/ppermute | solution.py:293
  99.8 1.5 %collective-permute-start.21 = (bf16[4,2,32,128]{3,2,1,0:T(8,128)(2,1)S(1)}, bf16[4,2,32,128]{3,2,1,0:T(8,128)(2,1)S(1)}, u32[]{:S(2)}, u32[]{:S(2)}) collective-permute-start(bf16[4,2,32,128]{3,2,1,0:T(8,128)(2,1)S(1)} %get-tuple-element.25), channel_id=1, source_target_pairs={{48,0},{56,8},{0,16},{8,24},{16,32},{24,40},{32,48},{40,56},{49,1}... | collective-permute-start | bytes 196616 | tf_op jit(solution)/shard_map/ppermute | solution.py:293
  101.3 0.0 collective-permute-done.18
  101.3 1.5 %collective-permute-start.20 = (bf16[4,2,32,128]{3,2,1,0:T(8,128)(2,1)S(1)}, bf16[4,2,32,128]{3,2,1,0:T(8,128)(2,1)S(1)}, u32[]{:S(2)}, u32[]{:S(2)}) collective-permute-start(bf16[4,2,32,128]{3,2,1,0:T(8,128)(2,1)S(1)} %get-tuple-element.26), channel_id=1, source_target_pairs={{56,0},{0,8},{8,16},{16,24},{24,32},{32,40},{40,48},{48,56},{57,1}... | collective-permute-start | bytes 196616 | tf_op jit(solution)/shard_map/ppermute | solution.py:293
  102.8 3.6 %collective-permute-start.19 = (bf16[4,2,32,128]{3,2,1,0:T(8,128)(2,1)S(1)}, bf16[4,2,32,128]{3,2,1,0:T(8,128)(2,1)S(1)}, u32[]{:S(2)}, u32[]{:S(2)}) collective-permute-start(bf16[4,2,32,128]{3,2,1,0:T(8,128)(2,1)S(1)} %fusion.2), channel_id=1, source_target_pairs={{40,0},{48,8},{56,16},{0,24},{8,32},{16,40},{24,48},{32,56},{41,1}... | collective-permute-start | bytes 196616 | tf_op jit(solution)/shard_map/ppermute | solution.py:293
  106.4 1.0 collective-permute-start.14
  107.4 0.9 collective-permute-start.15
  108.3 0.0 collective-permute-done.21
  108.3 0.5 collective-permute-start.16
  108.9 0.0 collective-permute-done.20
  108.9 2.2 %collective-permute-done.19 = bf16[4,2,32,128]{3,2,1,0:T(8,128)(2,1)S(1)} collective-permute-done((bf16[4,2,32,128]{3,2,1,0:T(8,128)(2,1)S(1)}, bf16[4,2,32,128]{3,2,1,0:T(8,128)(2,1)S(1)}, u32[]{:S(2)}, u32[]{:S(2)}) %collective-permute-start.19) | collective-permute-done | bytes 65568 | tf_op jit(solution)/shard_map/ppermute | solution.py:293
  111.1 0.1 fusion.9
  111.1 3.4 %collective-permute-start.28 = (bf16[2,32,128]{2,1,0:T(8,128)(2,1)S(1)}, bf16[2,32,128]{2,1,0:T(8,128)(2,1)S(1)}, u32[]{:S(2)}, u32[]{:S(2)}) collective-permute-start(bf16[2,32,128]{2,1,0:T(8,128)(2,1)S(1)} %get-tuple-element.27), channel_id=1, source_target_pairs={{3,0},{67,1},{131,2},{195,3},{0,64},{64,65},{128,66},{192,67},{1,1... | collective-permute-start | bytes 49160 | tf_op jit(solution)/shard_map/ppermute | solution.py:337
  114.6 1.7 %collective-permute-start.27 = (bf16[2,32,128]{2,1,0:T(8,128)(2,1)S(1)}, bf16[2,32,128]{2,1,0:T(8,128)(2,1)S(1)}, u32[]{:S(2)}, u32[]{:S(2)}) collective-permute-start(bf16[2,32,128]{2,1,0:T(8,128)(2,1)S(1)} %get-tuple-element.28), channel_id=1, source_target_pairs={{2,0},{66,1},{130,2},{194,3},{3,64},{67,65},{131,66},{195,67},{0,1... | collective-permute-start | bytes 49160 | tf_op jit(solution)/shard_map/ppermute | solution.py:337
  116.2 8.8 %collective-permute-start.26 = (bf16[2,32,128]{2,1,0:T(8,128)(2,1)S(1)}, bf16[2,32,128]{2,1,0:T(8,128)(2,1)S(1)}, u32[]{:S(2)}, u32[]{:S(2)}) collective-permute-start(bf16[2,32,128]{2,1,0:T(8,128)(2,1)S(1)} %get-tuple-element.29), channel_id=1, source_target_pairs={{1,0},{65,1},{129,2},{193,3},{2,64},{66,65},{130,66},{194,67},{3,1... | collective-permute-start | bytes 49160 | tf_op jit(solution)/shard_map/ppermute | solution.py:337
  125.1 0.0 collective-permute-done.15
  125.1 1.9 %collective-permute-start.25 = (bf16[2,32,128]{2,1,0:T(8,128)(2,1)S(1)}, bf16[2,32,128]{2,1,0:T(8,128)(2,1)S(1)}, u32[]{:S(2)}, u32[]{:S(2)}) collective-permute-start(bf16[2,32,128]{2,1,0:T(8,128)(2,1)S(1)} %get-tuple-element.30), channel_id=1, source_target_pairs={{0,0},{64,1},{128,2},{192,3},{1,64},{65,65},{129,66},{193,67},{2,1... | collective-permute-start | bytes 49160 | tf_op jit(solution)/shard_map/ppermute | solution.py:337
  127.0 0.0 collective-permute-done.16
  127.0 0.8 fusion
  127.9 6.7 %collective-permute-done.25.b0 = bf16[2,32,128]{2,1,0:T(8,128)(2,1)S(1)} collective-permute-done((bf16[2,32,128]{2,1,0:T(8,128)(2,1)S(1)}, bf16[2,32,128]{2,1,0:T(8,128)(2,1)S(1)}, u32[]{:S(2)}, u32[]{:S(2)}) %collective-permute-start.25) | collective-permute-done | bytes 16416 | tf_op jit(solution)/shard_map/ppermute | solution.py:337
  134.6 0.7 spread.1
  (21 shorter events, 0.1 us)
Async XLA Ops:
  0.6 0.8 copy-start.5
  0.7 0.8 copy-start.4
  1.5 9.5 %collective-permute-start.6 = (bf16[2,32,128]{2,1,0:T(8,128)(2,1)S(1)}, bf16[2,32,128]{2,1,0:T(8,128)(2,1)S(1)}, u32[]{:S(2)}, u32[]{:S(2)}) collective-permute-start(bf16[2,32,128]{2,1,0:T(8,128)(2,1)S(1)} %get-tuple-element.31), channel_id=1, source_target_pairs={{0,0},{1,64},{2,128},{3,192},{64,1},{65,65},{66,129},{67,193},{128... | collective-permute-start | bytes 49160 | tf_op jit(solution)/shard_map/ppermute | solution.py:305
  6.2 7.4 %collective-permute-start.7 = (bf16[2,32,128]{2,1,0:T(8,128)(2,1)S(1)}, bf16[2,32,128]{2,1,0:T(8,128)(2,1)S(1)}, u32[]{:S(2)}, u32[]{:S(2)}) collective-permute-start(bf16[2,32,128]{2,1,0:T(8,128)(2,1)S(1)} %get-tuple-element.32), channel_id=1, source_target_pairs={{0,1},{1,65},{2,129},{3,193},{64,2},{65,66},{66,130},{67,194},{128... | collective-permute-start | bytes 49160 | tf_op jit(solution)/shard_map/ppermute | solution.py:305
  6.3 7.3 %collective-permute-start.8 = (bf16[2,32,128]{2,1,0:T(8,128)(2,1)S(1)}, bf16[2,32,128]{2,1,0:T(8,128)(2,1)S(1)}, u32[]{:S(2)}, u32[]{:S(2)}) collective-permute-start(bf16[2,32,128]{2,1,0:T(8,128)(2,1)S(1)} %get-tuple-element.33), channel_id=1, source_target_pairs={{0,2},{1,66},{2,130},{3,194},{64,3},{65,67},{66,131},{67,195},{128... | collective-permute-start | bytes 49160 | tf_op jit(solution)/shard_map/ppermute | solution.py:305
  7.7 6.2 %collective-permute-start.9 = (bf16[2,32,128]{2,1,0:T(8,128)(2,1)S(1)}, bf16[2,32,128]{2,1,0:T(8,128)(2,1)S(1)}, u32[]{:S(2)}, u32[]{:S(2)}) collective-permute-start(bf16[2,32,128]{2,1,0:T(8,128)(2,1)S(1)} %get-tuple-element.34), channel_id=1, source_target_pairs={{0,3},{1,67},{2,131},{3,195},{64,0},{65,64},{66,128},{67,192},{128... | collective-permute-start | bytes 49160 | tf_op jit(solution)/shard_map/ppermute | solution.py:305
  14.9 8.6 %copy-start = (bf16[128,8,128]{2,1,0:T(8,128)(2,1)S(1)}, bf16[128,8,128]{2,1,0:T(8,128)(2,1)}, u32[]{:S(2)}) copy-start(bf16[128,8,128]{2,1,0:T(8,128)(2,1)} %param.6) | copy-start | bytes 786436
  14.9 9.3 %copy-start.1 = (bf16[128,8,128]{2,1,0:T(8,128)(2,1)S(1)}, bf16[128,8,128]{2,1,0:T(8,128)(2,1)}, u32[]{:S(2)}) copy-start(bf16[128,8,128]{2,1,0:T(8,128)(2,1)} %param.9) | copy-start | bytes 786436
  14.9 24.3 %all-to-all-start = ((bf16[8,4,2,32,128]{4,3,2,1,0:T(8,128)(2,1)}), bf16[8,4,2,32,128]{4,3,2,1,0:T(8,128)(2,1)S(1)}, u32[]{:S(2)}, u32[]{:S(2)}) async-start(bf16[8,4,2,32,128]{4,3,2,1,0:T(8,128)(2,1)} %broadcast_in_dim.2), calls=%async_computation | async-start | bytes 1048576 | tf_op jit(solution)/shard_map/all_to_all | solution.py:311
  23.5 31.4 %copy-start.2 = (s32[32]{0:T(128)S(1)}, s32[32]{0:T(128)}, u32[]{:S(2)}) copy-start(s32[32]{0:T(128)} %seg_blocks.3) | copy-start | bytes 388
  23.5 31.4 %copy-start.3 = (s32[32]{0:T(128)S(1)}, s32[32]{0:T(128)}, u32[]{:S(2)}) copy-start(s32[32]{0:T(128)} %seg_audio.3) | copy-start | bytes 388
  23.5 17.7 %collective-permute-start = (bf16[1024,128]{1,0:T(8,128)(2,1)S(1)}, bf16[1024,128]{1,0:T(8,128)(2,1)S(1)}, u32[]{:S(2)}, u32[]{:S(2)}) collective-permute-start(bf16[1024,128]{1,0:T(8,128)(2,1)S(1)} %bitcast.62), channel_id=1, source_target_pairs={{64,0},{128,64},{192,128},{0,192},{65,1},{129,65},{193,129},{1,193... | collective-permute-start | bytes 786440 | tf_op jit(solution)/shard_map/ppermute | solution.py:293
  24.2 17.4 %collective-permute-start.4 = (bf16[1024,128]{1,0:T(8,128)(2,1)S(1)}, bf16[1024,128]{1,0:T(8,128)(2,1)S(1)}, u32[]{:S(2)}, u32[]{:S(2)}) collective-permute-start(bf16[1024,128]{1,0:T(8,128)(2,1)S(1)} %bitcast.66), channel_id=1, source_target_pairs={{192,0},{0,64},{64,128},{128,192},{193,1},{1,65},{65,129},{129,193... | collective-permute-start | bytes 786440 | tf_op jit(solution)/shard_map/ppermute | solution.py:293
  39.2 15.7 %collective-permute-start.10 = (bf16[8,4,2,32,128]{4,3,2,1,0:T(8,128)(2,1)S(1)}, bf16[8,4,2,32,128]{4,3,2,1,0:T(8,128)(2,1)S(1)}, u32[]{:S(2)}, u32[]{:S(2)}) collective-permute-start(bf16[8,4,2,32,128]{4,3,2,1,0:T(8,128)(2,1)S(1)} %all-to-all-done.refs_8_.refs_12_), channel_id=1, source_target_pairs={{4,0},{0,4},{5,1},{1,5},{6,2},{2,6},{7,3},{3,7},{12,8},{8,12},{13,... | collective-permute-start | bytes 1572872 | tf_op jit(solution)/shard_map/ppermute | solution.py:293
  39.2 9.2 %collective-permute-start.2 = (bf16[1024,128]{1,0:T(8,128)(2,1)S(1)}, bf16[1024,128]{1,0:T(8,128)(2,1)S(1)}, u32[]{:S(2)}, u32[]{:S(2)}) collective-permute-start(bf16[1024,128]{1,0:T(8,128)(2,1)S(1)} %bitcast.63), channel_id=1, source_target_pairs={{192,0},{0,64},{64,128},{128,192},{193,1},{1,65},{65,129},{129,193... | collective-permute-start | bytes 786440 | tf_op jit(solution)/shard_map/ppermute | solution.py:293
  39.6 10.4 %collective-permute-start.3 = (bf16[1024,128]{1,0:T(8,128)(2,1)S(1)}, bf16[1024,128]{1,0:T(8,128)(2,1)S(1)}, u32[]{:S(2)}, u32[]{:S(2)}) collective-permute-start(bf16[1024,128]{1,0:T(8,128)(2,1)S(1)} %bitcast.67), channel_id=1, source_target_pairs={{64,0},{128,64},{192,128},{0,192},{65,1},{129,65},{193,129},{1,193... | collective-permute-start | bytes 786440 | tf_op jit(solution)/shard_map/ppermute | solution.py:293
  41.2 13.6 %collective-permute-start.1 = (bf16[1024,128]{1,0:T(8,128)(2,1)S(1)}, bf16[1024,128]{1,0:T(8,128)(2,1)S(1)}, u32[]{:S(2)}, u32[]{:S(2)}) collective-permute-start(bf16[1024,128]{1,0:T(8,128)(2,1)S(1)} %collective-permute-done.refs_1_), channel_id=1, source_target_pairs={{64,0},{128,64},{192,128},{0,192},{65,1},{129,65},{193,129},{1,193... | collective-permute-start | bytes 786440 | tf_op jit(solution)/shard_map/ppermute | solution.py:293
  41.7 13.2 %collective-permute-start.5 = (bf16[1024,128]{1,0:T(8,128)(2,1)S(1)}, bf16[1024,128]{1,0:T(8,128)(2,1)S(1)}, u32[]{:S(2)}, u32[]{:S(2)}) collective-permute-start(bf16[1024,128]{1,0:T(8,128)(2,1)S(1)} %collective-permute-done.4.refs_7_), channel_id=1, source_target_pairs={{192,0},{0,64},{64,128},{128,192},{193,1},{1,65},{65,129},{129,193... | collective-permute-start | bytes 786440 | tf_op jit(solution)/shard_map/ppermute | solution.py:293
  65.9 4.3 %collective-permute-start.13 = (f32[4,3,1024]{2,1,0:T(4,128)S(1)}, f32[4,3,1024]{2,1,0:T(4,128)S(1)}, u32[]{:S(2)}, u32[]{:S(2)}) collective-permute-start(f32[4,3,1024]{2,1,0:T(4,128)S(1)} %stats.1.refs_8_), channel_id=1, source_target_pairs={{192,0},{0,64},{64,128},{128,192},{193,1},{1,65},{65,129},{129,193... | collective-permute-start | bytes 147464 | tf_op jit(solution)/shard_map/ppermute | solution.py:293
  67.1 5.9 %collective-permute-start.12 = (f32[4,3,1024]{2,1,0:T(4,128)S(1)}, f32[4,3,1024]{2,1,0:T(4,128)S(1)}, u32[]{:S(2)}, u32[]{:S(2)}) collective-permute-start(f32[4,3,1024]{2,1,0:T(4,128)S(1)} %stats.1.refs_8_), channel_id=1, source_target_pairs={{128,0},{192,64},{0,128},{64,192},{129,1},{193,65},{1,129},{65,193... | collective-permute-start | bytes 147464 | tf_op jit(solution)/shard_map/ppermute | solution.py:293
  68.5 5.5 %collective-permute-start.11 = (f32[4,3,1024]{2,1,0:T(4,128)S(1)}, f32[4,3,1024]{2,1,0:T(4,128)S(1)}, u32[]{:S(2)}, u32[]{:S(2)}) collective-permute-start(f32[4,3,1024]{2,1,0:T(4,128)S(1)} %stats.1.refs_8_), channel_id=1, source_target_pairs={{64,0},{128,64},{192,128},{0,192},{65,1},{129,65},{193,129},{1,193... | collective-permute-start | bytes 147464 | tf_op jit(solution)/shard_map/ppermute | solution.py:293
  92.0 2.7 %collective-permute-start.17 = (f32[8,4,2,32,128]{4,3,2,1,0:T(8,128)S(1)}, f32[8,4,2,32,128]{4,3,2,1,0:T(8,128)S(1)}, u32[]{:S(2)}, u32[]{:S(2)}) collective-permute-start(f32[8,4,2,32,128]{4,3,2,1,0:T(8,128)S(1)} %get-tuple-element.16), channel_id=1, source_target_pairs={{4,0},{0,4},{5,1},{1,5},{6,2},{2,6},{7,3},{3,7},{12,8},{8,12},{13,... | collective-permute-start | bytes 3145736 | tf_op jit(solution)/shard_map/ppermute | solution.py:293
  95.0 6.2 %collective-permute-start.18 = (bf16[4,2,32,128]{3,2,1,0:T(8,128)(2,1)S(1)}, bf16[4,2,32,128]{3,2,1,0:T(8,128)(2,1)S(1)}, u32[]{:S(2)}, u32[]{:S(2)}) collective-permute-start(bf16[4,2,32,128]{3,2,1,0:T(8,128)(2,1)S(1)} %get-tuple-element.21), channel_id=1, source_target_pairs={{56,0},{0,8},{8,16},{16,24},{24,32},{32,40},{40,48},{48,56},{57,1}... | collective-permute-start | bytes 196616 | tf_op jit(solution)/shard_map/ppermute | solution.py:293
  95.7 7.1 %collective-permute-start.24 = (bf16[4,2,32,128]{3,2,1,0:T(8,128)(2,1)S(1)}, bf16[4,2,32,128]{3,2,1,0:T(8,128)(2,1)S(1)}, u32[]{:S(2)}, u32[]{:S(2)}) collective-permute-start(bf16[4,2,32,128]{3,2,1,0:T(8,128)(2,1)S(1)} %get-tuple-element.22), channel_id=1, source_target_pairs={{8,0},{16,8},{24,16},{32,24},{40,32},{48,40},{56,48},{0,56},{9,1},... | collective-permute-start | bytes 196616 | tf_op jit(solution)/shard_map/ppermute | solution.py:293
  98.3 8.1 %collective-permute-start.23 = (bf16[4,2,32,128]{3,2,1,0:T(8,128)(2,1)S(1)}, bf16[4,2,32,128]{3,2,1,0:T(8,128)(2,1)S(1)}, u32[]{:S(2)}, u32[]{:S(2)}) collective-permute-start(bf16[4,2,32,128]{3,2,1,0:T(8,128)(2,1)S(1)} %get-tuple-element.23), channel_id=1, source_target_pairs={{16,0},{24,8},{32,16},{40,24},{48,32},{56,40},{0,48},{8,56},{17,1}... | collective-permute-start | bytes 196616 | tf_op jit(solution)/shard_map/ppermute | solution.py:293
  98.3 9.1 %collective-permute-start.22 = (bf16[4,2,32,128]{3,2,1,0:T(8,128)(2,1)S(1)}, bf16[4,2,32,128]{3,2,1,0:T(8,128)(2,1)S(1)}, u32[]{:S(2)}, u32[]{:S(2)}) collective-permute-start(bf16[4,2,32,128]{3,2,1,0:T(8,128)(2,1)S(1)} %get-tuple-element.24), channel_id=1, source_target_pairs={{24,0},{32,8},{40,16},{48,24},{56,32},{0,40},{8,48},{16,56},{25,1}... | collective-permute-start | bytes 196616 | tf_op jit(solution)/shard_map/ppermute | solution.py:293
  99.8 8.6 %collective-permute-start.21 = (bf16[4,2,32,128]{3,2,1,0:T(8,128)(2,1)S(1)}, bf16[4,2,32,128]{3,2,1,0:T(8,128)(2,1)S(1)}, u32[]{:S(2)}, u32[]{:S(2)}) collective-permute-start(bf16[4,2,32,128]{3,2,1,0:T(8,128)(2,1)S(1)} %get-tuple-element.25), channel_id=1, source_target_pairs={{48,0},{56,8},{0,16},{8,24},{16,32},{24,40},{32,48},{40,56},{49,1}... | collective-permute-start | bytes 196616 | tf_op jit(solution)/shard_map/ppermute | solution.py:293
  101.3 7.6 %collective-permute-start.20 = (bf16[4,2,32,128]{3,2,1,0:T(8,128)(2,1)S(1)}, bf16[4,2,32,128]{3,2,1,0:T(8,128)(2,1)S(1)}, u32[]{:S(2)}, u32[]{:S(2)}) collective-permute-start(bf16[4,2,32,128]{3,2,1,0:T(8,128)(2,1)S(1)} %get-tuple-element.26), channel_id=1, source_target_pairs={{56,0},{0,8},{8,16},{16,24},{24,32},{32,40},{40,48},{48,56},{57,1}... | collective-permute-start | bytes 196616 | tf_op jit(solution)/shard_map/ppermute | solution.py:293
  102.8 8.3 %collective-permute-start.19 = (bf16[4,2,32,128]{3,2,1,0:T(8,128)(2,1)S(1)}, bf16[4,2,32,128]{3,2,1,0:T(8,128)(2,1)S(1)}, u32[]{:S(2)}, u32[]{:S(2)}) collective-permute-start(bf16[4,2,32,128]{3,2,1,0:T(8,128)(2,1)S(1)} %fusion.2), channel_id=1, source_target_pairs={{40,0},{48,8},{56,16},{0,24},{8,32},{16,40},{24,48},{32,56},{41,1}... | collective-permute-start | bytes 196616 | tf_op jit(solution)/shard_map/ppermute | solution.py:293
  106.4 9.8 %collective-permute-start.14 = (bf16[1024,128]{1,0:T(8,128)(2,1)S(1)}, bf16[1024,128]{1,0:T(8,128)(2,1)S(1)}, u32[]{:S(2)}, u32[]{:S(2)}) collective-permute-start(bf16[1024,128]{1,0:T(8,128)(2,1)S(1)} %get-tuple-element.12), channel_id=1, source_target_pairs={{192,0},{0,64},{64,128},{128,192},{193,1},{1,65},{65,129},{129,193... | collective-permute-start | bytes 786440 | tf_op jit(solution)/shard_map/ppermute | solution.py:293
  107.4 17.7 %collective-permute-start.15 = (bf16[1024,128]{1,0:T(8,128)(2,1)S(1)}, bf16[1024,128]{1,0:T(8,128)(2,1)S(1)}, u32[]{:S(2)}, u32[]{:S(2)}) collective-permute-start(bf16[1024,128]{1,0:T(8,128)(2,1)S(1)} %get-tuple-element.13), channel_id=1, source_target_pairs={{128,0},{192,64},{0,128},{64,192},{129,1},{193,65},{1,129},{65,193... | collective-permute-start | bytes 786440 | tf_op jit(solution)/shard_map/ppermute | solution.py:293
  108.3 18.7 %collective-permute-start.16 = (bf16[1024,128]{1,0:T(8,128)(2,1)S(1)}, bf16[1024,128]{1,0:T(8,128)(2,1)S(1)}, u32[]{:S(2)}, u32[]{:S(2)}) collective-permute-start(bf16[1024,128]{1,0:T(8,128)(2,1)S(1)} %get-tuple-element.14), channel_id=1, source_target_pairs={{64,0},{128,64},{192,128},{0,192},{65,1},{129,65},{193,129},{1,193... | collective-permute-start | bytes 786440 | tf_op jit(solution)/shard_map/ppermute | solution.py:293
  111.1 16.7 %collective-permute-start.28 = (bf16[2,32,128]{2,1,0:T(8,128)(2,1)S(1)}, bf16[2,32,128]{2,1,0:T(8,128)(2,1)S(1)}, u32[]{:S(2)}, u32[]{:S(2)}) collective-permute-start(bf16[2,32,128]{2,1,0:T(8,128)(2,1)S(1)} %get-tuple-element.27), channel_id=1, source_target_pairs={{3,0},{67,1},{131,2},{195,3},{0,64},{64,65},{128,66},{192,67},{1,1... | collective-permute-start | bytes 49160 | tf_op jit(solution)/shard_map/ppermute | solution.py:337
  114.6 13.3 %collective-permute-start.27 = (bf16[2,32,128]{2,1,0:T(8,128)(2,1)S(1)}, bf16[2,32,128]{2,1,0:T(8,128)(2,1)S(1)}, u32[]{:S(2)}, u32[]{:S(2)}) collective-permute-start(bf16[2,32,128]{2,1,0:T(8,128)(2,1)S(1)} %get-tuple-element.28), channel_id=1, source_target_pairs={{2,0},{66,1},{130,2},{194,3},{3,64},{67,65},{131,66},{195,67},{0,1... | collective-permute-start | bytes 49160 | tf_op jit(solution)/shard_map/ppermute | solution.py:337
  116.2 11.6 %collective-permute-start.26 = (bf16[2,32,128]{2,1,0:T(8,128)(2,1)S(1)}, bf16[2,32,128]{2,1,0:T(8,128)(2,1)S(1)}, u32[]{:S(2)}, u32[]{:S(2)}) collective-permute-start(bf16[2,32,128]{2,1,0:T(8,128)(2,1)S(1)} %get-tuple-element.29), channel_id=1, source_target_pairs={{1,0},{65,1},{129,2},{193,3},{2,64},{66,65},{130,66},{194,67},{3,1... | collective-permute-start | bytes 49160 | tf_op jit(solution)/shard_map/ppermute | solution.py:337
  125.1 9.5 %collective-permute-start.25 = (bf16[2,32,128]{2,1,0:T(8,128)(2,1)S(1)}, bf16[2,32,128]{2,1,0:T(8,128)(2,1)S(1)}, u32[]{:S(2)}, u32[]{:S(2)}) collective-permute-start(bf16[2,32,128]{2,1,0:T(8,128)(2,1)S(1)} %get-tuple-element.30), channel_id=1, source_target_pairs={{0,0},{64,1},{128,2},{192,3},{1,64},{65,65},{129,66},{193,67},{2,1... | collective-permute-start | bytes 49160 | tf_op jit(solution)/shard_map/ppermute | solution.py:337
